TPU v7x, 32 devices: a whole 2x2x4 slice. The times are simulated.
32 devices in a mesh: gx: 8 (over z, y), gy: 4 (over x, core).
Axes of the slice: x: 2, y: 2, z: 4, core: 2. Of those that a mesh axis runs over, the one named last changes fastest.
Arguments:
- right_side: float32 [128, 512, 128], P('gx', 'gy'), may hold values from -21 to 21
- conductivity: float32 [128, 512, 128], P('gx', 'gy'), may hold values from 0.1 to 10
Outputs:
- pressure: float32 [128, 512, 128], P('gx', 'gy')
- residual: float32 [128, 512, 128], P('gx', 'gy')
All inputs are finite; a program needn't handle non-finite values.
Results may differ from a plain program's by a relative error of at most 0.00035.
Values sent between devices are 32-bit elements; how exact they have to be, the bound alone decides.
No kernel may reach another device: no remote copies, remote signals or barrier semaphores. Data moves between devices by JAX's collectives and lax.ppermute only.
A program may use at most 64 MiB of HBM per device.

v0:
```python
import jax
import jax.numpy as jnp
from jax import lax
from jax.sharding import PartitionSpec as P


def extended(array, sides, width):
    for axis, dim in sides:
        count, length = (lax.axis_size(axis), array.shape[dim])
        up = [(i, (i + 1) % count) for i in range(count - 1)]
        down = [(j, i) for i, j in up]
        last = lax.slice_in_dim(array, length - width, length, axis=dim)
        leading = lax.slice_in_dim(array, 0, width, axis=dim)
        before = lax.ppermute(last, axis, up)
        after = lax.ppermute(leading, axis, down)
        array = jnp.concatenate([before, array, after], axis=dim)
    return array


def passed_along(value, axis, steps):
    count = lax.axis_size(axis)
    leading, last = (max(0, -steps), min(count, count - steps))
    return lax.ppermute(value, axis, [(source, source + steps) for source in range(leading, last)])


def face_coeffs(cond_grown):
    middle = cond_grown[1:-1, 1:-1]
    along_z = jnp.pad(middle, ((0, 0), (0, 0), (1, 1)))
    to_west = 0.5 * (middle + cond_grown[:-2, 1:-1])
    to_east = 0.5 * (middle + cond_grown[2:, 1:-1])
    to_south = 0.5 * (middle + cond_grown[1:-1, :-2])
    to_north = 0.5 * (middle + cond_grown[1:-1, 2:])
    to_below = 0.5 * (middle + along_z[:, :, :-2])
    to_above = 0.5 * (middle + along_z[:, :, 2:])
    return (to_west, to_east, to_south, to_north, to_below, to_above)


def neighbour_sum(coeffs, grown):
    padded = jnp.pad(grown, ((0, 0), (0, 0), (1, 1)))
    to_west, to_east, to_south, to_north, to_below, to_above = coeffs
    summed = to_west * padded[:-2, 1:-1, 1:-1] + to_east * padded[2:, 1:-1, 1:-1]
    summed = summed + to_south * padded[1:-1, :-2, 1:-1] + to_north * padded[1:-1, 2:, 1:-1]
    summed = summed + to_below * padded[1:-1, 1:-1, :-2] + to_above * padded[1:-1, 1:-1, 2:]
    return summed


def pad_plane(values):
    return jnp.pad(values, ((1, 1), (1, 1), (0, 0)))


def add_six(coeffs):
    return coeffs[0] + coeffs[1] + coeffs[2] + coeffs[3] + coeffs[4] + coeffs[5]


def two_sweeps(coeffs, diagonal, resid):
    initial = resid / diagonal
    return (resid + neighbour_sum(coeffs, pad_plane(initial))) / diagonal


def on_device(right_side, conductivity):
    cells_x, cells_y, cells_z = right_side.shape
    stacked = jnp.stack((conductivity, right_side))
    grown = extended(stacked, (("gx", 1), ("gy", 2)), 3)
    cond_grown = grown[0]
    resid_grown = grown[1]
    box_coeffs = face_coeffs(cond_grown)
    index_x = lax.axis_index("gx")
    index_y = lax.axis_index("gy")
    parts_x = lax.axis_size("gx")
    parts_y = lax.axis_size("gy")
    global_x = index_x * cells_x - 2 + jnp.arange(cells_x + 4, dtype=jnp.int32)
    global_y = index_y * cells_y - 2 + jnp.arange(cells_y + 4, dtype=jnp.int32)
    inside_x = (global_x >= 0) & (global_x < cells_x * parts_x)
    inside_y = (global_y >= 0) & (global_y < cells_y * parts_y)
    inside = (inside_x[:, None, None] & inside_y[None, :, None]).astype(jnp.float32)
    box_diag = jnp.where(inside > 0, add_six(box_coeffs), 1.0)
    box_resid = resid_grown[1:-1, 1:-1]
    solved = two_sweeps(box_coeffs, box_diag, box_resid) * inside
    middle = solved[2:-2]
    for offset in (1, -1):
        margin = solved[-2:] if offset == 1 else solved[:2]
        arrived = passed_along(margin, "gx", offset)
        if offset == 1:
            middle = middle.at[:2].add(arrived)
        else:
            middle = middle.at[-2:].add(arrived)
    precond = middle[:, 2:-2]
    for offset in (1, -1):
        margin = middle[:, -2:] if offset == 1 else middle[:, :2]
        arrived = passed_along(margin, "gy", offset)
        if offset == 1:
            precond = precond.at[:, :2].add(arrived)
        else:
            precond = precond.at[:, -2:].add(arrived)
    own_coeffs = face_coeffs(cond_grown[2:-2, 2:-2])
    own_diag = add_six(own_coeffs)
    precond_grown = extended(precond, (("gx", 0), ("gy", 1)), 1)
    image = own_diag * precond - neighbour_sum(own_coeffs, precond_grown)
    inner_rz = lax.psum(jnp.sum(right_side * precond), ("gx", "gy"))
    inner_pq = lax.psum(jnp.sum(precond * image), ("gx", "gy"))
    alpha = inner_rz / inner_pq
    return (alpha * precond, right_side - alpha * image)


def solution(mesh):
    in_specs = (P("gx", "gy", None), P("gx", "gy", None))
    out_specs = (P("gx", "gy", None), P("gx", "gy", None))
    return jax.shard_map(
        on_device, mesh=mesh, in_specs=in_specs, out_specs=out_specs, check_vma=False
    )
```

profile of v0, /device:TPU:0, one launch (start us, length us, event | category | flops | bytes accessed | tf_op | source)
XLA Modules:
  0.0 123.0 jit_solution(11712124633386631157)
XLA Ops:
  0.6 0.0 copy-start
  0.6 0.0 copy-start.1
  0.6 2.2 %pad_maximum_fusion.10 = (f32[2,3,128,128]{3,2,1,0:T(8,128)}, f32[2,3,128,128]{3,2,1,0:T(8,128)S(1)}) fusion(f32[1,16,128,128]{3,2,1,0:T(8,128)} %bitcast.6, f32[1,16,128,128]{3,2,1,0:T(8,128)} %bitcast.9), kind=kLoop, calls=%fused_computation.74 | loop fusion | flops 196608 | bytes 2883584 | tf_op jit(solution)/shard_map/slice | solution.py:12
  2.8 4.9 %collective-permute-start = (f32[2,3,128,128]{3,2,1,0:T(8,128)}, f32[2,3,128,128]{3,2,1,0:T(8,128)S(1)}, u32[]{:S(2)}, u32[]{:S(2)}) collective-permute-start(f32[2,3,128,128]{3,2,1,0:T(8,128)} %get-tuple-element.59), channel_id=1, source_target_pairs={{0,4},{4,8},{8,12},{12,16},{16,20},{20,24},{24,28},{1,5},{5,9},{9,... | collective-permute-start | bytes 1179656 | tf_op jit(solution)/shard_map/ppermute | solution.py:14
  7.7 1.3 %collective-permute-start.1 = (f32[2,3,128,128]{3,2,1,0:T(8,128)S(1)}, f32[2,3,128,128]{3,2,1,0:T(8,128)S(1)}, u32[]{:S(2)}, u32[]{:S(2)}) collective-permute-start(f32[2,3,128,128]{3,2,1,0:T(8,128)S(1)} %get-tuple-element.60), channel_id=1, source_target_pairs={{4,0},{8,4},{12,8},{16,12},{20,16},{24,20},{28,24},{5,1},{9,5},{13... | collective-permute-start | bytes 1179656 | tf_op jit(solution)/shard_map/ppermute | solution.py:15
  9.0 15.7 %collective-permute-done = f32[2,3,128,128]{3,2,1,0:T(8,128)S(1)} collective-permute-done((f32[2,3,128,128]{3,2,1,0:T(8,128)}, f32[2,3,128,128]{3,2,1,0:T(8,128)S(1)}, u32[]{:S(2)}, u32[]{:S(2)}) %collective-permute-start) | collective-permute-done | bytes 393248 | tf_op jit(solution)/shard_map/ppermute | solution.py:14
  24.8 0.0 collective-permute-done.1
  24.8 0.0 copy-done
  24.8 0.0 copy-done.1
  24.8 1.3 %collective-permute-start.2 = (f32[2,22,3,128]{3,2,1,0:T(4,128)S(1)}, f32[2,22,3,128]{3,2,1,0:T(4,128)S(1)}, u32[]{:S(2)}, u32[]{:S(2)}) collective-permute-start(f32[2,22,3,128]{3,2,1,0:T(4,128)S(1)} %get-tuple-element.57), channel_id=1, source_target_pairs={{0,1},{1,2},{2,3},{4,5},{5,6},{6,7},{8,9},{9,10},{10,11},{12,13},{... | collective-permute-start | bytes 202760 | tf_op jit(solution)/shard_map/ppermute | solution.py:14
  26.1 1.3 %collective-permute-start.3 = (f32[2,22,3,128]{3,2,1,0:T(4,128)S(1)}, f32[2,22,3,128]{3,2,1,0:T(4,128)S(1)}, u32[]{:S(2)}, u32[]{:S(2)}) collective-permute-start(f32[2,22,3,128]{3,2,1,0:T(4,128)S(1)} %get-tuple-element.58), channel_id=1, source_target_pairs={{1,0},{2,1},{3,2},{5,4},{6,5},{7,6},{9,8},{10,9},{11,10},{13,12},{... | collective-permute-start | bytes 202760 | tf_op jit(solution)/shard_map/ppermute | solution.py:15
  27.4 0.1 and_convert_fusion
  27.5 0.0 collective-permute-done.2
  27.5 3.5 %collective-permute-done.3 = f32[2,22,3,128]{3,2,1,0:T(4,128)S(1)} collective-permute-done((f32[2,22,3,128]{3,2,1,0:T(4,128)S(1)}, f32[2,22,3,128]{3,2,1,0:T(4,128)S(1)}, u32[]{:S(2)}, u32[]{:S(2)}) %collective-permute-start.3) | collective-permute-done | bytes 67616 | tf_op jit(solution)/shard_map/ppermute | solution.py:15
  31.0 0.3 pad_maximum_fusion
  31.4 0.2 slice_bitcast_fusion
  31.6 0.1 slice.297
  31.7 1.7 %fusion.15 = f32[20,132,128]{2,1,0:T(8,128)S(1)} fusion(f32[22,134,128]{2,1,0:T(8,128)S(1)} %get-tuple-element.56, pred[20,132]{1,0:T(8,128)(4,1)S(1)} %get-tuple-element.70, f32[20,132,128]{2,1,0:T(8,128)S(1)} %slice.297, f32[22,134,128]{2,1,0:T(8,128)S(1)} %get-tuple-element.55), kind=kLoop, calls=%fused_computation.35 | loop fusion | flops 6420480 | bytes 9464400 | tf_op jit(solution)/shard_map/div | solution.py:56
  33.4 0.1 pad.29
  33.5 3.1 %fusion.16 = f32[20,132,128]{2,1,0:T(8,128)S(1)} fusion(f32[22,134,128]{2,1,0:T(8,128)S(1)} %pad.29, f32[22,134,128]{2,1,0:T(8,128)S(1)} %get-tuple-element.56, f32[20,132]{1,0:T(8,128)S(1)} %get-tuple-element.69, pred[20,132]{1,0:T(8,128)(4,1)S(1)} %get-tuple-element.70, f32[20,132,128]{2,1,0:T(8,128)S(1)} %slice.297, f32[22,134,128]{2,1,0:T(8,128)S(1)} %get-tuple-element.55), kind=kLoop, calls=%fused_computation.36 | loop fusion | flops 10813440 | bytes 16840704 | tf_op jit(solution)/shard_map/mul | solution.py:78
  36.7 4.3 %collective-permute-start.4 = (f32[2,132,128]{2,1,0:T(8,128)S(1)}, f32[2,132,128]{2,1,0:T(8,128)S(1)}, u32[]{:S(2)}, u32[]{:S(2)}) collective-permute-start(f32[2,132,128]{2,1,0:T(8,128)S(1)} %get-tuple-element.62), channel_id=1, source_target_pairs={{0,4},{4,8},{8,12},{12,16},{16,20},{20,24},{24,28},{1,5},{5,9},{9,... | collective-permute-start | bytes 405512 | tf_op jit(solution)/shard_map/ppermute | solution.py:23
  41.0 0.1 slice.302
  41.0 1.3 %collective-permute-start.5 = (f32[2,132,128]{2,1,0:T(8,128)S(1)}, f32[2,132,128]{2,1,0:T(8,128)S(1)}, u32[]{:S(2)}, u32[]{:S(2)}) collective-permute-start(f32[2,132,128]{2,1,0:T(8,128)S(1)} %get-tuple-element.61), channel_id=1, source_target_pairs={{4,0},{8,4},{12,8},{16,12},{20,16},{24,20},{28,24},{5,1},{9,5},{13... | collective-permute-start | bytes 405512 | tf_op jit(solution)/shard_map/ppermute | solution.py:23
  42.3 1.2 collective-permute-done.4
  43.5 4.8 %collective-permute-done.5 = f32[2,132,128]{2,1,0:T(8,128)S(1)} collective-permute-done((f32[2,132,128]{2,1,0:T(8,128)S(1)}, f32[2,132,128]{2,1,0:T(8,128)S(1)}, u32[]{:S(2)}, u32[]{:S(2)}) %collective-permute-start.5) | collective-permute-done | bytes 135200 | tf_op jit(solution)/shard_map/ppermute | solution.py:23
  48.4 3.9 %collective-permute-start.6 = (f32[16,2,128]{2,1,0:T(2,128)S(1)}, f32[16,2,128]{2,1,0:T(2,128)S(1)}, u32[]{:S(2)}, u32[]{:S(2)}) collective-permute-start(f32[16,2,128]{2,1,0:T(2,128)S(1)} %get-tuple-element.66), channel_id=1, source_target_pairs={{0,1},{1,2},{2,3},{4,5},{5,6},{6,7},{8,9},{9,10},{10,11},{12,13},{... | collective-permute-start | bytes 49160 | tf_op jit(solution)/shard_map/ppermute | solution.py:23
  52.4 0.1 slice.307
  52.5 1.3 %collective-permute-start.7 = (f32[16,2,128]{2,1,0:T(2,128)S(1)}, f32[16,2,128]{2,1,0:T(2,128)S(1)}, u32[]{:S(2)}, u32[]{:S(2)}) collective-permute-start(f32[16,2,128]{2,1,0:T(2,128)S(1)} %get-tuple-element.65), channel_id=1, source_target_pairs={{1,0},{2,1},{3,2},{5,4},{6,5},{7,6},{9,8},{10,9},{11,10},{13,12},{... | collective-permute-start | bytes 49160 | tf_op jit(solution)/shard_map/ppermute | solution.py:23
  53.8 0.0 collective-permute-done.6
  53.8 2.3 %collective-permute-done.7 = f32[16,2,128]{2,1,0:T(2,128)S(1)} collective-permute-done((f32[16,2,128]{2,1,0:T(2,128)S(1)}, f32[16,2,128]{2,1,0:T(2,128)S(1)}, u32[]{:S(2)}, u32[]{:S(2)}) %collective-permute-start.7) | collective-permute-done | bytes 16416 | tf_op jit(solution)/shard_map/ppermute | solution.py:23
  56.2 4.8 %collective-permute-start.8 = (f32[1,128,128]{2,1,0:T(8,128)S(1)}, f32[1,128,128]{2,1,0:T(8,128)S(1)}, u32[]{:S(2)}, u32[]{:S(2)}) collective-permute-start(f32[1,128,128]{2,1,0:T(8,128)S(1)} %get-tuple-element.67), channel_id=1, source_target_pairs={{0,4},{4,8},{8,12},{12,16},{16,20},{20,24},{24,28},{1,5},{5,9},{9,... | collective-permute-start | bytes 196616 | tf_op jit(solution)/shard_map/ppermute | solution.py:14
  61.0 1.3 %collective-permute-start.9 = (f32[1,128,128]{2,1,0:T(8,128)S(1)}, f32[1,128,128]{2,1,0:T(8,128)S(1)}, u32[]{:S(2)}, u32[]{:S(2)}) collective-permute-start(f32[1,128,128]{2,1,0:T(8,128)S(1)} %get-tuple-element.68), channel_id=1, source_target_pairs={{4,0},{8,4},{12,8},{16,12},{20,16},{24,20},{28,24},{5,1},{9,5},{13... | collective-permute-start | bytes 196616 | tf_op jit(solution)/shard_map/ppermute | solution.py:15
  62.3 0.6 collective-permute-done.8
  62.9 4.3 %collective-permute-done.9 = f32[1,128,128]{2,1,0:T(8,128)S(1)} collective-permute-done((f32[1,128,128]{2,1,0:T(8,128)S(1)}, f32[1,128,128]{2,1,0:T(8,128)S(1)}, u32[]{:S(2)}, u32[]{:S(2)}) %collective-permute-start.9) | collective-permute-done | bytes 65568 | tf_op jit(solution)/shard_map/ppermute | solution.py:15
  67.2 3.0 %collective-permute-start.10 = (f32[18,1,128]{2,1,0:T(1,128)S(1)}, f32[18,1,128]{2,1,0:T(1,128)S(1)}, u32[]{:S(2)}, u32[]{:S(2)}) collective-permute-start(f32[18,1,128]{2,1,0:T(1,128)S(1)} %get-tuple-element.63), channel_id=1, source_target_pairs={{0,1},{1,2},{2,3},{4,5},{5,6},{6,7},{8,9},{9,10},{10,11},{12,13},{... | collective-permute-start | bytes 27656 | tf_op jit(solution)/shard_map/ppermute | solution.py:14
  70.1 1.3 %collective-permute-start.11 = (f32[18,1,128]{2,1,0:T(1,128)S(1)}, f32[18,1,128]{2,1,0:T(1,128)S(1)}, u32[]{:S(2)}, u32[]{:S(2)}) collective-permute-start(f32[18,1,128]{2,1,0:T(1,128)S(1)} %get-tuple-element.64), channel_id=1, source_target_pairs={{1,0},{2,1},{3,2},{5,4},{6,5},{7,6},{9,8},{10,9},{11,10},{13,12},{... | collective-permute-start | bytes 27656 | tf_op jit(solution)/shard_map/ppermute | solution.py:15
  71.4 0.1 slice.312
  71.6 0.0 collective-permute-done.10
  71.6 2.6 %collective-permute-done.11 = f32[18,1,128]{2,1,0:T(1,128)S(1)} collective-permute-done((f32[18,1,128]{2,1,0:T(1,128)S(1)}, f32[18,1,128]{2,1,0:T(1,128)S(1)}, u32[]{:S(2)}, u32[]{:S(2)}) %collective-permute-start.11) | collective-permute-done | bytes 9248 | tf_op jit(solution)/shard_map/ppermute | solution.py:15
  74.2 0.8 select_maximum_fusion
  75.0 4.1 %multiply_reduce_fusion = (f32[]{:T(128)}, f32[]{:T(128)}, f32[16,128,128]{2,1,0:T(8,128)S(1)}) fusion(f32[16,128,128]{2,1,0:T(8,128)S(1)} %fusion.37, f32[16,128,128]{2,1,0:T(8,128)S(1)} %copy-done, f32[18,130,130]{2,1,0:T(8,128)S(1)} %select_maximum_fusion, f32[18,1,128]{2,1,0:T(1,128)S(1)} %collective-permute-done.11, ...), kind=kLoop, calls=%fused_computation.70 | loop fusion | flops 11010046 | bytes 10635272 | tf_op jit(solution)/shard_map/reduce_sum | solution.py:100
  79.1 41.0 %all-reduce.5 = (f32[]{:T(128)}, f32[]{:T(128)}) all-reduce(f32[]{:T(128)} %get-tuple-element.51, f32[]{:T(128)} %get-tuple-element.50), channel_id=1, replica_groups=mesh['gx'=8,'gy'=4] {'gx','gy'}, use_global_device_ids=true, to_apply=%region_1.2 | all-reduce | flops 2 | bytes 16 | tf_op jit(solution)/shard_map/psum | solution.py:99
  121.4 1.5 %multiply_subtract_fusion = (f32[16,128,128]{2,1,0:T(8,128)}, f32[16,128,128]{2,1,0:T(8,128)}) fusion(f32[16,128,128]{2,1,0:T(8,128)S(1)} %copy-done, f32[16,128,128]{2,1,0:T(8,128)S(1)} %get-tuple-element.54, f32[]{:T(128)S(6)} %div.11, f32[16,128,128]{2,1,0:T(8,128)S(1)} %fusion.37), kind=kLoop, calls=%fused_computation.69 | loop fusion | flops 786432 | bytes 5242884 | tf_op jit(solution)/shard_map/sub | solution.py:102
  (11 shorter events, 0.2 us)
Async XLA Ops:
  0.6 24.1 %copy-start = (f32[16,128,128]{2,1,0:T(8,128)S(1)}, f32[16,128,128]{2,1,0:T(8,128)}, u32[]{:S(2)}) copy-start(f32[16,128,128]{2,1,0:T(8,128)} %param.10) | copy-start | bytes 3145732
  0.6 24.1 %copy-start.1 = (f32[16,128,128]{2,1,0:T(8,128)S(1)}, f32[16,128,128]{2,1,0:T(8,128)}, u32[]{:S(2)}) copy-start(f32[16,128,128]{2,1,0:T(8,128)} %param.11) | copy-start | bytes 3145732
  2.8 22.0 %collective-permute-start = (f32[2,3,128,128]{3,2,1,0:T(8,128)}, f32[2,3,128,128]{3,2,1,0:T(8,128)S(1)}, u32[]{:S(2)}, u32[]{:S(2)}) collective-permute-start(f32[2,3,128,128]{3,2,1,0:T(8,128)} %get-tuple-element.59), channel_id=1, source_target_pairs={{0,4},{4,8},{8,12},{12,16},{16,20},{20,24},{24,28},{1,5},{5,9},{9,... | collective-permute-start | bytes 1179656 | tf_op jit(solution)/shard_map/ppermute | solution.py:14
  7.7 17.1 %collective-permute-start.1 = (f32[2,3,128,128]{3,2,1,0:T(8,128)S(1)}, f32[2,3,128,128]{3,2,1,0:T(8,128)S(1)}, u32[]{:S(2)}, u32[]{:S(2)}) collective-permute-start(f32[2,3,128,128]{3,2,1,0:T(8,128)S(1)} %get-tuple-element.60), channel_id=1, source_target_pairs={{4,0},{8,4},{12,8},{16,12},{20,16},{24,20},{28,24},{5,1},{9,5},{13... | collective-permute-start | bytes 1179656 | tf_op jit(solution)/shard_map/ppermute | solution.py:15
  24.8 2.7 %collective-permute-start.2 = (f32[2,22,3,128]{3,2,1,0:T(4,128)S(1)}, f32[2,22,3,128]{3,2,1,0:T(4,128)S(1)}, u32[]{:S(2)}, u32[]{:S(2)}) collective-permute-start(f32[2,22,3,128]{3,2,1,0:T(4,128)S(1)} %get-tuple-element.57), channel_id=1, source_target_pairs={{0,1},{1,2},{2,3},{4,5},{5,6},{6,7},{8,9},{9,10},{10,11},{12,13},{... | collective-permute-start | bytes 202760 | tf_op jit(solution)/shard_map/ppermute | solution.py:14
  26.1 4.9 %collective-permute-start.3 = (f32[2,22,3,128]{3,2,1,0:T(4,128)S(1)}, f32[2,22,3,128]{3,2,1,0:T(4,128)S(1)}, u32[]{:S(2)}, u32[]{:S(2)}) collective-permute-start(f32[2,22,3,128]{3,2,1,0:T(4,128)S(1)} %get-tuple-element.58), channel_id=1, source_target_pairs={{1,0},{2,1},{3,2},{5,4},{6,5},{7,6},{9,8},{10,9},{11,10},{13,12},{... | collective-permute-start | bytes 202760 | tf_op jit(solution)/shard_map/ppermute | solution.py:15
  36.7 6.9 %collective-permute-start.4 = (f32[2,132,128]{2,1,0:T(8,128)S(1)}, f32[2,132,128]{2,1,0:T(8,128)S(1)}, u32[]{:S(2)}, u32[]{:S(2)}) collective-permute-start(f32[2,132,128]{2,1,0:T(8,128)S(1)} %get-tuple-element.62), channel_id=1, source_target_pairs={{0,4},{4,8},{8,12},{12,16},{16,20},{20,24},{24,28},{1,5},{5,9},{9,... | collective-permute-start | bytes 405512 | tf_op jit(solution)/shard_map/ppermute | solution.py:23
  41.0 7.3 %collective-permute-start.5 = (f32[2,132,128]{2,1,0:T(8,128)S(1)}, f32[2,132,128]{2,1,0:T(8,128)S(1)}, u32[]{:S(2)}, u32[]{:S(2)}) collective-permute-start(f32[2,132,128]{2,1,0:T(8,128)S(1)} %get-tuple-element.61), channel_id=1, source_target_pairs={{4,0},{8,4},{12,8},{16,12},{20,16},{24,20},{28,24},{5,1},{9,5},{13... | collective-permute-start | bytes 405512 | tf_op jit(solution)/shard_map/ppermute | solution.py:23
  48.4 5.3 %collective-permute-start.6 = (f32[16,2,128]{2,1,0:T(2,128)S(1)}, f32[16,2,128]{2,1,0:T(2,128)S(1)}, u32[]{:S(2)}, u32[]{:S(2)}) collective-permute-start(f32[16,2,128]{2,1,0:T(2,128)S(1)} %get-tuple-element.66), channel_id=1, source_target_pairs={{0,1},{1,2},{2,3},{4,5},{5,6},{6,7},{8,9},{9,10},{10,11},{12,13},{... | collective-permute-start | bytes 49160 | tf_op jit(solution)/shard_map/ppermute | solution.py:23
  52.5 3.7 %collective-permute-start.7 = (f32[16,2,128]{2,1,0:T(2,128)S(1)}, f32[16,2,128]{2,1,0:T(2,128)S(1)}, u32[]{:S(2)}, u32[]{:S(2)}) collective-permute-start(f32[16,2,128]{2,1,0:T(2,128)S(1)} %get-tuple-element.65), channel_id=1, source_target_pairs={{1,0},{2,1},{3,2},{5,4},{6,5},{7,6},{9,8},{10,9},{11,10},{13,12},{... | collective-permute-start | bytes 49160 | tf_op jit(solution)/shard_map/ppermute | solution.py:23
  56.2 6.7 %collective-permute-start.8 = (f32[1,128,128]{2,1,0:T(8,128)S(1)}, f32[1,128,128]{2,1,0:T(8,128)S(1)}, u32[]{:S(2)}, u32[]{:S(2)}) collective-permute-start(f32[1,128,128]{2,1,0:T(8,128)S(1)} %get-tuple-element.67), channel_id=1, source_target_pairs={{0,4},{4,8},{8,12},{12,16},{16,20},{20,24},{24,28},{1,5},{5,9},{9,... | collective-permute-start | bytes 196616 | tf_op jit(solution)/shard_map/ppermute | solution.py:14
  61.0 6.2 %collective-permute-start.9 = (f32[1,128,128]{2,1,0:T(8,128)S(1)}, f32[1,128,128]{2,1,0:T(8,128)S(1)}, u32[]{:S(2)}, u32[]{:S(2)}) collective-permute-start(f32[1,128,128]{2,1,0:T(8,128)S(1)} %get-tuple-element.68), channel_id=1, source_target_pairs={{4,0},{8,4},{12,8},{16,12},{20,16},{24,20},{28,24},{5,1},{9,5},{13... | collective-permute-start | bytes 196616 | tf_op jit(solution)/shard_map/ppermute | solution.py:15
  67.2 4.4 %collective-permute-start.10 = (f32[18,1,128]{2,1,0:T(1,128)S(1)}, f32[18,1,128]{2,1,0:T(1,128)S(1)}, u32[]{:S(2)}, u32[]{:S(2)}) collective-permute-start(f32[18,1,128]{2,1,0:T(1,128)S(1)} %get-tuple-element.63), channel_id=1, source_target_pairs={{0,1},{1,2},{2,3},{4,5},{5,6},{6,7},{8,9},{9,10},{10,11},{12,13},{... | collective-permute-start | bytes 27656 | tf_op jit(solution)/shard_map/ppermute | solution.py:14
  70.1 4.0 %collective-permute-start.11 = (f32[18,1,128]{2,1,0:T(1,128)S(1)}, f32[18,1,128]{2,1,0:T(1,128)S(1)}, u32[]{:S(2)}, u32[]{:S(2)}) collective-permute-start(f32[18,1,128]{2,1,0:T(1,128)S(1)} %get-tuple-element.64), channel_id=1, source_target_pairs={{1,0},{2,1},{3,2},{5,4},{6,5},{7,6},{9,8},{10,9},{11,10},{13,12},{... | collective-permute-start | bytes 27656 | tf_op jit(solution)/shard_map/ppermute | solution.py:15
where the time goes:
time: 124 us; the launch traced here: 123 us
  blocking collectives  41 us (33%)
  waiting for transfers between devices  35.1 us (28%)
  starting transfers between devices  29.9 us (24%)
  other arithmetic  14 us (11%)
  between operations  2.25 us (2%)
    psum x1, blocking collectives, on_device(): inner_rz = lax.psum(jnp.sum(right_side * precond), ('gx', 'gy'))  41 us
    ppermute x4, waiting for transfers between devices, extended(): before = lax.ppermute(last, axis, up)  16.3 us
    ppermute x4, starting transfers between devices, extended(): before = lax.ppermute(last, axis, up)  14 us
    ppermute x4, starting transfers between devices, passed_along(): lax.ppermute(value, axis, [(source, source + steps) for source in range(l...  10.8 us
    ppermute x4, waiting for transfers between devices, extended(): after = lax.ppermute(leading, axis, down)  10.4 us
    ppermute x4, waiting for transfers between devices, passed_along(): lax.ppermute(value, axis, [(source, source + steps) for source in range(l...  8.35 us
    ppermute x4, starting transfers between devices, extended(): after = lax.ppermute(leading, axis, down)  5.17 us
    reduce_sum x1, other arithmetic, on_device(): inner_pq = lax.psum(jnp.sum(precond * image), ('gx', 'gy'))  4.08 us
  transfers between devices with their start and end apart: 12, of which 8 were waited for; matrix products, arithmetic and copies ran while one was open for 0% of the time, Pallas kernels for 0%

commit v1 on v0

v1 whole, which is shorter than its diff:
```python
import jax
import jax.numpy as jnp
from jax import lax
from jax.experimental import pallas as pl
from jax.experimental.pallas import tpu as pltpu
from jax.sharding import PartitionSpec as P

F32 = jnp.float32
HALO = 8
LOW = 2 * HALO
TINY = 1e-30
ANY = pl.BlockSpec(memory_space=pl.ANY)
VMEM = pl.BlockSpec(memory_space=pltpu.VMEM)


def params():
    return pltpu.CompilerParams(vmem_limit_bytes=48 << 20)


def shape(*dims):
    return jax.ShapeDtypeStruct(dims, F32)


def ordered(first_pair_partner, count):
    return [(i, first_pair_partner(i) % count) for i in range(count)]


def swap_even(value, axis):
    count = lax.axis_size(axis)
    return lax.ppermute(value, axis, ordered(lambda i: i ^ 1, count))


def swap_odd(value, axis):
    count = lax.axis_size(axis)
    return lax.ppermute(value, axis, ordered(lambda i: ((i + 1) ^ 1) - 1, count))


def place(axis):
    index, count = lax.axis_index(axis), lax.axis_size(axis)
    odd = lax.rem(index, 2) == 1
    has_low = (index > 0).astype(F32)
    has_high = (index < count - 1).astype(F32)
    return odd, has_low, has_high


def z_sum(value):
    lane = lax.broadcasted_iota(jnp.int32, value.shape, 1)
    last = value.shape[1] - 1
    below = jnp.where(lane > 0, pltpu.roll(value, 1, 1), 0.0)
    above = jnp.where(lane < last, pltpu.roll(value, last, 1), 0.0)
    return below + above


def pack_kernel(cond, resid, x_even, x_odd, y_even, y_odd, sem):
    layers, rows, _ = cond.shape
    copies = []
    for axis, outs in (("gx", (x_even, x_odd)), ("gy", (y_even, y_odd))):
        odd = lax.rem(lax.axis_index(axis), 2)
        for out, high in zip(outs, (1 - odd, odd)):
            if axis == "gx":
                two = pl.ds(high * (layers - 2), 2)
                one = pl.ds(high * (layers - 1), 1)
                copies.append((cond.at[two], out.at[pl.ds(0, 2)]))
                copies.append((resid.at[one], out.at[pl.ds(2, 1)]))
            else:
                tile = pl.ds(pl.multiple_of(high * (rows - HALO), HALO), HALO)
                copies.append((cond.at[:, tile], out.at[:, pl.ds(0, HALO)]))
                copies.append((resid.at[:, tile], out.at[:, pl.ds(HALO, HALO)]))
    started = [
        pltpu.make_async_copy(source, target, sem.at[i])
        for i, (source, target) in enumerate(copies)
    ]
    for copy in started:
        copy.start()
    for copy in started:
        copy.wait()


def pack(cond, resid):
    layers, rows, lanes = cond.shape
    x_out, y_out = shape(3, rows, lanes), shape(layers, 2 * HALO, lanes)
    return pl.pallas_call(
        pack_kernel,
        out_shape=(x_out, x_out, y_out, y_out),
        in_specs=[ANY, ANY],
        out_specs=(ANY, ANY, ANY, ANY),
        scratch_shapes=[pltpu.SemaphoreType.DMA((8,))],
        compiler_params=params(),
        name="pack",
    )(cond, resid)


def y_tiles(y_even, y_odd, layer, part):
    odd, has_low, has_high = place("gy")
    rows = pl.ds(part * HALO, HALO)
    first, second = y_even[layer, rows], y_odd[layer, rows]
    south = jnp.where(odd, first, second) * has_low
    north = jnp.where(odd, second, first) * has_high
    return south, north


def edge_kernel(u_low, u_high, r_low, r_high, y_even, y_odd, t_even, t_odd, grown):
    layers, rows = y_even.shape[0], u_low.shape[1]
    odd = place("gx")[0]
    end = HALO + rows
    sends = []
    for side in range(2):
        u_side, r_side = ((u_low, r_low), (u_high, r_high))[side]
        locals_ = ((0, 1, 2), (3, 2, 1))[side]
        layer_of = ((0, 1, 2), (layers - 1, layers - 2, layers - 3))[side]
        south, north = y_tiles(y_even, y_odd, layer_of[1], 0)
        grown[side, 0:HALO] = south
        grown[side, HALO:end] = u_side[locals_[1]]
        grown[side, end : end + HALO] = north
        middle = u_side[locals_[1]]
        edge = u_side[locals_[0]]
        total = 6.0 * middle + edge + u_side[locals_[2]] + z_sum(middle)
        total = total + grown[side, HALO - 1 : end - 1] + grown[side, HALO + 1 : end + 1]
        term = (edge + middle) * (2.0 * r_side[0] / total)
        edge_south, edge_north = y_tiles(y_even, y_odd, layer_of[0], 0)
        r_south, r_north = y_tiles(y_even, y_odd, layer_of[0], 1)
        corner = jnp.concatenate(
            [
                edge_south[HALO - 1 : HALO],
                edge_south[HALO - 2 : HALO - 1],
                south[HALO - 1 : HALO],
                r_south[HALO - 1 : HALO],
                edge_north[0:1],
                edge_north[1:2],
                north[0:1],
                r_north[0:1],
            ],
            axis=0,
        )
        sends.append((term, corner))
    (t_low, c_low), (t_high, c_high) = sends
    t_even[0:rows] = jnp.where(odd, t_low, t_high)
    t_even[rows : rows + 8] = jnp.where(odd, c_low, c_high)
    t_odd[0:rows] = jnp.where(odd, t_high, t_low)
    t_odd[rows : rows + 8] = jnp.where(odd, c_high, c_low)


def edge_terms(cond, resid, y_even, y_odd):
    layers, rows, lanes = cond.shape
    four, one = (4, rows, lanes), (1, rows, lanes)
    whole = pl.BlockSpec(y_even.shape, lambda i: (0, 0, 0))
    out = pl.BlockSpec((rows + 8, lanes), lambda i: (0, 0))
    return pl.pallas_call(
        edge_kernel,
        grid=(1,),
        out_shape=(shape(rows + 8, lanes), shape(rows + 8, lanes)),
        in_specs=[
            pl.BlockSpec(four, lambda i: (0, 0, 0)),
            pl.BlockSpec(four, lambda i: (layers // 4 - 1, 0, 0)),
            pl.BlockSpec(one, lambda i: (1, 0, 0)),
            pl.BlockSpec(one, lambda i: (layers - 2, 0, 0)),
            whole,
            whole,
        ],
        out_specs=(out, out),
        scratch_shapes=[pltpu.VMEM((2, rows + 2 * HALO, lanes), F32)],
        compiler_params=params(),
        name="edge_terms",
    )(cond, cond, resid, resid, y_even, y_odd)


def row_chunks(rows):
    total = rows + 2 * HALO
    step = total // 3 if total % 24 == 0 else total
    return [(HALO + i * step, step) for i in range(total // step)]


def own_chunks(rows):
    step = 32 if rows % 32 == 0 else rows
    return [(LOW + i * step, step) for i in range(rows // step)]


def fill_rows(masks, rows):
    _, has_low, has_high = place("gy")
    row = lax.broadcasted_iota(jnp.int32, masks.shape[1:], 0) - LOW
    inside = jnp.where(row < 0, has_low, jnp.where(row >= rows, has_high, 1.0))
    near_low, near_high = row < 2, row >= rows - 2
    count = jnp.where(near_low, 1.0 + has_low, jnp.where(near_high, 1.0 + has_high, 1.0))
    masks[0] = inside
    masks[1] = count
    masks[2] = jnp.where(row == rows - 2, 1.0 / (1.0 + has_high), 1.0)
    masks[3] = jnp.where(row == 1, 1.0 / (1.0 + has_low), 1.0)


def is_plain(start, size, rows):
    return start >= LOW + 2 and start + size <= LOW + rows - 2


def eight(value):
    return jnp.sum(value.reshape(value.shape[0] // 8, 8, value.shape[1]), axis=0)


def inner_kernel(
    cond, resid, y_even, y_odd,
    p_out, i_out, e_u, e_r, e_v, e_i, e_d, e_p, sums,
    u, r, inv, v, w, d, p, q, masks, sem,
):
    layers, rows = cond.shape[0], cond.shape[1]
    own = pl.ds(LOW, rows)
    loads = [
        pltpu.make_async_copy(cond, u.at[:, own], sem.at[0]),
        pltpu.make_async_copy(resid, r.at[:, own], sem.at[1]),
    ]
    for copy in loads:
        copy.start()
    fill_rows(masks, rows)

    def halo(k, carry):
        for part, target in enumerate((u, r)):
            south, north = y_tiles(y_even, y_odd, k, part)
            target[k, HALO:LOW] = south
            target[k, LOW + rows : LOW + rows + HALO] = north
        return carry

    lax.fori_loop(0, layers, halo, 0)
    for copy in loads:
        copy.wait()
    chunks = row_chunks(rows)

    def first(k, carry):
        for start, size in chunks:
            here = slice(start, start + size)
            down, up = slice(start - 1, start + size - 1), slice(start + 1, start + size + 1)
            mid = u[k, here]
            total = 6.0 * mid + u[k - 1, here] + u[k + 1, here]
            total = total + u[k, down] + u[k, up] + z_sum(mid)
            inverse = 1.0 / jnp.maximum(total, TINY)
            if not is_plain(start, size, rows):
                inverse = inverse * masks[0, here]
            value = 2.0 * r[k, here] * inverse
            d[k, here] = total
            inv[k, here] = inverse
            v[k, here] = value
            w[k, here] = mid * value
        return carry

    lax.fori_loop(1, layers - 1, first, 0)

    def second(k, carry):
        for start, size in chunks:
            here = slice(start, start + size)
            down, up = slice(start - 1, start + size - 1), slice(start + 1, start + size + 1)
            mid = u[k, here]
            total = 2.0 * r[k, here]
            total = total + mid * (v[k - 1, here] + v[k + 1, here] + z_sum(v[k, here]))
            total = total + (w[k - 1, here] + w[k + 1, here] + z_sum(w[k, here]))
            south = mid * v[k, down] + w[k, down]
            north = mid * v[k, up] + w[k, up]
            if is_plain(start, size, rows):
                value = inv[k, here] * (total + south + north)
            else:
                total = total + masks[2, here] * south + masks[3, here] * north
                value = masks[1, here] * inv[k, here] * total
            p[k, here] = value
            q[k, here] = mid * value
        return carry

    lax.fori_loop(2, layers - 2, second, 0)

    def third(k, carry):
        rz, pq = carry
        for start, size in own_chunks(rows):
            here = slice(start, start + size)
            down, up = slice(start - 1, start + size - 1), slice(start + 1, start + size + 1)
            mid = p[k, here]
            around = p[k - 1, here] + p[k + 1, here] + p[k, down] + p[k, up] + z_sum(mid)
            scaled = q[k - 1, here] + q[k + 1, here] + q[k, down] + q[k, up]
            scaled = scaled + z_sum(q[k, here])
            image = d[k, here] * mid - u[k, here] * around - scaled
            i_out[k, start - LOW : start - LOW + size] = image
            p_out[k, start - LOW : start - LOW + size] = mid
            rz = rz + eight(r[k, here] * mid)
            pq = pq + eight(mid * image)
        return rz, pq

    zero = jnp.zeros((8, u.shape[2]), F32)
    rz, pq = lax.fori_loop(3, layers - 3, third, (zero, zero))
    sums[0] = rz
    sums[1] = pq
    full = slice(HALO, LOW + rows + HALO)
    for side in range(2):
        order = (0, 1, 2, 3) if side == 0 else tuple(layers - 1 - k for k in range(4))
        for k in range(4):
            e_u[side, k, full] = u[order[k], full]
        for k in range(3):
            e_r[side, k, full] = r[order[k], full]
        for k in range(2):
            e_v[side, k, full] = v[order[k + 1], full]
            e_d[side, k, full] = d[order[k + 1], full]
            e_p[side, k, full] = p[order[k + 2], full]
        e_i[side, 0, full] = inv[order[1], full]


def inner(cond, resid, y_even, y_odd):
    layers, rows, lanes = cond.shape
    grown = rows + 4 * HALO
    field = pltpu.VMEM((layers, grown, lanes), F32)

    def edge(count):
        return shape(2, count, grown, lanes)

    outs = (
        shape(layers, rows, lanes), shape(layers, rows, lanes),
        edge(4), edge(3), edge(2), edge(1), edge(2), edge(2), shape(2, 8, lanes),
    )
    return pl.pallas_call(
        inner_kernel,
        out_shape=outs,
        in_specs=[ANY, ANY, VMEM, VMEM],
        out_specs=(VMEM,) * len(outs),
        scratch_shapes=[field] * 8
        + [pltpu.VMEM((4, grown, lanes), F32), pltpu.SemaphoreType.DMA((2,))],
        compiler_params=params(),
        name="inner",
    )(cond, resid, y_even, y_odd)


def outer_kernel(
    p_in, i_in, e_u, e_r, e_v, e_i, e_d, e_p, sums, x_even, x_odd, t_even, t_odd,
    p_out, i_out, total_out,
    u, r, v, w, p, q, d, t, masks,
):
    layers, rows = p_in.shape[0], p_in.shape[1]
    odd, has_low, has_high = place("gx")
    fill_rows(masks, rows)
    own = slice(LOW, LOW + rows)
    zero = jnp.zeros((8, u.shape[2]), F32)
    rz, pq = sums[0], sums[1]
    chunks = row_chunks(rows)
    for side in range(2):
        has = (has_low, has_high)[side]
        pick = jnp.logical_xor(odd, side == 1)
        twice = 1.0 + has

        def arrived(first, second):
            return jnp.where(pick, first, second) * has

        near, far = (1, 0) if side == 0 else (0, 1)
        for slot, source in ((0, far), (1, near)):
            u[slot, own] = arrived(x_even[source], x_odd[source])
        r[own] = arrived(x_even[2], x_odd[2])
        t[own] = arrived(t_even[0:rows], t_odd[0:rows])
        corner = arrived(t_even[rows : rows + 8], t_odd[rows : rows + 8])
        low, high = slice(HALO, LOW), slice(LOW + rows, LOW + rows + HALO)
        row = lax.broadcasted_iota(jnp.int32, zero.shape, 0)

        def one(k):
            return jnp.broadcast_to(corner[k : k + 1], zero.shape)

        u[1, low] = jnp.where(row == 7, one(0), jnp.where(row == 6, one(1), 0.0))
        u[0, low] = jnp.where(row == 7, one(2), 0.0)
        r[low] = jnp.where(row == 7, one(3), 0.0)
        u[1, high] = jnp.where(row == 0, one(4), jnp.where(row == 1, one(5), 0.0))
        u[0, high] = jnp.where(row == 0, one(6), 0.0)
        r[high] = jnp.where(row == 0, one(7), 0.0)
        t[low] = zero
        t[high] = zero

        for start, size in chunks:
            here = slice(start, start + size)
            down, up = slice(start - 1, start + size - 1), slice(start + 1, start + size + 1)
            inside = masks[0, here]
            mid, edge = u[1, here], e_u[side, 0, here]
            total = 6.0 * mid + u[0, here] + edge + u[1, down] + u[1, up] + z_sum(mid)
            inverse = has * inside / jnp.maximum(total, TINY)
            value = 2.0 * r[here] * inverse
            d[1, here] = inverse
            v[0, here] = value
            w[0, here] = mid * value
            total = 6.0 * edge + mid + e_u[side, 1, here]
            total = total + e_u[side, 0, down] + e_u[side, 0, up] + z_sum(edge)
            inverse = inside / jnp.maximum(total, TINY)
            value = 2.0 * e_r[side, 0, here] * inverse
            d[0, here] = total
            d[2, here] = inverse
            v[1, here] = value
            w[1, here] = edge * value

        for start, size in chunks:
            here = slice(start, start + size)
            down, up = slice(start - 1, start + size - 1), slice(start + 1, start + size + 1)
            plain = is_plain(start, size, rows)

            def finish(mid, total, south, north, inverse, slot, twice):
                if plain:
                    value = twice * inverse * (total + south + north)
                else:
                    total = total + masks[2, here] * south + masks[3, here] * north
                    value = twice * masks[1, here] * inverse * total
                p[slot, here] = value
                q[slot, here] = mid * value

            mid = u[1, here]
            total = 2.0 * r[here] + t[here]
            total = total + mid * (v[1, here] + z_sum(v[0, here]))
            total = total + w[1, here] + z_sum(w[0, here])
            south = mid * v[0, down] + w[0, down]
            north = mid * v[0, up] + w[0, up]
            finish(mid, total, south, north, d[1, here], 0, twice)

            mid, next_u = e_u[side, 0, here], e_u[side, 1, here]
            next_v = e_v[side, 0, here]
            total = 2.0 * e_r[side, 0, here]
            total = total + mid * (v[0, here] + next_v + z_sum(v[1, here]))
            total = total + w[0, here] + next_u * next_v + z_sum(w[1, here])
            south = mid * v[1, down] + w[1, down]
            north = mid * v[1, up] + w[1, up]
            finish(mid, total, south, north, d[2, here], 1, twice)

            inner_v = e_v[side, 1, here]
            total = 2.0 * e_r[side, 1, here]
            total = total + next_u * (v[1, here] + z_sum(next_v))
            total = total + w[1, here] + z_sum(next_u * next_v)
            total = total + (next_u * inner_v + e_u[side, 2, here] * inner_v) / twice
            south = (next_u + e_u[side, 1, down]) * e_v[side, 0, down]
            north = (next_u + e_u[side, 1, up]) * e_v[side, 0, up]
            finish(next_u, total, south, north, e_i[side, 0, here], 2, twice)

        for start, size in own_chunks(rows):
            here = slice(start, start + size)
            down, up = slice(start - 1, start + size - 1), slice(start + 1, start + size + 1)
            out_rows = slice(start - LOW, start - LOW + size)
            for k in range(3):
                layer = k if side == 0 else layers - 1 - k
                mid_u = e_u[side, k, here]
                if k < 2:
                    mid = p[k + 1, here]
                    near_y = p[k + 1, down] + p[k + 1, up]
                    near_q = q[k + 1, down] + q[k + 1, up]
                    mid_q = q[k + 1, here]
                    before_p, before_q = p[k, here], q[k, here]
                    if k == 0:
                        after_p, after_q = p[2, here], q[2, here]
                    else:
                        after_p = e_p[side, 0, here]
                        after_q = e_u[side, 2, here] * after_p
                else:
                    mid = e_p[side, 0, here]
                    mid_q = mid_u * mid
                    low_p, high_p = e_p[side, 0, down], e_p[side, 0, up]
                    near_y = low_p + high_p
                    near_q = e_u[side, 2, down] * low_p + e_u[side, 2, up] * high_p
                    before_p, before_q = p[2, here], q[2, here]
                    after_p = e_p[side, 1, here]
                    after_q = None
                around = before_p + after_p + near_y + z_sum(mid)
                if after_q is None:
                    after_q = e_u[side, 3, here] * after_p
                scaled = before_q + after_q + near_q + z_sum(mid_q)
                total = d[0, here] if k == 0 else e_d[side, k - 1, here]
                image = total * mid - mid_u * around - scaled
                p_out[layer, out_rows] = mid
                i_out[layer, out_rows] = image
                rz = rz + eight(e_r[side, k, here] * mid)
                pq = pq + eight(mid * image)
    total_out[0:1] = jnp.broadcast_to(jnp.sum(rz, keepdims=True), (1, zero.shape[1]))
    total_out[1:2] = jnp.broadcast_to(jnp.sum(pq, keepdims=True), (1, zero.shape[1]))


def outer(found, x_even, x_odd, t_even, t_odd):
    p_in = found[0]
    layers, rows, lanes = p_in.shape
    grown = rows + 4 * HALO

    def field(*lead):
        return pltpu.VMEM((*lead, grown, lanes), F32)

    return pl.pallas_call(
        outer_kernel,
        out_shape=(shape(layers, rows, lanes), shape(layers, rows, lanes), shape(2, lanes)),
        in_specs=[VMEM] * 13,
        out_specs=(VMEM, VMEM, VMEM),
        scratch_shapes=[
            field(2), field(), field(2), field(2), field(3), field(3), field(3), field(), field(4),
        ],
        input_output_aliases={0: 0, 1: 1},
        compiler_params=params(),
        name="outer",
    )(*found, x_even, x_odd, t_even, t_odd)


def power_of_two(count):
    return count & (count - 1) == 0


def sum_everywhere(value):
    count_x, count_y = lax.axis_size("gx"), lax.axis_size("gy")
    if not (power_of_two(count_x) and power_of_two(count_y)):
        return lax.psum(value, ("gx", "gy"))
    low = 1 if count_y > 1 else 0
    steps = [(0, 1 << bit | low) for bit in range(count_y.bit_length() - 1)]
    steps += [(1 << bit, low) for bit in range(count_x.bit_length() - 1)]
    for step_x, step_y in steps:
        pairs = [
            (x * count_y + y, (x ^ step_x) * count_y + (y ^ step_y))
            for x in range(count_x)
            for y in range(count_y)
        ]
        value = value + lax.ppermute(value, ("gx", "gy"), pairs)
    return value


def on_device(right_side, conductivity):
    x_even, x_odd, y_even, y_odd = pack(conductivity, right_side)
    x_even = swap_even(x_even, "gx")
    y_even = swap_even(y_even, "gy")
    y_odd = swap_odd(y_odd, "gy")
    x_odd = swap_odd(x_odd, "gx")
    t_even, t_odd = edge_terms(conductivity, right_side, y_even, y_odd)
    t_even = swap_even(t_even, "gx")
    t_odd = swap_odd(t_odd, "gx")
    found = inner(conductivity, right_side, y_even, y_odd)
    precond, image, sums = outer(found, x_even, x_odd, t_even, t_odd)
    sums = sum_everywhere(sums)
    half_alpha = sums[0, 0] / sums[1, 0]
    return (2.0 * half_alpha) * precond, right_side - half_alpha * image


def solution(mesh):
    in_specs = (P("gx", "gy", None), P("gx", "gy", None))
    out_specs = (P("gx", "gy", None), P("gx", "gy", None))
    return jax.shard_map(
        on_device, mesh=mesh, in_specs=in_specs, out_specs=out_specs, check_vma=False
    )
```

time: 124 us -> 41.3 us (0.33)
  blocking collectives: 41 us -> 0 us
  waiting for transfers between devices: 35.1 us -> 11.3 us
  starting transfers between devices: 29.9 us -> 14.7 us
  other arithmetic: 14 us -> 1.54 us
  Pallas kernels: 0 us -> 8.46 us
  local copies, waits for them, and re-layouts: 0.74 us -> 2.97 us
    psum x1 -> x0, blocking collectives: 41 us -> none  [on_device(): inner_rz = lax.psum(jnp.sum(right_side * precond), ('gx', 'gy'))]
    ppermute x12 -> x11, waiting for transfers between devices: 35.1 us -> 11.3 us  [the longest x5 11.3 us: sum_everywhere(): value = value + lax.ppermute(value, ('gx', 'gy'), pairs)]
    ppermute x12 -> x11, starting transfers between devices: 29.9 us -> 14.7 us  [the longest x3 9.7 us: swap_odd(): return lax.ppermute(value, axis, ordered(lambda i: (i + 1 ^ 1) - 1, count))]
    pallas_call x0 -> x4, Pallas kernels: none -> 8.46 us  [the longest x1 6.31 us: inner(): pl.pallas_call(inner_kernel, out_shape=outs, in_specs=[ANY, ANY, VMEM, VM...]
    reduce_sum x1 -> x0, other arithmetic: 4.08 us -> none  [on_device(): inner_pq = lax.psum(jnp.sum(precond * image), ('gx', 'gy'))]
    mul x1 -> x0, other arithmetic: 3.11 us -> none  [on_device(): solved = two_sweeps(box_coeffs, box_diag, box_resid) * inside]
    unnamed x4 -> x6, local copies, waits for them, and re-layouts: 0.01 us -> 2.45 us
    slice x3 -> x0, other arithmetic: 2.2 us -> none  [extended(): last = lax.slice_in_dim(array, length - width, length, axis=dim)]
  transfers between devices with their start and end apart: 12 -> 11, of which waited for: 8 -> 5; matrix products, arithmetic and copies ran while one was open for 0% -> 0% of each run, Pallas kernels for 0% -> 16%
where the time goes in v1:
time: 41.3 us; the launch traced here: 41.1 us
  starting transfers between devices  14.7 us (36%)
  waiting for transfers between devices  11.3 us (27%)
  Pallas kernels  8.46 us (20%)
  local copies, waits for them, and re-layouts  2.97 us (7%)
  between operations  2.07 us (5%)
  other arithmetic  1.54 us (4%)
    ppermute x5, waiting for transfers between devices, sum_everywhere(): value = value + lax.ppermute(value, ('gx', 'gy'), pairs)  11.3 us
    ppermute x3, starting transfers between devices, swap_odd(): return lax.ppermute(value, axis, ordered(lambda i: (i + 1 ^ 1) - 1, count))  9.7 us
    pallas_call x1, Pallas kernels, inner(): pl.pallas_call(inner_kernel, out_shape=outs, in_specs=[ANY, ANY, VMEM, VM...  6.31 us
    ppermute x5, starting transfers between devices, sum_everywhere(): value = value + lax.ppermute(value, ('gx', 'gy'), pairs)  2.76 us
    unnamed x6, local copies, waits for them, and re-layouts  2.45 us
    ppermute x3, starting transfers between devices, swap_even(): return lax.ppermute(value, axis, ordered(lambda i: i ^ 1, count))  2.23 us
    sub x1, other arithmetic, on_device(): return (2.0 * half_alpha * precond, right_side - half_alpha * image)  1.53 us
    pallas_call x1, Pallas kernels, outer(): pl.pallas_call(outer_kernel, out_shape=(shape(layers, rows, lanes), shape...  1.4 us
  transfers between devices with their start and end apart: 11, of which 5 were waited for; matrix products, arithmetic and copies ran while one was open for 0% of the time, Pallas kernels for 16%

profile of v1, /device:TPU:0, one launch (start us, length us, event | category | flops | bytes accessed | tf_op | source)
XLA Modules:
  0.0 41.1 jit_solution(3179007516501527801)
XLA Ops:
  0.6 0.0 copy-start
  0.6 1.2 %copy-done = f32[16,128,128]{2,1,0:T(8,128)S(1)} copy-done((f32[16,128,128]{2,1,0:T(8,128)S(1)}, f32[16,128,128]{2,1,0:T(8,128)}, u32[]{:S(2)}) %copy-start) | copy-done | bytes 1048600
  1.9 0.0 copy-start.2
  1.9 1.2 %copy-done.2 = f32[16,128,128]{2,1,0:T(8,128)S(1)} copy-done((f32[16,128,128]{2,1,0:T(8,128)S(1)}, f32[16,128,128]{2,1,0:T(8,128)}, u32[]{:S(2)}) %copy-start.2) | copy-done | bytes 1048600
  3.1 0.6 %pack.1 = (f32[3,128,128]{2,1,0:T(8,128)S(1)}, f32[3,128,128]{2,1,0:T(8,128)S(1)}, f32[16,16,128]{2,1,0:T(8,128)S(1)}, f32[16,16,128]{2,1,0:T(8,128)S(1)}) custom-call(f32[16,128,128]{2,1,0:T(8,128)S(1)} %copy-done.2, f32[16,128,128]{2,1,0:T(8,128)S(1)} %copy-done), custom_call_target="tpu_custom_call" | custom-call | tf_op jit(solution)/shard_map/pack/pallas_call | solution.py:82
  3.7 0.5 %collective-permute-start = (f32[16,16,128]{2,1,0:T(8,128)S(1)}, f32[16,16,128]{2,1,0:T(8,128)S(1)}, u32[]{:S(2)}, u32[]{:S(2)}) collective-permute-start(f32[16,16,128]{2,1,0:T(8,128)S(1)} %get-tuple-element.20), channel_id=1, source_target_pairs={{0,1},{1,0},{2,3},{3,2},{4,5},{5,4},{6,7},{7,6},{8,9},{9,8},{10,11... | collective-permute-start | bytes 393224 | tf_op jit(solution)/shard_map/ppermute | solution.py:30
  4.2 2.6 %collective-permute-start.1 = (f32[16,16,128]{2,1,0:T(8,128)S(1)}, f32[16,16,128]{2,1,0:T(8,128)S(1)}, u32[]{:S(2)}, u32[]{:S(2)}) collective-permute-start(f32[16,16,128]{2,1,0:T(8,128)S(1)} %get-tuple-element.21), channel_id=1, source_target_pairs={{0,3},{1,2},{2,1},{3,0},{4,7},{5,6},{6,5},{7,4},{8,11},{9,10},{10,... | collective-permute-start | bytes 393224 | tf_op jit(solution)/shard_map/ppermute | solution.py:35
  6.8 1.5 %collective-permute-start.2 = (f32[3,128,128]{2,1,0:T(8,128)S(1)}, f32[3,128,128]{2,1,0:T(8,128)S(1)}, u32[]{:S(2)}, u32[]{:S(2)}) collective-permute-start(f32[3,128,128]{2,1,0:T(8,128)S(1)} %get-tuple-element.31), channel_id=1, source_target_pairs={{0,4},{4,0},{8,12},{12,8},{16,20},{20,16},{24,28},{28,24},{1,5},{5... | collective-permute-start | bytes 589832 | tf_op jit(solution)/shard_map/ppermute | solution.py:30
  8.3 3.5 %collective-permute-start.3 = (f32[3,128,128]{2,1,0:T(8,128)S(1)}, f32[3,128,128]{2,1,0:T(8,128)S(1)}, u32[]{:S(2)}, u32[]{:S(2)}) collective-permute-start(f32[3,128,128]{2,1,0:T(8,128)S(1)} %get-tuple-element.32), channel_id=1, source_target_pairs={{0,28},{4,8},{8,4},{12,16},{16,12},{20,24},{24,20},{28,0},{1,29},{... | collective-permute-start | bytes 589832 | tf_op jit(solution)/shard_map/ppermute | solution.py:35
  11.9 0.0 collective-permute-done.y_even
  11.9 0.0 collective-permute-done.1.y_odd
  11.9 0.2 edge_terms.1
  12.1 0.2 collective-permute-start.4
  12.3 3.5 %collective-permute-start.5 = (f32[136,128]{1,0:T(8,128)S(1)}, f32[136,128]{1,0:T(8,128)S(1)}, u32[]{:S(2)}, u32[]{:S(2)}) collective-permute-start(f32[136,128]{1,0:T(8,128)S(1)} %get-tuple-element.34), channel_id=1, source_target_pairs={{0,28},{4,8},{8,4},{12,16},{16,12},{20,24},{24,20},{28,0},{1,29},{... | collective-permute-start | bytes 208904 | tf_op jit(solution)/shard_map/ppermute | solution.py:35
  15.8 6.3 %inner.1 = (f32[16,128,128]{2,1,0:T(8,128)S(1)}, f32[16,128,128]{2,1,0:T(8,128)S(1)}, f32[2,4,160,128]{3,2,1,0:T(8,128)S(1)}, f32[2,3,160,128]{3,2,1,0:T(8,128)S...) custom-call(f32[16,128,128]{2,1,0:T(8,128)S(1)} %copy-done.2, ...), custom_call_target="tpu_custom_call" | custom-call | tf_op jit(solution)/shard_map/inner/pallas_call | solution.py:311
  22.1 0.0 collective-permute-done.2.x_even
  22.1 0.0 collective-permute-done.3.x_odd
  22.1 0.0 collective-permute-done.4.t_even
  22.1 0.0 collective-permute-done.5.t_odd
  22.2 0.0 copy-start.1
  22.2 1.4 %outer.1 = (f32[16,128,128]{2,1,0:T(8,128)S(1)}, f32[16,128,128]{2,1,0:T(8,128)S(1)}, f32[2,128]{1,0:T(2,128)S(1)}) custom-call(f32[16,128,128]{2,1,0:T(8,128)S(1)} %get-tuple-element.22.p_in, f32[16,128,128]{2,1,0:T(8,128)S(1)} %get-tuple-element.23.i_in, ...), custom_call_target="tpu_custom_call", output_to_operand_aliasing={{0}: (0, {}), {1}: (1, {})} | custom-call | tf_op jit(solution)/shard_map/outer/pallas_call | solution.py:473
  23.6 0.2 collective-permute-start.6
  23.8 1.0 %collective-permute-done.6 = f32[2,128]{1,0:T(2,128)S(1)} collective-permute-done((f32[2,128]{1,0:T(2,128)S(1)}, f32[2,128]{1,0:T(2,128)S(1)}, u32[]{:S(2)}, u32[]{:S(2)}) %collective-permute-start.6) | collective-permute-done | bytes 1056 | tf_op jit(solution)/shard_map/ppermute | solution.py:504
  24.8 1.3 %collective-permute-start.7 = (f32[2,128]{1,0:T(2,128)S(1)}, f32[2,128]{1,0:T(2,128)S(1)}, u32[]{:S(2)}, u32[]{:S(2)}) collective-permute-start(f32[2,128]{1,0:T(2,128)S(1)} %add.15), channel_id=1, source_target_pairs={{0,3},{1,2},{2,1},{3,0},{4,7},{5,6},{6,5},{7,4},{8,11},{9,10},{10,... | collective-permute-start | bytes 3080 | tf_op jit(solution)/shard_map/ppermute | solution.py:504
  26.1 1.7 %collective-permute-done.7 = f32[2,128]{1,0:T(2,128)S(1)} collective-permute-done((f32[2,128]{1,0:T(2,128)S(1)}, f32[2,128]{1,0:T(2,128)S(1)}, u32[]{:S(2)}, u32[]{:S(2)}) %collective-permute-start.7) | collective-permute-done | bytes 1056 | tf_op jit(solution)/shard_map/ppermute | solution.py:504
  27.8 0.0 collective-permute-start.8
  27.8 3.0 %collective-permute-done.8 = f32[2,128]{1,0:T(2,128)S(1)} collective-permute-done((f32[2,128]{1,0:T(2,128)S(1)}, f32[2,128]{1,0:T(2,128)S(1)}, u32[]{:S(2)}, u32[]{:S(2)}) %collective-permute-start.8) | collective-permute-done | bytes 1056 | tf_op jit(solution)/shard_map/ppermute | solution.py:504
  30.8 0.1 collective-permute-start.9
  30.9 2.9 %collective-permute-done.9 = f32[2,128]{1,0:T(2,128)S(1)} collective-permute-done((f32[2,128]{1,0:T(2,128)S(1)}, f32[2,128]{1,0:T(2,128)S(1)}, u32[]{:S(2)}, u32[]{:S(2)}) %collective-permute-start.9) | collective-permute-done | bytes 1056 | tf_op jit(solution)/shard_map/ppermute | solution.py:504
  33.8 1.1 %collective-permute-start.10 = (f32[2,128]{1,0:T(2,128)S(1)}, f32[2,128]{1,0:T(2,128)S(1)}, u32[]{:S(2)}, u32[]{:S(2)}) collective-permute-start(f32[2,128]{1,0:T(2,128)S(1)} %add.18), channel_id=1, source_target_pairs={{0,17},{1,16},{2,19},{3,18},{4,21},{5,20},{6,23},{7,22},{8,25},{9,... | collective-permute-start | bytes 3080 | tf_op jit(solution)/shard_map/ppermute | solution.py:504
  34.9 2.8 %collective-permute-done.10 = f32[2,128]{1,0:T(2,128)S(1)} collective-permute-done((f32[2,128]{1,0:T(2,128)S(1)}, f32[2,128]{1,0:T(2,128)S(1)}, u32[]{:S(2)}, u32[]{:S(2)}) %collective-permute-start.10) | collective-permute-done | bytes 1056 | tf_op jit(solution)/shard_map/ppermute | solution.py:504
  37.7 0.5 %fusion = (f32[1,1]{1,0:T(1,128)}, f32[1,1]{1,0:T(1,128)}) fusion(f32[2,128]{1,0:T(2,128)S(1)} %add.19), kind=kLoop, calls=%fused_computation.2 | loop fusion | bytes 16 | tf_op jit(solution)/shard_map/slice | solution.py:520
  39.5 0.0 copy-done.1
  39.5 1.5 %multiply_subtract_fusion = (f32[16,128,128]{2,1,0:T(8,128)}, f32[16,128,128]{2,1,0:T(8,128)}) fusion(f32[16,128,128]{2,1,0:T(8,128)S(1)} %copy-done.1, f32[16,128,128]{2,1,0:T(8,128)S(1)} %get-tuple-element.37, f32[]{:T(128)} %bitcast, f32[16,128,128]{2,1,0:T(8,128)S(1)} %get-tuple-element.36, f32[]{:T(128)S(6)} %mul_shard_map.3), kind=kLoop, calls=%fused_computation | loop fusion | flops 786432 | bytes 5242888 | tf_op jit(solution)/shard_map/sub | solution.py:521
  (5 shorter events, 0.0 us)
Async XLA Ops:
  0.6 1.2 %copy-start = (f32[16,128,128]{2,1,0:T(8,128)S(1)}, f32[16,128,128]{2,1,0:T(8,128)}, u32[]{:S(2)}) copy-start(f32[16,128,128]{2,1,0:T(8,128)} %r_high.1) | copy-start | bytes 3145732
  1.9 1.2 %copy-start.2 = (f32[16,128,128]{2,1,0:T(8,128)S(1)}, f32[16,128,128]{2,1,0:T(8,128)}, u32[]{:S(2)}) copy-start(f32[16,128,128]{2,1,0:T(8,128)} %u_high.1) | copy-start | bytes 3145732
  3.7 8.2 %collective-permute-start = (f32[16,16,128]{2,1,0:T(8,128)S(1)}, f32[16,16,128]{2,1,0:T(8,128)S(1)}, u32[]{:S(2)}, u32[]{:S(2)}) collective-permute-start(f32[16,16,128]{2,1,0:T(8,128)S(1)} %get-tuple-element.20), channel_id=1, source_target_pairs={{0,1},{1,0},{2,3},{3,2},{4,5},{5,4},{6,7},{7,6},{8,9},{9,8},{10,11... | collective-permute-start | bytes 393224 | tf_op jit(solution)/shard_map/ppermute | solution.py:30
  4.2 7.7 %collective-permute-start.1 = (f32[16,16,128]{2,1,0:T(8,128)S(1)}, f32[16,16,128]{2,1,0:T(8,128)S(1)}, u32[]{:S(2)}, u32[]{:S(2)}) collective-permute-start(f32[16,16,128]{2,1,0:T(8,128)S(1)} %get-tuple-element.21), channel_id=1, source_target_pairs={{0,3},{1,2},{2,1},{3,0},{4,7},{5,6},{6,5},{7,4},{8,11},{9,10},{10,... | collective-permute-start | bytes 393224 | tf_op jit(solution)/shard_map/ppermute | solution.py:35
  6.8 15.3 %collective-permute-start.2 = (f32[3,128,128]{2,1,0:T(8,128)S(1)}, f32[3,128,128]{2,1,0:T(8,128)S(1)}, u32[]{:S(2)}, u32[]{:S(2)}) collective-permute-start(f32[3,128,128]{2,1,0:T(8,128)S(1)} %get-tuple-element.31), channel_id=1, source_target_pairs={{0,4},{4,0},{8,12},{12,8},{16,20},{20,16},{24,28},{28,24},{1,5},{5... | collective-permute-start | bytes 589832 | tf_op jit(solution)/shard_map/ppermute | solution.py:30
  8.3 13.8 %collective-permute-start.3 = (f32[3,128,128]{2,1,0:T(8,128)S(1)}, f32[3,128,128]{2,1,0:T(8,128)S(1)}, u32[]{:S(2)}, u32[]{:S(2)}) collective-permute-start(f32[3,128,128]{2,1,0:T(8,128)S(1)} %get-tuple-element.32), channel_id=1, source_target_pairs={{0,28},{4,8},{8,4},{12,16},{16,12},{20,24},{24,20},{28,0},{1,29},{... | collective-permute-start | bytes 589832 | tf_op jit(solution)/shard_map/ppermute | solution.py:35
  12.1 10.1 %collective-permute-start.4 = (f32[136,128]{1,0:T(8,128)S(1)}, f32[136,128]{1,0:T(8,128)S(1)}, u32[]{:S(2)}, u32[]{:S(2)}) collective-permute-start(f32[136,128]{1,0:T(8,128)S(1)} %get-tuple-element.33), channel_id=1, source_target_pairs={{0,4},{4,0},{8,12},{12,8},{16,20},{20,16},{24,28},{28,24},{1,5},{5... | collective-permute-start | bytes 208904 | tf_op jit(solution)/shard_map/ppermute | solution.py:30
  12.3 9.9 %collective-permute-start.5 = (f32[136,128]{1,0:T(8,128)S(1)}, f32[136,128]{1,0:T(8,128)S(1)}, u32[]{:S(2)}, u32[]{:S(2)}) collective-permute-start(f32[136,128]{1,0:T(8,128)S(1)} %get-tuple-element.34), channel_id=1, source_target_pairs={{0,28},{4,8},{8,4},{12,16},{16,12},{20,24},{24,20},{28,0},{1,29},{... | collective-permute-start | bytes 208904 | tf_op jit(solution)/shard_map/ppermute | solution.py:35
  22.2 17.4 %copy-start.1 = (f32[16,128,128]{2,1,0:T(8,128)S(1)}, f32[16,128,128]{2,1,0:T(8,128)}, u32[]{:S(2)}) copy-start(f32[16,128,128]{2,1,0:T(8,128)} %r_high.1) | copy-start | bytes 3145732
  23.6 1.2 %collective-permute-start.6 = (f32[2,128]{1,0:T(2,128)S(1)}, f32[2,128]{1,0:T(2,128)S(1)}, u32[]{:S(2)}, u32[]{:S(2)}) collective-permute-start(f32[2,128]{1,0:T(2,128)S(1)} %get-tuple-element.35), channel_id=1, source_target_pairs={{0,1},{1,0},{2,3},{3,2},{4,5},{5,4},{6,7},{7,6},{8,9},{9,8},{10,11... | collective-permute-start | bytes 3080 | tf_op jit(solution)/shard_map/ppermute | solution.py:504
  24.8 3.0 %collective-permute-start.7 = (f32[2,128]{1,0:T(2,128)S(1)}, f32[2,128]{1,0:T(2,128)S(1)}, u32[]{:S(2)}, u32[]{:S(2)}) collective-permute-start(f32[2,128]{1,0:T(2,128)S(1)} %add.15), channel_id=1, source_target_pairs={{0,3},{1,2},{2,1},{3,0},{4,7},{5,6},{6,5},{7,4},{8,11},{9,10},{10,... | collective-permute-start | bytes 3080 | tf_op jit(solution)/shard_map/ppermute | solution.py:504
  27.8 3.0 %collective-permute-start.8 = (f32[2,128]{1,0:T(2,128)S(1)}, f32[2,128]{1,0:T(2,128)S(1)}, u32[]{:S(2)}, u32[]{:S(2)}) collective-permute-start(f32[2,128]{1,0:T(2,128)S(1)} %add.16), channel_id=1, source_target_pairs={{0,5},{1,4},{2,7},{3,6},{4,1},{5,0},{6,3},{7,2},{8,13},{9,12},{10,... | collective-permute-start | bytes 3080 | tf_op jit(solution)/shard_map/ppermute | solution.py:504
  30.8 3.0 %collective-permute-start.9 = (f32[2,128]{1,0:T(2,128)S(1)}, f32[2,128]{1,0:T(2,128)S(1)}, u32[]{:S(2)}, u32[]{:S(2)}) collective-permute-start(f32[2,128]{1,0:T(2,128)S(1)} %add.17), channel_id=1, source_target_pairs={{0,9},{1,8},{2,11},{3,10},{4,13},{5,12},{6,15},{7,14},{8,1},{9,0},... | collective-permute-start | bytes 3080 | tf_op jit(solution)/shard_map/ppermute | solution.py:504
  33.8 3.9 %collective-permute-start.10 = (f32[2,128]{1,0:T(2,128)S(1)}, f32[2,128]{1,0:T(2,128)S(1)}, u32[]{:S(2)}, u32[]{:S(2)}) collective-permute-start(f32[2,128]{1,0:T(2,128)S(1)} %add.18), channel_id=1, source_target_pairs={{0,17},{1,16},{2,19},{3,18},{4,21},{5,20},{6,23},{7,22},{8,25},{9,... | collective-permute-start | bytes 3080 | tf_op jit(solution)/shard_map/ppermute | solution.py:504

commit v2 on v1

--- a/solution.py
+++ b/solution.py
@@ -9,12 +9,12 @@
 HALO = 8
 LOW = 2 * HALO
 TINY = 1e-30
-ANY = pl.BlockSpec(memory_space=pl.ANY)
+HBM = pl.BlockSpec(memory_space=pltpu.HBM)
 VMEM = pl.BlockSpec(memory_space=pltpu.VMEM)
 
 
-def params():
-    return pltpu.CompilerParams(vmem_limit_bytes=48 << 20)
+def params(mebibytes):
+    return pltpu.CompilerParams(vmem_limit_bytes=mebibytes << 20)
 
 
 def shape(*dims):
@@ -51,21 +51,22 @@
     return below + above
 
 
-def pack_kernel(cond, resid, x_even, x_odd, y_even, y_odd, sem):
+def pack_kernel(cond, resid, x_even, y_even, y_odd, u, r, sem):
     layers, rows, _ = cond.shape
-    copies = []
-    for axis, outs in (("gx", (x_even, x_odd)), ("gy", (y_even, y_odd))):
-        odd = lax.rem(lax.axis_index(axis), 2)
-        for out, high in zip(outs, (1 - odd, odd)):
-            if axis == "gx":
-                two = pl.ds(high * (layers - 2), 2)
-                one = pl.ds(high * (layers - 1), 1)
-                copies.append((cond.at[two], out.at[pl.ds(0, 2)]))
-                copies.append((resid.at[one], out.at[pl.ds(2, 1)]))
-            else:
-                tile = pl.ds(pl.multiple_of(high * (rows - HALO), HALO), HALO)
-                copies.append((cond.at[:, tile], out.at[:, pl.ds(0, HALO)]))
-                copies.append((resid.at[:, tile], out.at[:, pl.ds(HALO, HALO)]))
+    own = pl.ds(LOW, rows)
+    high = 1 - lax.rem(lax.axis_index("gx"), 2)
+    two = pl.ds(high * (layers - 2), 2)
+    one = pl.ds(high * (layers - 1), 1)
+    copies = [
+        (cond.at[two], x_even.at[pl.ds(0, 2)]),
+        (resid.at[one], x_even.at[pl.ds(2, 1)]),
+    ]
+    odd = lax.rem(lax.axis_index("gy"), 2)
+    for out, high in ((y_even, 1 - odd), (y_odd, odd)):
+        tile = pl.ds(pl.multiple_of(high * (rows - HALO), HALO), HALO)
+        copies.append((cond.at[:, tile], out.at[:, pl.ds(0, HALO)]))
+        copies.append((resid.at[:, tile], out.at[:, pl.ds(HALO, HALO)]))
+    copies += [(cond, u.at[:, own]), (resid, r.at[:, own])]
     started = [
         pltpu.make_async_copy(source, target, sem.at[i])
         for i, (source, target) in enumerate(copies)
@@ -78,16 +79,20 @@
 
 def pack(cond, resid):
     layers, rows, lanes = cond.shape
-    x_out, y_out = shape(3, rows, lanes), shape(layers, 2 * HALO, lanes)
+    y_out = shape(layers, 2 * HALO, lanes)
+    grown = shape(layers, rows + 4 * HALO, lanes)
     return pl.pallas_call(
         pack_kernel,
-        out_shape=(x_out, x_out, y_out, y_out),
-        in_specs=[ANY, ANY],
-        out_specs=(ANY, ANY, ANY, ANY),
+        out_shape=(shape(3, rows, lanes), y_out, y_out, grown, grown),
+        in_specs=[HBM, HBM],
+        out_specs=(VMEM,) * 5,
         scratch_shapes=[pltpu.SemaphoreType.DMA((8,))],
-        compiler_params=params(),
+        compiler_params=params(1),
         name="pack",
-    )(cond, resid)
+    )(
+        pltpu.with_memory_space_constraint(cond, pltpu.HBM),
+        pltpu.with_memory_space_constraint(resid, pltpu.HBM),
+    )
 
 
 def y_tiles(y_even, y_odd, layer, part):
@@ -99,26 +104,24 @@
     return south, north
 
 
-def edge_kernel(u_low, u_high, r_low, r_high, y_even, y_odd, t_even, t_odd, grown):
-    layers, rows = y_even.shape[0], u_low.shape[1]
+def edge_kernel(u, r, y_even, y_odd, t_even, x_odd, grown):
+    layers, rows = u.shape[0], u.shape[1] - 4 * HALO
     odd = place("gx")[0]
     end = HALO + rows
+    own = slice(LOW, LOW + rows)
     sends = []
     for side in range(2):
-        u_side, r_side = ((u_low, r_low), (u_high, r_high))[side]
-        locals_ = ((0, 1, 2), (3, 2, 1))[side]
-        layer_of = ((0, 1, 2), (layers - 1, layers - 2, layers - 3))[side]
-        south, north = y_tiles(y_even, y_odd, layer_of[1], 0)
+        edge, mid, far = ((0, 1, 2), (layers - 1, layers - 2, layers - 3))[side]
+        south, north = y_tiles(y_even, y_odd, mid, 0)
+        middle = u[mid, own]
         grown[side, 0:HALO] = south
-        grown[side, HALO:end] = u_side[locals_[1]]
+        grown[side, HALO:end] = middle
         grown[side, end : end + HALO] = north
-        middle = u_side[locals_[1]]
-        edge = u_side[locals_[0]]
-        total = 6.0 * middle + edge + u_side[locals_[2]] + z_sum(middle)
+        total = 6.0 * middle + u[edge, own] + u[far, own] + z_sum(middle)
         total = total + grown[side, HALO - 1 : end - 1] + grown[side, HALO + 1 : end + 1]
-        term = (edge + middle) * (2.0 * r_side[0] / total)
-        edge_south, edge_north = y_tiles(y_even, y_odd, layer_of[0], 0)
-        r_south, r_north = y_tiles(y_even, y_odd, layer_of[0], 1)
+        term = (u[edge, own] + middle) * (2.0 * r[mid, own] / total)
+        edge_south, edge_north = y_tiles(y_even, y_odd, edge, 0)
+        r_south, r_north = y_tiles(y_even, y_odd, edge, 1)
         corner = jnp.concatenate(
             [
                 edge_south[HALO - 1 : HALO],
@@ -136,32 +139,24 @@
     (t_low, c_low), (t_high, c_high) = sends
     t_even[0:rows] = jnp.where(odd, t_low, t_high)
     t_even[rows : rows + 8] = jnp.where(odd, c_low, c_high)
-    t_odd[0:rows] = jnp.where(odd, t_high, t_low)
-    t_odd[rows : rows + 8] = jnp.where(odd, c_high, c_low)
-
-
-def edge_terms(cond, resid, y_even, y_odd):
-    layers, rows, lanes = cond.shape
-    four, one = (4, rows, lanes), (1, rows, lanes)
-    whole = pl.BlockSpec(y_even.shape, lambda i: (0, 0, 0))
-    out = pl.BlockSpec((rows + 8, lanes), lambda i: (0, 0))
+    x_odd[0:rows] = jnp.where(odd, u[layers - 2, own], u[0, own])
+    x_odd[rows : 2 * rows] = jnp.where(odd, u[layers - 1, own], u[1, own])
+    x_odd[2 * rows : 3 * rows] = jnp.where(odd, r[layers - 1, own], r[0, own])
+    x_odd[3 * rows : 4 * rows] = jnp.where(odd, t_high, t_low)
+    x_odd[4 * rows : 4 * rows + 8] = jnp.where(odd, c_high, c_low)
+
+
+def edge_terms(u, r, y_even, y_odd):
+    rows, lanes = u.shape[1] - 4 * HALO, u.shape[2]
     return pl.pallas_call(
         edge_kernel,
-        grid=(1,),
-        out_shape=(shape(rows + 8, lanes), shape(rows + 8, lanes)),
-        in_specs=[
-            pl.BlockSpec(four, lambda i: (0, 0, 0)),
-            pl.BlockSpec(four, lambda i: (layers // 4 - 1, 0, 0)),
-            pl.BlockSpec(one, lambda i: (1, 0, 0)),
-            pl.BlockSpec(one, lambda i: (layers - 2, 0, 0)),
-            whole,
-            whole,
-        ],
-        out_specs=(out, out),
+        out_shape=(shape(rows + 8, lanes), shape(4 * rows + 8, lanes)),
+        in_specs=[VMEM] * 4,
+        out_specs=(VMEM, VMEM),
         scratch_shapes=[pltpu.VMEM((2, rows + 2 * HALO, lanes), F32)],
-        compiler_params=params(),
+        compiler_params=params(2),
         name="edge_terms",
-    )(cond, cond, resid, resid, y_even, y_odd)
+    )(u, r, y_even, y_odd)
 
 
 def row_chunks(rows):
@@ -196,18 +191,11 @@
 
 
 def inner_kernel(
-    cond, resid, y_even, y_odd,
-    p_out, i_out, e_u, e_r, e_v, e_i, e_d, e_p, sums,
-    u, r, inv, v, w, d, p, q, masks, sem,
+    u_in, r_in, y_even, y_odd,
+    u, r, p_out, i_out, e_v, e_i, e_d, e_p, sums,
+    inv, v, w, d, p, q, masks,
 ):
-    layers, rows = cond.shape[0], cond.shape[1]
-    own = pl.ds(LOW, rows)
-    loads = [
-        pltpu.make_async_copy(cond, u.at[:, own], sem.at[0]),
-        pltpu.make_async_copy(resid, r.at[:, own], sem.at[1]),
-    ]
-    for copy in loads:
-        copy.start()
+    layers, rows = p_out.shape[0], p_out.shape[1]
     fill_rows(masks, rows)
 
     def halo(k, carry):
@@ -218,8 +206,6 @@
         return carry
 
     lax.fori_loop(0, layers, halo, 0)
-    for copy in loads:
-        copy.wait()
     chunks = row_chunks(rows)
 
     def first(k, carry):
@@ -285,10 +271,6 @@
     full = slice(HALO, LOW + rows + HALO)
     for side in range(2):
         order = (0, 1, 2, 3) if side == 0 else tuple(layers - 1 - k for k in range(4))
-        for k in range(4):
-            e_u[side, k, full] = u[order[k], full]
-        for k in range(3):
-            e_r[side, k, full] = r[order[k], full]
         for k in range(2):
             e_v[side, k, full] = v[order[k + 1], full]
             e_d[side, k, full] = d[order[k + 1], full]
@@ -296,32 +278,31 @@
         e_i[side, 0, full] = inv[order[1], full]
 
 
-def inner(cond, resid, y_even, y_odd):
-    layers, rows, lanes = cond.shape
-    grown = rows + 4 * HALO
+def inner(u, r, y_even, y_odd):
+    layers, grown, lanes = u.shape
+    rows = grown - 4 * HALO
     field = pltpu.VMEM((layers, grown, lanes), F32)
 
     def edge(count):
         return shape(2, count, grown, lanes)
 
-    outs = (
-        shape(layers, rows, lanes), shape(layers, rows, lanes),
-        edge(4), edge(3), edge(2), edge(1), edge(2), edge(2), shape(2, 8, lanes),
-    )
+    own, ext = shape(layers, rows, lanes), shape(layers, grown, lanes)
+    outs = (ext, ext, own, own, edge(2), edge(1), edge(2), edge(2), shape(2, 8, lanes))
     return pl.pallas_call(
         inner_kernel,
         out_shape=outs,
-        in_specs=[ANY, ANY, VMEM, VMEM],
+        in_specs=[VMEM] * 4,
         out_specs=(VMEM,) * len(outs),
-        scratch_shapes=[field] * 8
-        + [pltpu.VMEM((4, grown, lanes), F32), pltpu.SemaphoreType.DMA((2,))],
-        compiler_params=params(),
+        scratch_shapes=[field] * 6 + [pltpu.VMEM((4, grown, lanes), F32)],
+        input_output_aliases={0: 0, 1: 1},
+        compiler_params=params(12),
+        cost_estimate=pl.CostEstimate(flops=4_000_000_000, transcendentals=0, bytes_accessed=1),
         name="inner",
-    )(cond, resid, y_even, y_odd)
+    )(u, r, y_even, y_odd)
 
 
 def outer_kernel(
-    p_in, i_in, e_u, e_r, e_v, e_i, e_d, e_p, sums, x_even, x_odd, t_even, t_odd,
+    b_u, b_r, p_in, i_in, e_v, e_i, e_d, e_p, sums, x_even, t_even, x_odd,
     p_out, i_out, total_out,
     u, r, v, w, p, q, d, t, masks,
 ):
@@ -333,6 +314,7 @@
     rz, pq = sums[0], sums[1]
     chunks = row_chunks(rows)
     for side in range(2):
+        at = tuple(k if side == 0 else layers - 1 - k for k in range(4))
         has = (has_low, has_high)[side]
         pick = jnp.logical_xor(odd, side == 1)
         twice = 1.0 + has
@@ -342,10 +324,10 @@
 
         near, far = (1, 0) if side == 0 else (0, 1)
         for slot, source in ((0, far), (1, near)):
-            u[slot, own] = arrived(x_even[source], x_odd[source])
-        r[own] = arrived(x_even[2], x_odd[2])
-        t[own] = arrived(t_even[0:rows], t_odd[0:rows])
-        corner = arrived(t_even[rows : rows + 8], t_odd[rows : rows + 8])
+            u[slot, own] = arrived(x_even[source], x_odd[source * rows : (source + 1) * rows])
+        r[own] = arrived(x_even[2], x_odd[2 * rows : 3 * rows])
+        t[own] = arrived(t_even[0:rows], x_odd[3 * rows : 4 * rows])
+        corner = arrived(t_even[rows : rows + 8], x_odd[4 * rows : 4 * rows + 8])
         low, high = slice(HALO, LOW), slice(LOW + rows, LOW + rows + HALO)
         row = lax.broadcasted_iota(jnp.int32, zero.shape, 0)
 
@@ -365,17 +347,17 @@
             here = slice(start, start + size)
             down, up = slice(start - 1, start + size - 1), slice(start + 1, start + size + 1)
             inside = masks[0, here]
-            mid, edge = u[1, here], e_u[side, 0, here]
+            mid, edge = u[1, here], b_u[at[0], here]
             total = 6.0 * mid + u[0, here] + edge + u[1, down] + u[1, up] + z_sum(mid)
             inverse = has * inside / jnp.maximum(total, TINY)
             value = 2.0 * r[here] * inverse
             d[1, here] = inverse
             v[0, here] = value
             w[0, here] = mid * value
-            total = 6.0 * edge + mid + e_u[side, 1, here]
-            total = total + e_u[side, 0, down] + e_u[side, 0, up] + z_sum(edge)
+            total = 6.0 * edge + mid + b_u[at[1], here]
+            total = total + b_u[at[0], down] + b_u[at[0], up] + z_sum(edge)
             inverse = inside / jnp.maximum(total, TINY)
-            value = 2.0 * e_r[side, 0, here] * inverse
+            value = 2.0 * b_r[at[0], here] * inverse
             d[0, here] = total
             d[2, here] = inverse
             v[1, here] = value
@@ -403,9 +385,9 @@
             north = mid * v[0, up] + w[0, up]
             finish(mid, total, south, north, d[1, here], 0, twice)
 
-            mid, next_u = e_u[side, 0, here], e_u[side, 1, here]
+            mid, next_u = b_u[at[0], here], b_u[at[1], here]
             next_v = e_v[side, 0, here]
-            total = 2.0 * e_r[side, 0, here]
+            total = 2.0 * b_r[at[0], here]
             total = total + mid * (v[0, here] + next_v + z_sum(v[1, here]))
             total = total + w[0, here] + next_u * next_v + z_sum(w[1, here])
             south = mid * v[1, down] + w[1, down]
@@ -413,12 +395,12 @@
             finish(mid, total, south, north, d[2, here], 1, twice)
 
             inner_v = e_v[side, 1, here]
-            total = 2.0 * e_r[side, 1, here]
+            total = 2.0 * b_r[at[1], here]
             total = total + next_u * (v[1, here] + z_sum(next_v))
             total = total + w[1, here] + z_sum(next_u * next_v)
-            total = total + (next_u * inner_v + e_u[side, 2, here] * inner_v) / twice
-            south = (next_u + e_u[side, 1, down]) * e_v[side, 0, down]
-            north = (next_u + e_u[side, 1, up]) * e_v[side, 0, up]
+            total = total + (next_u * inner_v + b_u[at[2], here] * inner_v) / twice
+            south = (next_u + b_u[at[1], down]) * e_v[side, 0, down]
+            north = (next_u + b_u[at[1], up]) * e_v[side, 0, up]
             finish(next_u, total, south, north, e_i[side, 0, here], 2, twice)
 
         for start, size in own_chunks(rows):
@@ -426,8 +408,7 @@
             down, up = slice(start - 1, start + size - 1), slice(start + 1, start + size + 1)
             out_rows = slice(start - LOW, start - LOW + size)
             for k in range(3):
-                layer = k if side == 0 else layers - 1 - k
-                mid_u = e_u[side, k, here]
+                mid_u = b_u[at[k], here]
                 if k < 2:
                     mid = p[k + 1, here]
                     near_y = p[k + 1, down] + p[k + 1, up]
@@ -438,32 +419,32 @@
                         after_p, after_q = p[2, here], q[2, here]
                     else:
                         after_p = e_p[side, 0, here]
-                        after_q = e_u[side, 2, here] * after_p
+                        after_q = b_u[at[2], here] * after_p
                 else:
                     mid = e_p[side, 0, here]
                     mid_q = mid_u * mid
                     low_p, high_p = e_p[side, 0, down], e_p[side, 0, up]
                     near_y = low_p + high_p
-                    near_q = e_u[side, 2, down] * low_p + e_u[side, 2, up] * high_p
+                    near_q = b_u[at[2], down] * low_p + b_u[at[2], up] * high_p
                     before_p, before_q = p[2, here], q[2, here]
                     after_p = e_p[side, 1, here]
                     after_q = None
                 around = before_p + after_p + near_y + z_sum(mid)
                 if after_q is None:
-                    after_q = e_u[side, 3, here] * after_p
+                    after_q = b_u[at[3], here] * after_p
                 scaled = before_q + after_q + near_q + z_sum(mid_q)
                 total = d[0, here] if k == 0 else e_d[side, k - 1, here]
                 image = total * mid - mid_u * around - scaled
-                p_out[layer, out_rows] = mid
-                i_out[layer, out_rows] = image
-                rz = rz + eight(e_r[side, k, here] * mid)
+                p_out[at[k], out_rows] = mid
+                i_out[at[k], out_rows] = image
+                rz = rz + eight(b_r[at[k], here] * mid)
                 pq = pq + eight(mid * image)
     total_out[0:1] = jnp.broadcast_to(jnp.sum(rz, keepdims=True), (1, zero.shape[1]))
     total_out[1:2] = jnp.broadcast_to(jnp.sum(pq, keepdims=True), (1, zero.shape[1]))
 
 
-def outer(found, x_even, x_odd, t_even, t_odd):
-    p_in = found[0]
+def outer(found, x_even, t_even, x_odd):
+    p_in = found[2]
     layers, rows, lanes = p_in.shape
     grown = rows + 4 * HALO
 
@@ -473,15 +454,15 @@
     return pl.pallas_call(
         outer_kernel,
         out_shape=(shape(layers, rows, lanes), shape(layers, rows, lanes), shape(2, lanes)),
-        in_specs=[VMEM] * 13,
+        in_specs=[VMEM] * 12,
         out_specs=(VMEM, VMEM, VMEM),
         scratch_shapes=[
             field(2), field(), field(2), field(2), field(3), field(3), field(3), field(), field(4),
         ],
-        input_output_aliases={0: 0, 1: 1},
-        compiler_params=params(),
+        input_output_aliases={2: 0, 3: 1},
+        compiler_params=params(4),
         name="outer",
-    )(*found, x_even, x_odd, t_even, t_odd)
+    )(*found, x_even, t_even, x_odd)
 
 
 def power_of_two(count):
@@ -505,20 +486,55 @@
     return value
 
 
+def update_kernel(sums, precond, image, resid, pressure, residual, held, sem):
+    half_alpha = sums[0:1] / sums[1:2]
+    alpha = 2.0 * half_alpha
+    layers, rows, _ = precond.shape
+    own = slice(LOW, LOW + rows)
+    step = 4 if layers % 4 == 0 else layers
+    started = []
+    for start in range(0, layers, step):
+        for k in range(start, start + step):
+            held[0, k] = alpha * precond[k]
+            held[1, k] = resid[k, own] - half_alpha * image[k]
+        part = pl.ds(start, step)
+        for i, out in enumerate((pressure, residual)):
+            copy = pltpu.make_async_copy(
+                held.at[i, part], out.at[part], sem.at[i, start // step]
+            )
+            copy.start()
+            started.append(copy)
+    for copy in started:
+        copy.wait()
+
+
+def update(sums, precond, image, resid):
+    out = shape(*precond.shape)
+    return pl.pallas_call(
+        update_kernel,
+        out_shape=(out, out),
+        in_specs=[VMEM] * 4,
+        out_specs=(HBM, HBM),
+        scratch_shapes=[
+            pltpu.VMEM((2, *precond.shape), F32),
+            pltpu.SemaphoreType.DMA((2, precond.shape[0])),
+        ],
+        compiler_params=params(4),
+        name="update",
+    )(sums, precond, image, resid)
+
+
 def on_device(right_side, conductivity):
-    x_even, x_odd, y_even, y_odd = pack(conductivity, right_side)
+    x_even, y_even, y_odd, u, r = pack(conductivity, right_side)
     x_even = swap_even(x_even, "gx")
     y_even = swap_even(y_even, "gy")
     y_odd = swap_odd(y_odd, "gy")
+    t_even, x_odd = edge_terms(u, r, y_even, y_odd)
     x_odd = swap_odd(x_odd, "gx")
-    t_even, t_odd = edge_terms(conductivity, right_side, y_even, y_odd)
     t_even = swap_even(t_even, "gx")
-    t_odd = swap_odd(t_odd, "gx")
-    found = inner(conductivity, right_side, y_even, y_odd)
-    precond, image, sums = outer(found, x_even, x_odd, t_even, t_odd)
-    sums = sum_everywhere(sums)
-    half_alpha = sums[0, 0] / sums[1, 0]
-    return (2.0 * half_alpha) * precond, right_side - half_alpha * image
+    found = inner(u, r, y_even, y_odd)
+    precond, image, sums = outer(found, x_even, t_even, x_odd)
+    return update(sum_everywhere(sums), precond, image, found[1])
 
 
 def solution(mesh):

time: 41.3 us -> 39.8 us (0.964)
  waiting for transfers between devices: 11.3 us -> 16.8 us
  local copies, waits for them, and re-layouts: 2.97 us -> 0 us
  starting transfers between devices: 14.7 us -> 11.8 us
  Pallas kernels: 8.46 us -> 10.3 us
  other arithmetic: 1.54 us -> 0.02 us
  between operations: 2.07 us -> 0.7 us
    ppermute x3 -> x2, waiting for transfers between devices: 0.01 us -> 4.84 us  [swap_odd(): return lax.ppermute(value, axis, ordered(lambda i: (i + 1 ^ 1) - 1, count))]
    ppermute x3 -> x2, starting transfers between devices: 9.7 us -> 6.16 us  [swap_odd(): return lax.ppermute(value, axis, ordered(lambda i: (i + 1 ^ 1) - 1, count))]
    unnamed x6 -> x0, local copies, waits for them, and re-layouts: 2.45 us -> none
    pallas_call x3 -> x4, Pallas kernels: 7.06 us -> 8.95 us  [the longest x1 5.26 us: inner(): pl.pallas_call(inner_kernel, out_shape=outs, in_specs=[VMEM] * 4, out_spe...]
    sub x1 -> x0, other arithmetic: 1.53 us -> none  [on_device(): return (2.0 * half_alpha * precond, right_side - half_alpha * image)]
    ppermute x3, starting transfers between devices: 2.23 us -> 3.53 us  [swap_even(): return lax.ppermute(value, axis, ordered(lambda i: i ^ 1, count))]
    ppermute x5, starting transfers between devices: 2.76 us -> 2.11 us  [sum_everywhere(): value = value + lax.ppermute(value, ('gx', 'gy'), pairs)]
    ppermute x5, waiting for transfers between devices: 11.3 us -> 12 us  [sum_everywhere(): value = value + lax.ppermute(value, ('gx', 'gy'), pairs)]
  transfers between devices with their start and end apart: 11 -> 10, of which waited for: 5 -> 7; matrix products, arithmetic and copies ran while one was open for 0% -> 0% of each run, Pallas kernels for 16% -> 14%
where the time goes in v2:
time: 39.8 us; the launch traced here: 39.6 us
  waiting for transfers between devices  16.8 us (42%)
  starting transfers between devices  11.8 us (30%)
  Pallas kernels  10.3 us (26%)
  between operations  0.7 us (2%)
    ppermute x5, waiting for transfers between devices, sum_everywhere(): value = value + lax.ppermute(value, ('gx', 'gy'), pairs)  12 us
    ppermute x2, starting transfers between devices, swap_odd(): return lax.ppermute(value, axis, ordered(lambda i: (i + 1 ^ 1) - 1, count))  6.16 us
    pallas_call x1, Pallas kernels, inner(): pl.pallas_call(inner_kernel, out_shape=outs, in_specs=[VMEM] * 4, out_spe...  5.26 us
    ppermute x2, waiting for transfers between devices, swap_odd(): return lax.ppermute(value, axis, ordered(lambda i: (i + 1 ^ 1) - 1, count))  4.84 us
    ppermute x3, starting transfers between devices, swap_even(): return lax.ppermute(value, axis, ordered(lambda i: i ^ 1, count))  3.53 us
    ppermute x5, starting transfers between devices, sum_everywhere(): value = value + lax.ppermute(value, ('gx', 'gy'), pairs)  2.11 us
    pallas_call x1, Pallas kernels, pack(): pl.pallas_call(pack_kernel, out_shape=(shape(3, rows, lanes), y_out, y_ou...  1.88 us
    pallas_call x1, Pallas kernels, update(): pl.pallas_call(update_kernel, out_shape=(out, out), in_specs=[VMEM] * 4,...  1.65 us
  transfers between devices with their start and end apart: 10, of which 7 were waited for; matrix products, arithmetic and copies ran while one was open for 0% of the time, Pallas kernels for 14%

profile of v2, /device:TPU:0, one launch (start us, length us, event | category | flops | bytes accessed | tf_op | source)
XLA Modules:
  0.0 39.6 jit_solution(12328369783416714692)
XLA Ops:
  0.6 1.9 %pack.1 = (f32[3,128,128]{2,1,0:T(8,128)S(1)}, f32[16,16,128]{2,1,0:T(8,128)S(1)}, f32[16,16,128]{2,1,0:T(8,128)S(1)}, f32[16,160,128]{2,1,0:T(8,128)S(1)}, f32[16,160,128]{2,1,0:T(8,128)S(1)}) custom-call(f32[16,128,128]{2,1,0:T(8,128)} %cond.1, f32[16,128,128]{2,1,0:T(8,128)} %resid.1), custom_call_target="tpu_custom_call" | custom-call | tf_op jit(solution)/shard_map/pack/pallas_call | solution.py:84
  2.5 0.5 %collective-permute-start = (f32[16,16,128]{2,1,0:T(8,128)S(1)}, f32[16,16,128]{2,1,0:T(8,128)S(1)}, u32[]{:S(2)}, u32[]{:S(2)}) collective-permute-start(f32[16,16,128]{2,1,0:T(8,128)S(1)} %get-tuple-element.23), channel_id=1, source_target_pairs={{0,1},{1,0},{2,3},{3,2},{4,5},{5,4},{6,7},{7,6},{8,9},{9,8},{10,11... | collective-permute-start | bytes 393224 | tf_op jit(solution)/shard_map/ppermute | solution.py:30
  3.0 2.6 %collective-permute-start.1 = (f32[16,16,128]{2,1,0:T(8,128)S(1)}, f32[16,16,128]{2,1,0:T(8,128)S(1)}, u32[]{:S(2)}, u32[]{:S(2)}) collective-permute-start(f32[16,16,128]{2,1,0:T(8,128)S(1)} %get-tuple-element.24), channel_id=1, source_target_pairs={{0,3},{1,2},{2,1},{3,0},{4,7},{5,6},{6,5},{7,4},{8,11},{9,10},{10,... | collective-permute-start | bytes 393224 | tf_op jit(solution)/shard_map/ppermute | solution.py:35
  5.6 1.5 %collective-permute-start.2 = (f32[3,128,128]{2,1,0:T(8,128)S(1)}, f32[3,128,128]{2,1,0:T(8,128)S(1)}, u32[]{:S(2)}, u32[]{:S(2)}) collective-permute-start(f32[3,128,128]{2,1,0:T(8,128)S(1)} %get-tuple-element.34), channel_id=1, source_target_pairs={{0,4},{4,0},{8,12},{12,8},{16,20},{20,16},{24,28},{28,24},{1,5},{5... | collective-permute-start | bytes 589832 | tf_op jit(solution)/shard_map/ppermute | solution.py:30
  7.2 0.0 collective-permute-done.y_even
  7.2 2.3 %collective-permute-done.1.y_odd = f32[16,16,128]{2,1,0:T(8,128)S(1)} collective-permute-done((f32[16,16,128]{2,1,0:T(8,128)S(1)}, f32[16,16,128]{2,1,0:T(8,128)S(1)}, u32[]{:S(2)}, u32[]{:S(2)}) %collective-permute-start.1) | collective-permute-done | bytes 131104 | tf_op jit(solution)/shard_map/ppermute | solution.py:35
  9.4 0.2 edge_terms.1
  9.6 1.5 %collective-permute-start.3 = (f32[136,128]{1,0:T(8,128)S(1)}, f32[136,128]{1,0:T(8,128)S(1)}, u32[]{:S(2)}, u32[]{:S(2)}) collective-permute-start(f32[136,128]{1,0:T(8,128)S(1)} %get-tuple-element.35), channel_id=1, source_target_pairs={{0,4},{4,0},{8,12},{12,8},{16,20},{20,16},{24,28},{28,24},{1,5},{5... | collective-permute-start | bytes 208904 | tf_op jit(solution)/shard_map/ppermute | solution.py:30
  11.1 3.5 %collective-permute-start.4 = (f32[520,128]{1,0:T(8,128)S(1)}, f32[520,128]{1,0:T(8,128)S(1)}, u32[]{:S(2)}, u32[]{:S(2)}) collective-permute-start(f32[520,128]{1,0:T(8,128)S(1)} %get-tuple-element.36), channel_id=1, source_target_pairs={{0,28},{4,8},{8,4},{12,16},{16,12},{20,24},{24,20},{28,0},{1,29},{... | collective-permute-start | bytes 798728 | tf_op jit(solution)/shard_map/ppermute | solution.py:35
  14.6 5.3 %inner.1 = (f32[16,160,128]{2,1,0:T(8,128)S(1)}, f32[16,160,128]{2,1,0:T(8,128)S(1)}, f32[16,128,128]{2,1,0:T(8,128)S(1)}, f32[16,128,128]{2,1,0:T(8,128)S(1)}, ...) custom-call(f32[16,160,128]{2,1,0:T(8,128)S(1)} %get-tuple-element.2, ...), custom_call_target="tpu_custom_call", output_to_operand_aliasing={{0}: (0, {}), {1}: (1, {})} | custom-call | flops 4000000000 | bytes 1 | tf_op jit(solution)/shard_map/inner/pallas_call | solution.py:291
  19.9 0.0 collective-permute-done.2.x_even
  19.9 0.0 collective-permute-done.3.t_even
  19.9 2.6 %collective-permute-done.4.x_odd = f32[520,128]{1,0:T(8,128)S(1)} collective-permute-done((f32[520,128]{1,0:T(8,128)S(1)}, f32[520,128]{1,0:T(8,128)S(1)}, u32[]{:S(2)}, u32[]{:S(2)}) %collective-permute-start.4) | collective-permute-done | bytes 266272 | tf_op jit(solution)/shard_map/ppermute | solution.py:35
  22.5 1.4 %outer.1 = (f32[16,128,128]{2,1,0:T(8,128)S(1)}, f32[16,128,128]{2,1,0:T(8,128)S(1)}, f32[2,128]{1,0:T(2,128)S(1)}) custom-call(f32[16,160,128]{2,1,0:T(8,128)S(1)} %get-tuple-element.25.b_u, f32[16,160,128]{2,1,0:T(8,128)S(1)} %get-tuple-element.26.b_r.resid, ...), custom_call_target="tpu_custom_call", output_to_operand_aliasing={{0}: (2, {}), {1}: (3, {})} | custom-call | tf_op jit(solution)/shard_map/outer/pallas_call | solution.py:454
  23.9 0.1 collective-permute-start.5
  24.0 1.1 %collective-permute-done.5 = f32[2,128]{1,0:T(2,128)S(1)} collective-permute-done((f32[2,128]{1,0:T(2,128)S(1)}, f32[2,128]{1,0:T(2,128)S(1)}, u32[]{:S(2)}, u32[]{:S(2)}) %collective-permute-start.5) | collective-permute-done | bytes 1056 | tf_op jit(solution)/shard_map/ppermute | solution.py:485
  25.1 1.3 %collective-permute-start.6 = (f32[2,128]{1,0:T(2,128)S(1)}, f32[2,128]{1,0:T(2,128)S(1)}, u32[]{:S(2)}, u32[]{:S(2)}) collective-permute-start(f32[2,128]{1,0:T(2,128)S(1)} %add.15), channel_id=1, source_target_pairs={{0,3},{1,2},{2,1},{3,0},{4,7},{5,6},{6,5},{7,4},{8,11},{9,10},{10,... | collective-permute-start | bytes 3080 | tf_op jit(solution)/shard_map/ppermute | solution.py:485
  26.4 1.7 %collective-permute-done.6 = f32[2,128]{1,0:T(2,128)S(1)} collective-permute-done((f32[2,128]{1,0:T(2,128)S(1)}, f32[2,128]{1,0:T(2,128)S(1)}, u32[]{:S(2)}, u32[]{:S(2)}) %collective-permute-start.6) | collective-permute-done | bytes 1056 | tf_op jit(solution)/shard_map/ppermute | solution.py:485
  28.1 0.0 collective-permute-start.7
  28.1 3.0 %collective-permute-done.7 = f32[2,128]{1,0:T(2,128)S(1)} collective-permute-done((f32[2,128]{1,0:T(2,128)S(1)}, f32[2,128]{1,0:T(2,128)S(1)}, u32[]{:S(2)}, u32[]{:S(2)}) %collective-permute-start.7) | collective-permute-done | bytes 1056 | tf_op jit(solution)/shard_map/ppermute | solution.py:485
  31.1 0.0 collective-permute-start.8
  31.1 3.0 %collective-permute-done.8 = f32[2,128]{1,0:T(2,128)S(1)} collective-permute-done((f32[2,128]{1,0:T(2,128)S(1)}, f32[2,128]{1,0:T(2,128)S(1)}, u32[]{:S(2)}, u32[]{:S(2)}) %collective-permute-start.8) | collective-permute-done | bytes 1056 | tf_op jit(solution)/shard_map/ppermute | solution.py:485
  34.1 0.7 %collective-permute-start.9 = (f32[2,128]{1,0:T(2,128)S(1)}, f32[2,128]{1,0:T(2,128)S(1)}, u32[]{:S(2)}, u32[]{:S(2)}) collective-permute-start(f32[2,128]{1,0:T(2,128)S(1)} %add.18), channel_id=1, source_target_pairs={{0,17},{1,16},{2,19},{3,18},{4,21},{5,20},{6,23},{7,22},{8,25},{9,... | collective-permute-start | bytes 3080 | tf_op jit(solution)/shard_map/ppermute | solution.py:485
  34.8 3.1 %collective-permute-done.9 = f32[2,128]{1,0:T(2,128)S(1)} collective-permute-done((f32[2,128]{1,0:T(2,128)S(1)}, f32[2,128]{1,0:T(2,128)S(1)}, u32[]{:S(2)}, u32[]{:S(2)}) %collective-permute-start.9) | collective-permute-done | bytes 1056 | tf_op jit(solution)/shard_map/ppermute | solution.py:485
  38.0 1.6 %update.1 = (f32[16,128,128]{2,1,0:T(8,128)}, f32[16,128,128]{2,1,0:T(8,128)}) custom-call(f32[2,128]{1,0:T(2,128)S(1)} %add.19.sums, f32[16,128,128]{2,1,0:T(8,128)S(1)} %get-tuple-element.38.precond, f32[16,128,128]{2,1,0:T(8,128)S(1)} %get-tuple-element.39.image, f32[16,160,128]{2,1,0:T(8,128)S(1)} %get-tuple-element.26.b_r.resid), custom_call_target="tpu_custom_call" | custom-call | tf_op jit(solution)/shard_map/update/pallas_call | solution.py:513
  (5 shorter events, 0.0 us)
Async XLA Ops:
  2.5 4.7 %collective-permute-start = (f32[16,16,128]{2,1,0:T(8,128)S(1)}, f32[16,16,128]{2,1,0:T(8,128)S(1)}, u32[]{:S(2)}, u32[]{:S(2)}) collective-permute-start(f32[16,16,128]{2,1,0:T(8,128)S(1)} %get-tuple-element.23), channel_id=1, source_target_pairs={{0,1},{1,0},{2,3},{3,2},{4,5},{5,4},{6,7},{7,6},{8,9},{9,8},{10,11... | collective-permute-start | bytes 393224 | tf_op jit(solution)/shard_map/ppermute | solution.py:30
  3.0 6.4 %collective-permute-start.1 = (f32[16,16,128]{2,1,0:T(8,128)S(1)}, f32[16,16,128]{2,1,0:T(8,128)S(1)}, u32[]{:S(2)}, u32[]{:S(2)}) collective-permute-start(f32[16,16,128]{2,1,0:T(8,128)S(1)} %get-tuple-element.24), channel_id=1, source_target_pairs={{0,3},{1,2},{2,1},{3,0},{4,7},{5,6},{6,5},{7,4},{8,11},{9,10},{10,... | collective-permute-start | bytes 393224 | tf_op jit(solution)/shard_map/ppermute | solution.py:35
  5.6 14.3 %collective-permute-start.2 = (f32[3,128,128]{2,1,0:T(8,128)S(1)}, f32[3,128,128]{2,1,0:T(8,128)S(1)}, u32[]{:S(2)}, u32[]{:S(2)}) collective-permute-start(f32[3,128,128]{2,1,0:T(8,128)S(1)} %get-tuple-element.34), channel_id=1, source_target_pairs={{0,4},{4,0},{8,12},{12,8},{16,20},{20,16},{24,28},{28,24},{1,5},{5... | collective-permute-start | bytes 589832 | tf_op jit(solution)/shard_map/ppermute | solution.py:30
  9.6 10.3 %collective-permute-start.3 = (f32[136,128]{1,0:T(8,128)S(1)}, f32[136,128]{1,0:T(8,128)S(1)}, u32[]{:S(2)}, u32[]{:S(2)}) collective-permute-start(f32[136,128]{1,0:T(8,128)S(1)} %get-tuple-element.35), channel_id=1, source_target_pairs={{0,4},{4,0},{8,12},{12,8},{16,20},{20,16},{24,28},{28,24},{1,5},{5... | collective-permute-start | bytes 208904 | tf_op jit(solution)/shard_map/ppermute | solution.py:30
  11.1 11.4 %collective-permute-start.4 = (f32[520,128]{1,0:T(8,128)S(1)}, f32[520,128]{1,0:T(8,128)S(1)}, u32[]{:S(2)}, u32[]{:S(2)}) collective-permute-start(f32[520,128]{1,0:T(8,128)S(1)} %get-tuple-element.36), channel_id=1, source_target_pairs={{0,28},{4,8},{8,4},{12,16},{16,12},{20,24},{24,20},{28,0},{1,29},{... | collective-permute-start | bytes 798728 | tf_op jit(solution)/shard_map/ppermute | solution.py:35
  23.9 1.2 %collective-permute-start.5 = (f32[2,128]{1,0:T(2,128)S(1)}, f32[2,128]{1,0:T(2,128)S(1)}, u32[]{:S(2)}, u32[]{:S(2)}) collective-permute-start(f32[2,128]{1,0:T(2,128)S(1)} %get-tuple-element.37), channel_id=1, source_target_pairs={{0,1},{1,0},{2,3},{3,2},{4,5},{5,4},{6,7},{7,6},{8,9},{9,8},{10,11... | collective-permute-start | bytes 3080 | tf_op jit(solution)/shard_map/ppermute | solution.py:485
  25.1 3.0 %collective-permute-start.6 = (f32[2,128]{1,0:T(2,128)S(1)}, f32[2,128]{1,0:T(2,128)S(1)}, u32[]{:S(2)}, u32[]{:S(2)}) collective-permute-start(f32[2,128]{1,0:T(2,128)S(1)} %add.15), channel_id=1, source_target_pairs={{0,3},{1,2},{2,1},{3,0},{4,7},{5,6},{6,5},{7,4},{8,11},{9,10},{10,... | collective-permute-start | bytes 3080 | tf_op jit(solution)/shard_map/ppermute | solution.py:485
  28.1 3.0 %collective-permute-start.7 = (f32[2,128]{1,0:T(2,128)S(1)}, f32[2,128]{1,0:T(2,128)S(1)}, u32[]{:S(2)}, u32[]{:S(2)}) collective-permute-start(f32[2,128]{1,0:T(2,128)S(1)} %add.16), channel_id=1, source_target_pairs={{0,5},{1,4},{2,7},{3,6},{4,1},{5,0},{6,3},{7,2},{8,13},{9,12},{10,... | collective-permute-start | bytes 3080 | tf_op jit(solution)/shard_map/ppermute | solution.py:485
  31.1 3.0 %collective-permute-start.8 = (f32[2,128]{1,0:T(2,128)S(1)}, f32[2,128]{1,0:T(2,128)S(1)}, u32[]{:S(2)}, u32[]{:S(2)}) collective-permute-start(f32[2,128]{1,0:T(2,128)S(1)} %add.17), channel_id=1, source_target_pairs={{0,9},{1,8},{2,11},{3,10},{4,13},{5,12},{6,15},{7,14},{8,1},{9,0},... | collective-permute-start | bytes 3080 | tf_op jit(solution)/shard_map/ppermute | solution.py:485
  34.1 3.9 %collective-permute-start.9 = (f32[2,128]{1,0:T(2,128)S(1)}, f32[2,128]{1,0:T(2,128)S(1)}, u32[]{:S(2)}, u32[]{:S(2)}) collective-permute-start(f32[2,128]{1,0:T(2,128)S(1)} %add.18), channel_id=1, source_target_pairs={{0,17},{1,16},{2,19},{3,18},{4,21},{5,20},{6,23},{7,22},{8,25},{9,... | collective-permute-start | bytes 3080 | tf_op jit(solution)/shard_map/ppermute | solution.py:485

commit v3 on v2

--- a/solution.py
+++ b/solution.py
@@ -21,18 +21,29 @@
     return jax.ShapeDtypeStruct(dims, F32)
 
 
-def ordered(first_pair_partner, count):
-    return [(i, first_pair_partner(i) % count) for i in range(count)]
-
-
-def swap_even(value, axis):
-    count = lax.axis_size(axis)
-    return lax.ppermute(value, axis, ordered(lambda i: i ^ 1, count))
-
-
-def swap_odd(value, axis):
-    count = lax.axis_size(axis)
-    return lax.ppermute(value, axis, ordered(lambda i: ((i + 1) ^ 1) - 1, count))
+def swap(value, partner):
+    count_x, count_y = lax.axis_size("gx"), lax.axis_size("gy")
+    pairs = []
+    for x in range(count_x):
+        for y in range(count_y):
+            to_x, to_y = partner(x, y)
+            pairs.append((x * count_y + y, to_x * count_y + to_y))
+    return lax.ppermute(value, ("gx", "gy"), pairs)
+
+
+def swap_x(value, odd):
+    count = lax.axis_size("gx")
+
+    def partner(x, y):
+        to = ((x + odd) ^ 1) - odd
+        return (to, y) if 0 <= to < count else (x, y ^ 1)
+
+    return swap(value, partner)
+
+
+def swap_y(value, odd):
+    count = lax.axis_size("gy")
+    return swap(value, lambda x, y: (x, (((y + odd) ^ 1) - odd) % count))
 
 
 def place(axis):
@@ -51,43 +62,52 @@
     return below + above
 
 
-def pack_kernel(cond, resid, x_even, y_even, y_odd, u, r, sem):
-    layers, rows, _ = cond.shape
-    own = pl.ds(LOW, rows)
-    high = 1 - lax.rem(lax.axis_index("gx"), 2)
-    two = pl.ds(high * (layers - 2), 2)
-    one = pl.ds(high * (layers - 1), 1)
-    copies = [
-        (cond.at[two], x_even.at[pl.ds(0, 2)]),
-        (resid.at[one], x_even.at[pl.ds(2, 1)]),
-    ]
-    odd = lax.rem(lax.axis_index("gy"), 2)
-    for out, high in ((y_even, 1 - odd), (y_odd, odd)):
-        tile = pl.ds(pl.multiple_of(high * (rows - HALO), HALO), HALO)
-        copies.append((cond.at[:, tile], out.at[:, pl.ds(0, HALO)]))
-        copies.append((resid.at[:, tile], out.at[:, pl.ds(HALO, HALO)]))
-    copies += [(cond, u.at[:, own]), (resid, r.at[:, own])]
+def pack_kernel(cond, resid, x_even, x_odd, y_even, y_odd, tiles, sem):
+    layers, rows, lanes = cond.shape
+    odd = lax.rem(lax.axis_index("gx"), 2)
+    x_copies, y_copies = [], []
+    for out, high in ((x_even, 1 - odd), (x_odd, odd)):
+        two = pl.ds(high * (layers - 2), 2)
+        one = pl.ds(high * (layers - 1), 1)
+        x_copies.append((cond.at[two], out.at[pl.ds(0, 2)]))
+        x_copies.append((resid.at[one], out.at[pl.ds(2, 1)]))
+    for side, start in enumerate((0, rows - HALO)):
+        for part, source in enumerate((cond, resid)):
+            y_copies.append((source.at[:, pl.ds(start, HALO)], tiles.at[side, part]))
     started = [
         pltpu.make_async_copy(source, target, sem.at[i])
-        for i, (source, target) in enumerate(copies)
+        for i, (source, target) in enumerate(y_copies + x_copies)
     ]
     for copy in started:
         copy.start()
-    for copy in started:
+    for copy in started[:4]:
+        copy.wait()
+    odd = lax.rem(lax.axis_index("gy"), 2) == 1
+    first = lax.broadcasted_iota(jnp.int32, (HALO, lanes), 0) < 3
+    for k in range(layers):
+        low = jnp.where(first, tiles[0, 0, k], pltpu.roll(tiles[0, 1, k], 3, 0))
+        high = jnp.where(
+            first, pltpu.roll(tiles[1, 0, k], 3, 0), pltpu.roll(tiles[1, 1, k], 5, 0)
+        )
+        y_even[k] = jnp.where(odd, low, high)
+        y_odd[k] = jnp.where(odd, high, low)
+    for copy in started[4:]:
         copy.wait()
 
 
 def pack(cond, resid):
     layers, rows, lanes = cond.shape
-    y_out = shape(layers, 2 * HALO, lanes)
-    grown = shape(layers, rows + 4 * HALO, lanes)
+    x_out, y_out = shape(3, rows, lanes), shape(layers, HALO, lanes)
     return pl.pallas_call(
         pack_kernel,
-        out_shape=(shape(3, rows, lanes), y_out, y_out, grown, grown),
+        out_shape=(x_out, x_out, y_out, y_out),
         in_specs=[HBM, HBM],
-        out_specs=(VMEM,) * 5,
-        scratch_shapes=[pltpu.SemaphoreType.DMA((8,))],
-        compiler_params=params(1),
+        out_specs=(VMEM,) * 4,
+        scratch_shapes=[
+            pltpu.VMEM((2, 2, layers, HALO, lanes), F32),
+            pltpu.SemaphoreType.DMA((8,)),
+        ],
+        compiler_params=params(2),
         name="pack",
     )(
         pltpu.with_memory_space_constraint(cond, pltpu.HBM),
@@ -95,16 +115,54 @@
     )
 
 
+def load_kernel(cond, resid, after, u, r, sem):
+    own = pl.ds(LOW, cond.shape[1])
+    copies = [
+        pltpu.make_async_copy(source, target.at[:, own], sem.at[i])
+        for i, (source, target) in enumerate(((cond, u), (resid, r)))
+    ]
+    for copy in copies:
+        copy.start()
+    for copy in copies:
+        copy.wait()
+
+
+def load(cond, resid, after):
+    layers, rows, lanes = cond.shape
+    grown = shape(layers, rows + 4 * HALO, lanes)
+    return pl.pallas_call(
+        load_kernel,
+        out_shape=(grown, grown),
+        in_specs=[HBM, HBM, VMEM],
+        out_specs=(VMEM, VMEM),
+        scratch_shapes=[pltpu.SemaphoreType.DMA((2,))],
+        compiler_params=params(1),
+        cost_estimate=pl.CostEstimate(
+            flops=1_000_000_000, transcendentals=0, bytes_accessed=4 * cond.size
+        ),
+        name="load",
+    )(
+        pltpu.with_memory_space_constraint(cond, pltpu.HBM),
+        pltpu.with_memory_space_constraint(resid, pltpu.HBM),
+        after,
+    )
+
+
 def y_tiles(y_even, y_odd, layer, part):
     odd, has_low, has_high = place("gy")
-    rows = pl.ds(part * HALO, HALO)
-    first, second = y_even[layer, rows], y_odd[layer, rows]
-    south = jnp.where(odd, first, second) * has_low
-    north = jnp.where(odd, second, first) * has_high
+    first, second = y_even[layer], y_odd[layer]
+    row = lax.broadcasted_iota(jnp.int32, first.shape, 0)
+    width = 3 - part
+    south = pltpu.roll(jnp.where(odd, first, second), (5, 3)[part], 0)
+    north = jnp.where(odd, second, first)
+    if part:
+        north = pltpu.roll(north, 5, 0)
+    south = jnp.where(row >= HALO - width, south, 0.0) * has_low
+    north = jnp.where(row < width, north, 0.0) * has_high
     return south, north
 
 
-def edge_kernel(u, r, y_even, y_odd, t_even, x_odd, grown):
+def edge_kernel(u, r, y_even, y_odd, t_even, t_odd, grown):
     layers, rows = u.shape[0], u.shape[1] - 4 * HALO
     odd = place("gx")[0]
     end = HALO + rows
@@ -139,18 +197,15 @@
     (t_low, c_low), (t_high, c_high) = sends
     t_even[0:rows] = jnp.where(odd, t_low, t_high)
     t_even[rows : rows + 8] = jnp.where(odd, c_low, c_high)
-    x_odd[0:rows] = jnp.where(odd, u[layers - 2, own], u[0, own])
-    x_odd[rows : 2 * rows] = jnp.where(odd, u[layers - 1, own], u[1, own])
-    x_odd[2 * rows : 3 * rows] = jnp.where(odd, r[layers - 1, own], r[0, own])
-    x_odd[3 * rows : 4 * rows] = jnp.where(odd, t_high, t_low)
-    x_odd[4 * rows : 4 * rows + 8] = jnp.where(odd, c_high, c_low)
+    t_odd[0:rows] = jnp.where(odd, t_high, t_low)
+    t_odd[rows : rows + 8] = jnp.where(odd, c_high, c_low)
 
 
 def edge_terms(u, r, y_even, y_odd):
     rows, lanes = u.shape[1] - 4 * HALO, u.shape[2]
     return pl.pallas_call(
         edge_kernel,
-        out_shape=(shape(rows + 8, lanes), shape(4 * rows + 8, lanes)),
+        out_shape=(shape(rows + 8, lanes), shape(rows + 8, lanes)),
         in_specs=[VMEM] * 4,
         out_specs=(VMEM, VMEM),
         scratch_shapes=[pltpu.VMEM((2, rows + 2 * HALO, lanes), F32)],
@@ -302,7 +357,7 @@
 
 
 def outer_kernel(
-    b_u, b_r, p_in, i_in, e_v, e_i, e_d, e_p, sums, x_even, t_even, x_odd,
+    b_u, b_r, p_in, i_in, e_v, e_i, e_d, e_p, sums, x_even, x_odd, t_even, t_odd,
     p_out, i_out, total_out,
     u, r, v, w, p, q, d, t, masks,
 ):
@@ -324,10 +379,10 @@
 
         near, far = (1, 0) if side == 0 else (0, 1)
         for slot, source in ((0, far), (1, near)):
-            u[slot, own] = arrived(x_even[source], x_odd[source * rows : (source + 1) * rows])
-        r[own] = arrived(x_even[2], x_odd[2 * rows : 3 * rows])
-        t[own] = arrived(t_even[0:rows], x_odd[3 * rows : 4 * rows])
-        corner = arrived(t_even[rows : rows + 8], x_odd[4 * rows : 4 * rows + 8])
+            u[slot, own] = arrived(x_even[source], x_odd[source])
+        r[own] = arrived(x_even[2], x_odd[2])
+        t[own] = arrived(t_even[0:rows], t_odd[0:rows])
+        corner = arrived(t_even[rows : rows + 8], t_odd[rows : rows + 8])
         low, high = slice(HALO, LOW), slice(LOW + rows, LOW + rows + HALO)
         row = lax.broadcasted_iota(jnp.int32, zero.shape, 0)
 
@@ -443,7 +498,7 @@
     total_out[1:2] = jnp.broadcast_to(jnp.sum(pq, keepdims=True), (1, zero.shape[1]))
 
 
-def outer(found, x_even, t_even, x_odd):
+def outer(found, x_even, x_odd, t_even, t_odd):
     p_in = found[2]
     layers, rows, lanes = p_in.shape
     grown = rows + 4 * HALO
@@ -454,7 +509,7 @@
     return pl.pallas_call(
         outer_kernel,
         out_shape=(shape(layers, rows, lanes), shape(layers, rows, lanes), shape(2, lanes)),
-        in_specs=[VMEM] * 12,
+        in_specs=[VMEM] * 13,
         out_specs=(VMEM, VMEM, VMEM),
         scratch_shapes=[
             field(2), field(), field(2), field(2), field(3), field(3), field(3), field(), field(4),
@@ -462,7 +517,7 @@
         input_output_aliases={2: 0, 3: 1},
         compiler_params=params(4),
         name="outer",
-    )(*found, x_even, t_even, x_odd)
+    )(*found, x_even, x_odd, t_even, t_odd)
 
 
 def power_of_two(count):
@@ -477,12 +532,7 @@
     steps = [(0, 1 << bit | low) for bit in range(count_y.bit_length() - 1)]
     steps += [(1 << bit, low) for bit in range(count_x.bit_length() - 1)]
     for step_x, step_y in steps:
-        pairs = [
-            (x * count_y + y, (x ^ step_x) * count_y + (y ^ step_y))
-            for x in range(count_x)
-            for y in range(count_y)
-        ]
-        value = value + lax.ppermute(value, ("gx", "gy"), pairs)
+        value = value + swap(value, lambda x, y: (x ^ step_x, y ^ step_y))
     return value
 
 
@@ -525,15 +575,14 @@
 
 
 def on_device(right_side, conductivity):
-    x_even, y_even, y_odd, u, r = pack(conductivity, right_side)
-    x_even = swap_even(x_even, "gx")
-    y_even = swap_even(y_even, "gy")
-    y_odd = swap_odd(y_odd, "gy")
-    t_even, x_odd = edge_terms(u, r, y_even, y_odd)
-    x_odd = swap_odd(x_odd, "gx")
-    t_even = swap_even(t_even, "gx")
+    x_even, x_odd, y_even, y_odd = pack(conductivity, right_side)
+    u, r = load(conductivity, right_side, y_even)
+    y_even, y_odd = swap_y(y_even, 0), swap_y(y_odd, 1)
+    x_even, x_odd = swap_x(x_even, 0), swap_x(x_odd, 1)
+    t_even, t_odd = edge_terms(u, r, y_even, y_odd)
+    t_even, t_odd = swap_x(t_even, 0), swap_x(t_odd, 1)
     found = inner(u, r, y_even, y_odd)
-    precond, image, sums = outer(found, x_even, t_even, x_odd)
+    precond, image, sums = outer(found, x_even, x_odd, t_even, t_odd)
     return update(sum_everywhere(sums), precond, image, found[1])
 
 

time: 39.8 us -> 36.1 us (0.907)
  waiting for transfers between devices: 16.8 us -> 9.08 us
  starting transfers between devices: 11.8 us -> 14.9 us
  Pallas kernels: 10.3 us -> 11.2 us
    ppermute x10 -> x11, waiting for transfers between devices: 16.8 us -> 9.08 us  [swap(): return lax.ppermute(value, ('gx', 'gy'), pairs)]
    ppermute x10 -> x11, starting transfers between devices: 11.8 us -> 14.9 us  [swap(): return lax.ppermute(value, ('gx', 'gy'), pairs)]
    pallas_call x2 -> x3, Pallas kernels: 2.04 us -> 2.93 us  [the longest x1 1.56 us: load(): pl.pallas_call(load_kernel, out_shape=(grown, grown), in_specs=[HBM, HBM,...]
  transfers between devices with their start and end apart: 10 -> 11, of which waited for: 7 -> 6; matrix products, arithmetic and copies ran while one was open for 0% -> 0% of each run, Pallas kernels for 14% -> 19%
where the time goes in v3:
time: 36.1 us; the launch traced here: 35.9 us
  starting transfers between devices  14.9 us (41%)
  Pallas kernels  11.2 us (31%)
  waiting for transfers between devices  9.08 us (25%)
  between operations  0.71 us (2%)
    ppermute x11, starting transfers between devices, swap(): return lax.ppermute(value, ('gx', 'gy'), pairs)  14.9 us
    ppermute x11, waiting for transfers between devices, swap(): return lax.ppermute(value, ('gx', 'gy'), pairs)  9.08 us
    pallas_call x1, Pallas kernels, inner(): pl.pallas_call(inner_kernel, out_shape=outs, in_specs=[VMEM] * 4, out_spe...  5.28 us
    pallas_call x1, Pallas kernels, update(): pl.pallas_call(update_kernel, out_shape=(out, out), in_specs=[VMEM] * 4,...  1.65 us
    pallas_call x1, Pallas kernels, load(): pl.pallas_call(load_kernel, out_shape=(grown, grown), in_specs=[HBM, HBM,...  1.56 us
    pallas_call x1, Pallas kernels, outer(): pl.pallas_call(outer_kernel, out_shape=(shape(layers, rows, lanes), shape...  1.36 us
    pallas_call x1, Pallas kernels, pack(): pl.pallas_call(pack_kernel, out_shape=(x_out, x_out, y_out, y_out), in_sp...  1.22 us
  transfers between devices with their start and end apart: 11, of which 6 were waited for; matrix products, arithmetic and copies ran while one was open for 0% of the time, Pallas kernels for 19%

profile of v3, /device:TPU:0, one launch (start us, length us, event | category | flops | bytes accessed | tf_op | source)
XLA Modules:
  0.0 35.9 jit_solution(10351129555818191349)
XLA Ops:
  0.6 1.2 %pack.1 = (f32[3,128,128]{2,1,0:T(8,128)S(1)}, f32[3,128,128]{2,1,0:T(8,128)S(1)}, f32[16,8,128]{2,1,0:T(8,128)S(1)}, f32[16,8,128]{2,1,0:T(8,128)S(1)}) custom-call(f32[16,128,128]{2,1,0:T(8,128)} %cond.3, f32[16,128,128]{2,1,0:T(8,128)} %resid.3), custom_call_target="tpu_custom_call" | custom-call | tf_op jit(solution)/shard_map/pack/pallas_call | solution.py:101
  1.9 2.4 %collective-permute-start.1 = (f32[16,8,128]{2,1,0:T(8,128)S(1)}, f32[16,8,128]{2,1,0:T(8,128)S(1)}, u32[]{:S(2)}, u32[]{:S(2)}) collective-permute-start(f32[16,8,128]{2,1,0:T(8,128)S(1)} %get-tuple-element.25), channel_id=1, source_target_pairs={{0,3},{1,2},{2,1},{3,0},{4,7},{5,6},{6,5},{7,4},{8,11},{9,10},{10,... | collective-permute-start | bytes 196616 | tf_op jit(solution)/shard_map/ppermute | solution.py:31
  4.3 0.7 %collective-permute-start = (f32[16,8,128]{2,1,0:T(8,128)S(1)}, f32[16,8,128]{2,1,0:T(8,128)S(1)}, u32[]{:S(2)}, u32[]{:S(2)}) collective-permute-start(f32[16,8,128]{2,1,0:T(8,128)S(1)} %get-tuple-element.22.after), channel_id=1, source_target_pairs={{0,1},{1,0},{2,3},{3,2},{4,5},{5,4},{6,7},{7,6},{8,9},{9,8},{10,11... | collective-permute-start | bytes 196616 | tf_op jit(solution)/shard_map/ppermute | solution.py:31
  5.0 1.5 %collective-permute-start.2 = (f32[3,128,128]{2,1,0:T(8,128)S(1)}, f32[3,128,128]{2,1,0:T(8,128)S(1)}, u32[]{:S(2)}, u32[]{:S(2)}) collective-permute-start(f32[3,128,128]{2,1,0:T(8,128)S(1)} %get-tuple-element.35), channel_id=1, source_target_pairs={{0,4},{1,5},{2,6},{3,7},{4,0},{5,1},{6,2},{7,3},{8,12},{9,13},{10,... | collective-permute-start | bytes 589832 | tf_op jit(solution)/shard_map/ppermute | solution.py:31
  6.5 0.0 collective-permute-start.3
  6.5 1.6 %load.1 = (f32[16,160,128]{2,1,0:T(8,128)S(1)}, f32[16,160,128]{2,1,0:T(8,128)S(1)}) custom-call(f32[16,128,128]{2,1,0:T(8,128)} %cond.3, f32[16,128,128]{2,1,0:T(8,128)} %resid.3, f32[16,8,128]{2,1,0:T(8,128)S(1)} %get-tuple-element.22.after), custom_call_target="tpu_custom_call" | custom-call | flops 1000000000 | bytes 1048576 | tf_op jit(solution)/shard_map/load/pallas_call | solution.py:133
  8.1 0.0 collective-permute-done.1.y_odd
  8.1 0.0 collective-permute-done.y_even
  8.1 0.2 edge_terms.1
  8.2 3.1 %collective-permute-start.4 = (f32[136,128]{1,0:T(8,128)S(1)}, f32[136,128]{1,0:T(8,128)S(1)}, u32[]{:S(2)}, u32[]{:S(2)}) collective-permute-start(f32[136,128]{1,0:T(8,128)S(1)} %get-tuple-element.37), channel_id=1, source_target_pairs={{0,4},{1,5},{2,6},{3,7},{4,0},{5,1},{6,2},{7,3},{8,12},{9,13},{10,... | collective-permute-start | bytes 208904 | tf_op jit(solution)/shard_map/ppermute | solution.py:31
  11.3 0.0 collective-permute-start.5
  11.4 5.3 %inner.1 = (f32[16,160,128]{2,1,0:T(8,128)S(1)}, f32[16,160,128]{2,1,0:T(8,128)S(1)}, f32[16,128,128]{2,1,0:T(8,128)S(1)}, f32[16,128,128]{2,1,0:T(8,128)S(1)}, ...) custom-call(f32[16,160,128]{2,1,0:T(8,128)S(1)} %get-tuple-element.2, ...), custom_call_target="tpu_custom_call", output_to_operand_aliasing={{0}: (0, {}), {1}: (1, {})} | custom-call | flops 4000000000 | bytes 1 | tf_op jit(solution)/shard_map/inner/pallas_call | solution.py:346
  16.6 1.4 %collective-permute-done.4.t_even = f32[136,128]{1,0:T(8,128)S(1)} collective-permute-done((f32[136,128]{1,0:T(8,128)S(1)}, f32[136,128]{1,0:T(8,128)S(1)}, u32[]{:S(2)}, u32[]{:S(2)}) %collective-permute-start.4) | collective-permute-done | bytes 69664 | tf_op jit(solution)/shard_map/ppermute | solution.py:31
  18.0 0.0 collective-permute-done.5.t_odd
  18.0 0.0 collective-permute-done.2.x_even
  18.0 0.0 collective-permute-done.3.x_odd
  18.0 1.4 %outer.1 = (f32[16,128,128]{2,1,0:T(8,128)S(1)}, f32[16,128,128]{2,1,0:T(8,128)S(1)}, f32[2,128]{1,0:T(2,128)S(1)}) custom-call(f32[16,160,128]{2,1,0:T(8,128)S(1)} %get-tuple-element.26.b_u, f32[16,160,128]{2,1,0:T(8,128)S(1)} %get-tuple-element.27.b_r.resid, ...), custom_call_target="tpu_custom_call", output_to_operand_aliasing={{0}: (2, {}), {1}: (3, {})} | custom-call | tf_op jit(solution)/shard_map/outer/pallas_call | solution.py:509
  19.4 0.1 collective-permute-start.6
  19.5 1.1 %collective-permute-done.6 = f32[2,128]{1,0:T(2,128)S(1)} collective-permute-done((f32[2,128]{1,0:T(2,128)S(1)}, f32[2,128]{1,0:T(2,128)S(1)}, u32[]{:S(2)}, u32[]{:S(2)}) %collective-permute-start.6) | collective-permute-done | bytes 1056 | tf_op jit(solution)/shard_map/ppermute | solution.py:31
  20.6 0.3 collective-permute-start.7
  20.9 2.7 %collective-permute-done.7 = f32[2,128]{1,0:T(2,128)S(1)} collective-permute-done((f32[2,128]{1,0:T(2,128)S(1)}, f32[2,128]{1,0:T(2,128)S(1)}, u32[]{:S(2)}, u32[]{:S(2)}) %collective-permute-start.7) | collective-permute-done | bytes 1056 | tf_op jit(solution)/shard_map/ppermute | solution.py:31
  23.6 2.3 %collective-permute-start.8 = (f32[2,128]{1,0:T(2,128)S(1)}, f32[2,128]{1,0:T(2,128)S(1)}, u32[]{:S(2)}, u32[]{:S(2)}) collective-permute-start(f32[2,128]{1,0:T(2,128)S(1)} %add.16), channel_id=1, source_target_pairs={{0,5},{1,4},{2,7},{3,6},{4,1},{5,0},{6,3},{7,2},{8,13},{9,12},{10,... | collective-permute-start | bytes 3080 | tf_op jit(solution)/shard_map/ppermute | solution.py:31
  25.9 1.3 %collective-permute-done.8 = f32[2,128]{1,0:T(2,128)S(1)} collective-permute-done((f32[2,128]{1,0:T(2,128)S(1)}, f32[2,128]{1,0:T(2,128)S(1)}, u32[]{:S(2)}, u32[]{:S(2)}) %collective-permute-start.8) | collective-permute-done | bytes 1056 | tf_op jit(solution)/shard_map/ppermute | solution.py:31
  27.2 1.8 %collective-permute-start.9 = (f32[2,128]{1,0:T(2,128)S(1)}, f32[2,128]{1,0:T(2,128)S(1)}, u32[]{:S(2)}, u32[]{:S(2)}) collective-permute-start(f32[2,128]{1,0:T(2,128)S(1)} %add.17), channel_id=1, source_target_pairs={{0,9},{1,8},{2,11},{3,10},{4,13},{5,12},{6,15},{7,14},{8,1},{9,0},... | collective-permute-start | bytes 3080 | tf_op jit(solution)/shard_map/ppermute | solution.py:31
  28.9 1.3 %collective-permute-done.9 = f32[2,128]{1,0:T(2,128)S(1)} collective-permute-done((f32[2,128]{1,0:T(2,128)S(1)}, f32[2,128]{1,0:T(2,128)S(1)}, u32[]{:S(2)}, u32[]{:S(2)}) %collective-permute-start.9) | collective-permute-done | bytes 1056 | tf_op jit(solution)/shard_map/ppermute | solution.py:31
  30.2 2.7 %collective-permute-start.10 = (f32[2,128]{1,0:T(2,128)S(1)}, f32[2,128]{1,0:T(2,128)S(1)}, u32[]{:S(2)}, u32[]{:S(2)}) collective-permute-start(f32[2,128]{1,0:T(2,128)S(1)} %add.18), channel_id=1, source_target_pairs={{0,17},{1,16},{2,19},{3,18},{4,21},{5,20},{6,23},{7,22},{8,25},{9,... | collective-permute-start | bytes 3080 | tf_op jit(solution)/shard_map/ppermute | solution.py:31
  33.0 1.3 %collective-permute-done.10 = f32[2,128]{1,0:T(2,128)S(1)} collective-permute-done((f32[2,128]{1,0:T(2,128)S(1)}, f32[2,128]{1,0:T(2,128)S(1)}, u32[]{:S(2)}, u32[]{:S(2)}) %collective-permute-start.10) | collective-permute-done | bytes 1056 | tf_op jit(solution)/shard_map/ppermute | solution.py:31
  34.3 1.6 %update.1 = (f32[16,128,128]{2,1,0:T(8,128)}, f32[16,128,128]{2,1,0:T(8,128)}) custom-call(f32[2,128]{1,0:T(2,128)S(1)} %add.19.sums, f32[16,128,128]{2,1,0:T(8,128)S(1)} %get-tuple-element.40.precond, f32[16,128,128]{2,1,0:T(8,128)S(1)} %get-tuple-element.41.image, f32[16,160,128]{2,1,0:T(8,128)S(1)} %get-tuple-element.27.b_r.resid), custom_call_target="tpu_custom_call" | custom-call | tf_op jit(solution)/shard_map/update/pallas_call | solution.py:563
  (5 shorter events, 0.0 us)
Async XLA Ops:
  1.9 6.2 %collective-permute-start.1 = (f32[16,8,128]{2,1,0:T(8,128)S(1)}, f32[16,8,128]{2,1,0:T(8,128)S(1)}, u32[]{:S(2)}, u32[]{:S(2)}) collective-permute-start(f32[16,8,128]{2,1,0:T(8,128)S(1)} %get-tuple-element.25), channel_id=1, source_target_pairs={{0,3},{1,2},{2,1},{3,0},{4,7},{5,6},{6,5},{7,4},{8,11},{9,10},{10,... | collective-permute-start | bytes 196616 | tf_op jit(solution)/shard_map/ppermute | solution.py:31
  4.3 3.8 %collective-permute-start = (f32[16,8,128]{2,1,0:T(8,128)S(1)}, f32[16,8,128]{2,1,0:T(8,128)S(1)}, u32[]{:S(2)}, u32[]{:S(2)}) collective-permute-start(f32[16,8,128]{2,1,0:T(8,128)S(1)} %get-tuple-element.22.after), channel_id=1, source_target_pairs={{0,1},{1,0},{2,3},{3,2},{4,5},{5,4},{6,7},{7,6},{8,9},{9,8},{10,11... | collective-permute-start | bytes 196616 | tf_op jit(solution)/shard_map/ppermute | solution.py:31
  5.0 13.1 %collective-permute-start.2 = (f32[3,128,128]{2,1,0:T(8,128)S(1)}, f32[3,128,128]{2,1,0:T(8,128)S(1)}, u32[]{:S(2)}, u32[]{:S(2)}) collective-permute-start(f32[3,128,128]{2,1,0:T(8,128)S(1)} %get-tuple-element.35), channel_id=1, source_target_pairs={{0,4},{1,5},{2,6},{3,7},{4,0},{5,1},{6,2},{7,3},{8,12},{9,13},{10,... | collective-permute-start | bytes 589832 | tf_op jit(solution)/shard_map/ppermute | solution.py:31
  6.5 11.5 %collective-permute-start.3 = (f32[3,128,128]{2,1,0:T(8,128)S(1)}, f32[3,128,128]{2,1,0:T(8,128)S(1)}, u32[]{:S(2)}, u32[]{:S(2)}) collective-permute-start(f32[3,128,128]{2,1,0:T(8,128)S(1)} %get-tuple-element.36), channel_id=1, source_target_pairs={{0,1},{1,0},{2,3},{3,2},{4,8},{5,9},{6,10},{7,11},{8,4},{9,5},{10,... | collective-permute-start | bytes 589832 | tf_op jit(solution)/shard_map/ppermute | solution.py:31
  8.2 9.8 %collective-permute-start.4 = (f32[136,128]{1,0:T(8,128)S(1)}, f32[136,128]{1,0:T(8,128)S(1)}, u32[]{:S(2)}, u32[]{:S(2)}) collective-permute-start(f32[136,128]{1,0:T(8,128)S(1)} %get-tuple-element.37), channel_id=1, source_target_pairs={{0,4},{1,5},{2,6},{3,7},{4,0},{5,1},{6,2},{7,3},{8,12},{9,13},{10,... | collective-permute-start | bytes 208904 | tf_op jit(solution)/shard_map/ppermute | solution.py:31
  11.3 6.7 %collective-permute-start.5 = (f32[136,128]{1,0:T(8,128)S(1)}, f32[136,128]{1,0:T(8,128)S(1)}, u32[]{:S(2)}, u32[]{:S(2)}) collective-permute-start(f32[136,128]{1,0:T(8,128)S(1)} %get-tuple-element.38), channel_id=1, source_target_pairs={{0,1},{1,0},{2,3},{3,2},{4,8},{5,9},{6,10},{7,11},{8,4},{9,5},{10,... | collective-permute-start | bytes 208904 | tf_op jit(solution)/shard_map/ppermute | solution.py:31
  19.4 1.2 %collective-permute-start.6 = (f32[2,128]{1,0:T(2,128)S(1)}, f32[2,128]{1,0:T(2,128)S(1)}, u32[]{:S(2)}, u32[]{:S(2)}) collective-permute-start(f32[2,128]{1,0:T(2,128)S(1)} %get-tuple-element.39), channel_id=1, source_target_pairs={{0,1},{1,0},{2,3},{3,2},{4,5},{5,4},{6,7},{7,6},{8,9},{9,8},{10,11... | collective-permute-start | bytes 3080 | tf_op jit(solution)/shard_map/ppermute | solution.py:31
  20.6 3.0 %collective-permute-start.7 = (f32[2,128]{1,0:T(2,128)S(1)}, f32[2,128]{1,0:T(2,128)S(1)}, u32[]{:S(2)}, u32[]{:S(2)}) collective-permute-start(f32[2,128]{1,0:T(2,128)S(1)} %add.15), channel_id=1, source_target_pairs={{0,3},{1,2},{2,1},{3,0},{4,7},{5,6},{6,5},{7,4},{8,11},{9,10},{10,... | collective-permute-start | bytes 3080 | tf_op jit(solution)/shard_map/ppermute | solution.py:31
  23.6 3.6 %collective-permute-start.8 = (f32[2,128]{1,0:T(2,128)S(1)}, f32[2,128]{1,0:T(2,128)S(1)}, u32[]{:S(2)}, u32[]{:S(2)}) collective-permute-start(f32[2,128]{1,0:T(2,128)S(1)} %add.16), channel_id=1, source_target_pairs={{0,5},{1,4},{2,7},{3,6},{4,1},{5,0},{6,3},{7,2},{8,13},{9,12},{10,... | collective-permute-start | bytes 3080 | tf_op jit(solution)/shard_map/ppermute | solution.py:31
  27.2 3.1 %collective-permute-start.9 = (f32[2,128]{1,0:T(2,128)S(1)}, f32[2,128]{1,0:T(2,128)S(1)}, u32[]{:S(2)}, u32[]{:S(2)}) collective-permute-start(f32[2,128]{1,0:T(2,128)S(1)} %add.17), channel_id=1, source_target_pairs={{0,9},{1,8},{2,11},{3,10},{4,13},{5,12},{6,15},{7,14},{8,1},{9,0},... | collective-permute-start | bytes 3080 | tf_op jit(solution)/shard_map/ppermute | solution.py:31
  30.2 4.0 %collective-permute-start.10 = (f32[2,128]{1,0:T(2,128)S(1)}, f32[2,128]{1,0:T(2,128)S(1)}, u32[]{:S(2)}, u32[]{:S(2)}) collective-permute-start(f32[2,128]{1,0:T(2,128)S(1)} %add.18), channel_id=1, source_target_pairs={{0,17},{1,16},{2,19},{3,18},{4,21},{5,20},{6,23},{7,22},{8,25},{9,... | collective-permute-start | bytes 3080 | tf_op jit(solution)/shard_map/ppermute | solution.py:31

commit v4 on v3

--- a/solution.py
+++ b/solution.py
@@ -494,12 +494,14 @@
                 i_out[at[k], out_rows] = image
                 rz = rz + eight(b_r[at[k], here] * mid)
                 pq = pq + eight(mid * image)
-    total_out[0:1] = jnp.broadcast_to(jnp.sum(rz, keepdims=True), (1, zero.shape[1]))
-    total_out[1:2] = jnp.broadcast_to(jnp.sum(pq, keepdims=True), (1, zero.shape[1]))
+    lane = lax.broadcasted_iota(jnp.int32, total_out.shape, 1)
+    rz, pq = jnp.sum(rz, keepdims=True), jnp.sum(pq, keepdims=True)
+    total_out[...] = jnp.where(lane < total_out.shape[1] // 2, rz, pq)
 
 
 def outer(found, x_even, x_odd, t_even, t_odd):
     p_in = found[2]
+    parts = lax.axis_size("gx") * lax.axis_size("gy")
     layers, rows, lanes = p_in.shape
     grown = rows + 4 * HALO
 
@@ -508,7 +510,9 @@
 
     return pl.pallas_call(
         outer_kernel,
-        out_shape=(shape(layers, rows, lanes), shape(layers, rows, lanes), shape(2, lanes)),
+        out_shape=(
+            shape(layers, rows, lanes), shape(layers, rows, lanes), shape(parts, lanes),
+        ),
         in_specs=[VMEM] * 13,
         out_specs=(VMEM, VMEM, VMEM),
         scratch_shapes=[
@@ -520,24 +524,10 @@
     )(*found, x_even, x_odd, t_even, t_odd)
 
 
-def power_of_two(count):
-    return count & (count - 1) == 0
-
-
-def sum_everywhere(value):
-    count_x, count_y = lax.axis_size("gx"), lax.axis_size("gy")
-    if not (power_of_two(count_x) and power_of_two(count_y)):
-        return lax.psum(value, ("gx", "gy"))
-    low = 1 if count_y > 1 else 0
-    steps = [(0, 1 << bit | low) for bit in range(count_y.bit_length() - 1)]
-    steps += [(1 << bit, low) for bit in range(count_x.bit_length() - 1)]
-    for step_x, step_y in steps:
-        value = value + swap(value, lambda x, y: (x ^ step_x, y ^ step_y))
-    return value
-
-
 def update_kernel(sums, precond, image, resid, pressure, residual, held, sem):
-    half_alpha = sums[0:1] / sums[1:2]
+    total = jnp.sum(sums[...], axis=0, keepdims=True)
+    half = total.shape[1] // 2
+    half_alpha = total[0:1, 0:1] / total[0:1, half : half + 1]
     alpha = 2.0 * half_alpha
     layers, rows, _ = precond.shape
     own = slice(LOW, LOW + rows)
@@ -583,7 +573,8 @@
     t_even, t_odd = swap_x(t_even, 0), swap_x(t_odd, 1)
     found = inner(u, r, y_even, y_odd)
     precond, image, sums = outer(found, x_even, x_odd, t_even, t_odd)
-    return update(sum_everywhere(sums), precond, image, found[1])
+    sums = lax.all_to_all(sums, ("gx", "gy"), 0, 0, tiled=True)
+    return update(sums, precond, image, found[1])
 
 
 def solution(mesh):

time: 36.1 us -> 33.2 us (0.920)
  blocking collectives: 0 us -> 11.9 us
  waiting for transfers between devices: 9.08 us -> 1.39 us
  starting transfers between devices: 14.9 us -> 7.74 us
    all_to_all x0 -> x1, blocking collectives: none -> 11.9 us  [on_device(): sums = lax.all_to_all(sums, ('gx', 'gy'), 0, 0, tiled=True)]
    ppermute x11 -> x6, waiting for transfers between devices: 9.08 us -> 1.39 us  [swap(): return lax.ppermute(value, ('gx', 'gy'), pairs)]
    ppermute x11 -> x6, starting transfers between devices: 14.9 us -> 7.74 us  [swap(): return lax.ppermute(value, ('gx', 'gy'), pairs)]
  transfers between devices with their start and end apart: 11 -> 6, of which waited for: 6 -> 1; matrix products, arithmetic and copies ran while one was open for 0% -> 0% of each run, Pallas kernels for 19% -> 21%
where the time goes in v4:
time: 33.2 us; the launch traced here: 33 us
  blocking collectives  11.9 us (36%)
  Pallas kernels  11.3 us (34%)
  starting transfers between devices  7.74 us (23%)
  waiting for transfers between devices  1.39 us (4%)
  between operations  0.69 us (2%)
    all_to_all x1, blocking collectives, on_device(): sums = lax.all_to_all(sums, ('gx', 'gy'), 0, 0, tiled=True)  11.9 us
    ppermute x6, starting transfers between devices, swap(): return lax.ppermute(value, ('gx', 'gy'), pairs)  7.74 us
    pallas_call x1, Pallas kernels, inner(): pl.pallas_call(inner_kernel, out_shape=outs, in_specs=[VMEM] * 4, out_spe...  5.28 us
    pallas_call x1, Pallas kernels, update(): pl.pallas_call(update_kernel, out_shape=(out, out), in_specs=[VMEM] * 4,...  1.75 us
    pallas_call x1, Pallas kernels, load(): pl.pallas_call(load_kernel, out_shape=(grown, grown), in_specs=[HBM, HBM,...  1.56 us
    ppermute x6, waiting for transfers between devices, swap(): return lax.ppermute(value, ('gx', 'gy'), pairs)  1.39 us
    pallas_call x1, Pallas kernels, outer(): pl.pallas_call(outer_kernel, out_shape=(shape(layers, rows, lanes), shape...  1.36 us
    pallas_call x1, Pallas kernels, pack(): pl.pallas_call(pack_kernel, out_shape=(x_out, x_out, y_out, y_out), in_sp...  1.22 us
  transfers between devices with their start and end apart: 6, of which 1 were waited for; matrix products, arithmetic and copies ran while one was open for 0% of the time, Pallas kernels for 21%

profile of v4, /device:TPU:0, one launch (start us, length us, event | category | flops | bytes accessed | tf_op | source)
XLA Modules:
  0.0 33.0 jit_solution(6540311954658173639)
XLA Ops:
  0.6 1.2 %pack.1 = (f32[3,128,128]{2,1,0:T(8,128)S(1)}, f32[3,128,128]{2,1,0:T(8,128)S(1)}, f32[16,8,128]{2,1,0:T(8,128)S(1)}, f32[16,8,128]{2,1,0:T(8,128)S(1)}) custom-call(f32[16,128,128]{2,1,0:T(8,128)} %cond.3, f32[16,128,128]{2,1,0:T(8,128)} %resid.3), custom_call_target="tpu_custom_call" | custom-call | tf_op jit(solution)/shard_map/pack/pallas_call | solution.py:101
  1.9 2.4 %collective-permute-start.1 = (f32[16,8,128]{2,1,0:T(8,128)S(1)}, f32[16,8,128]{2,1,0:T(8,128)S(1)}, u32[]{:S(2)}, u32[]{:S(2)}) collective-permute-start(f32[16,8,128]{2,1,0:T(8,128)S(1)} %get-tuple-element.25), channel_id=1, source_target_pairs={{0,3},{1,2},{2,1},{3,0},{4,7},{5,6},{6,5},{7,4},{8,11},{9,10},{10,... | collective-permute-start | bytes 196616 | tf_op jit(solution)/shard_map/ppermute | solution.py:31
  4.3 0.7 %collective-permute-start = (f32[16,8,128]{2,1,0:T(8,128)S(1)}, f32[16,8,128]{2,1,0:T(8,128)S(1)}, u32[]{:S(2)}, u32[]{:S(2)}) collective-permute-start(f32[16,8,128]{2,1,0:T(8,128)S(1)} %get-tuple-element.22.after), channel_id=1, source_target_pairs={{0,1},{1,0},{2,3},{3,2},{4,5},{5,4},{6,7},{7,6},{8,9},{9,8},{10,11... | collective-permute-start | bytes 196616 | tf_op jit(solution)/shard_map/ppermute | solution.py:31
  5.0 1.5 %collective-permute-start.2 = (f32[3,128,128]{2,1,0:T(8,128)S(1)}, f32[3,128,128]{2,1,0:T(8,128)S(1)}, u32[]{:S(2)}, u32[]{:S(2)}) collective-permute-start(f32[3,128,128]{2,1,0:T(8,128)S(1)} %get-tuple-element.35), channel_id=1, source_target_pairs={{0,4},{1,5},{2,6},{3,7},{4,0},{5,1},{6,2},{7,3},{8,12},{9,13},{10,... | collective-permute-start | bytes 589832 | tf_op jit(solution)/shard_map/ppermute | solution.py:31
  6.5 0.0 collective-permute-start.3
  6.5 1.6 %load.1 = (f32[16,160,128]{2,1,0:T(8,128)S(1)}, f32[16,160,128]{2,1,0:T(8,128)S(1)}) custom-call(f32[16,128,128]{2,1,0:T(8,128)} %cond.3, f32[16,128,128]{2,1,0:T(8,128)} %resid.3, f32[16,8,128]{2,1,0:T(8,128)S(1)} %get-tuple-element.22.after), custom_call_target="tpu_custom_call" | custom-call | flops 1000000000 | bytes 1048576 | tf_op jit(solution)/shard_map/load/pallas_call | solution.py:133
  8.1 0.0 collective-permute-done.1.y_odd
  8.1 0.0 collective-permute-done.y_even
  8.1 0.2 edge_terms.1
  8.2 3.1 %collective-permute-start.4 = (f32[136,128]{1,0:T(8,128)S(1)}, f32[136,128]{1,0:T(8,128)S(1)}, u32[]{:S(2)}, u32[]{:S(2)}) collective-permute-start(f32[136,128]{1,0:T(8,128)S(1)} %get-tuple-element.37), channel_id=1, source_target_pairs={{0,4},{1,5},{2,6},{3,7},{4,0},{5,1},{6,2},{7,3},{8,12},{9,13},{10,... | collective-permute-start | bytes 208904 | tf_op jit(solution)/shard_map/ppermute | solution.py:31
  11.3 0.0 collective-permute-start.5
  11.4 5.3 %inner.1 = (f32[16,160,128]{2,1,0:T(8,128)S(1)}, f32[16,160,128]{2,1,0:T(8,128)S(1)}, f32[16,128,128]{2,1,0:T(8,128)S(1)}, f32[16,128,128]{2,1,0:T(8,128)S(1)}, ...) custom-call(f32[16,160,128]{2,1,0:T(8,128)S(1)} %get-tuple-element.2, ...), custom_call_target="tpu_custom_call", output_to_operand_aliasing={{0}: (0, {}), {1}: (1, {})} | custom-call | flops 4000000000 | bytes 1 | tf_op jit(solution)/shard_map/inner/pallas_call | solution.py:346
  16.6 1.4 %collective-permute-done.4.t_even = f32[136,128]{1,0:T(8,128)S(1)} collective-permute-done((f32[136,128]{1,0:T(8,128)S(1)}, f32[136,128]{1,0:T(8,128)S(1)}, u32[]{:S(2)}, u32[]{:S(2)}) %collective-permute-start.4) | collective-permute-done | bytes 69664 | tf_op jit(solution)/shard_map/ppermute | solution.py:31
  18.0 0.0 collective-permute-done.5.t_odd
  18.0 0.0 collective-permute-done.2.x_even
  18.0 0.0 collective-permute-done.3.x_odd
  18.0 1.4 %outer.1 = (f32[16,128,128]{2,1,0:T(8,128)S(1)}, f32[16,128,128]{2,1,0:T(8,128)S(1)}, f32[32,128]{1,0:T(8,128)S(1)}) custom-call(f32[16,160,128]{2,1,0:T(8,128)S(1)} %get-tuple-element.26.b_u, f32[16,160,128]{2,1,0:T(8,128)S(1)} %get-tuple-element.27.b_r.resid, ...), custom_call_target="tpu_custom_call", output_to_operand_aliasing={{0}: (2, {}), {1}: (3, {})} | custom-call | tf_op jit(solution)/shard_map/outer/pallas_call | solution.py:511
  19.4 11.9 %all_to_all.11 = f32[32,1,128]{2,1,0:T(1,128)S(1)} all-to-all(f32[32,1,128]{2,1,0:T(1,128)S(1)} %bitcast.5), channel_id=1, replica_groups=mesh['gx'=8,'gy'=4] {'gx','gy'}, dimensions={0} | all-to-all | bytes 32768 | tf_op jit(solution)/shard_map/all_to_all | solution.py:576
  31.3 1.8 %update.1 = (f32[16,128,128]{2,1,0:T(8,128)}, f32[16,128,128]{2,1,0:T(8,128)}) custom-call(f32[32,128]{1,0:T(8,128)S(1)} %bitcast.4, f32[16,128,128]{2,1,0:T(8,128)S(1)} %get-tuple-element.40.precond, f32[16,128,128]{2,1,0:T(8,128)S(1)} %get-tuple-element.41.image, f32[16,160,128]{2,1,0:T(8,128)S(1)} %get-tuple-element.27.b_r.resid), custom_call_target="tpu_custom_call" | custom-call | tf_op jit(solution)/shard_map/update/pallas_call | solution.py:553
Async XLA Ops:
  1.9 6.2 %collective-permute-start.1 = (f32[16,8,128]{2,1,0:T(8,128)S(1)}, f32[16,8,128]{2,1,0:T(8,128)S(1)}, u32[]{:S(2)}, u32[]{:S(2)}) collective-permute-start(f32[16,8,128]{2,1,0:T(8,128)S(1)} %get-tuple-element.25), channel_id=1, source_target_pairs={{0,3},{1,2},{2,1},{3,0},{4,7},{5,6},{6,5},{7,4},{8,11},{9,10},{10,... | collective-permute-start | bytes 196616 | tf_op jit(solution)/shard_map/ppermute | solution.py:31
  4.3 3.8 %collective-permute-start = (f32[16,8,128]{2,1,0:T(8,128)S(1)}, f32[16,8,128]{2,1,0:T(8,128)S(1)}, u32[]{:S(2)}, u32[]{:S(2)}) collective-permute-start(f32[16,8,128]{2,1,0:T(8,128)S(1)} %get-tuple-element.22.after), channel_id=1, source_target_pairs={{0,1},{1,0},{2,3},{3,2},{4,5},{5,4},{6,7},{7,6},{8,9},{9,8},{10,11... | collective-permute-start | bytes 196616 | tf_op jit(solution)/shard_map/ppermute | solution.py:31
  5.0 13.1 %collective-permute-start.2 = (f32[3,128,128]{2,1,0:T(8,128)S(1)}, f32[3,128,128]{2,1,0:T(8,128)S(1)}, u32[]{:S(2)}, u32[]{:S(2)}) collective-permute-start(f32[3,128,128]{2,1,0:T(8,128)S(1)} %get-tuple-element.35), channel_id=1, source_target_pairs={{0,4},{1,5},{2,6},{3,7},{4,0},{5,1},{6,2},{7,3},{8,12},{9,13},{10,... | collective-permute-start | bytes 589832 | tf_op jit(solution)/shard_map/ppermute | solution.py:31
  6.5 11.5 %collective-permute-start.3 = (f32[3,128,128]{2,1,0:T(8,128)S(1)}, f32[3,128,128]{2,1,0:T(8,128)S(1)}, u32[]{:S(2)}, u32[]{:S(2)}) collective-permute-start(f32[3,128,128]{2,1,0:T(8,128)S(1)} %get-tuple-element.36), channel_id=1, source_target_pairs={{0,1},{1,0},{2,3},{3,2},{4,8},{5,9},{6,10},{7,11},{8,4},{9,5},{10,... | collective-permute-start | bytes 589832 | tf_op jit(solution)/shard_map/ppermute | solution.py:31
  8.2 9.8 %collective-permute-start.4 = (f32[136,128]{1,0:T(8,128)S(1)}, f32[136,128]{1,0:T(8,128)S(1)}, u32[]{:S(2)}, u32[]{:S(2)}) collective-permute-start(f32[136,128]{1,0:T(8,128)S(1)} %get-tuple-element.37), channel_id=1, source_target_pairs={{0,4},{1,5},{2,6},{3,7},{4,0},{5,1},{6,2},{7,3},{8,12},{9,13},{10,... | collective-permute-start | bytes 208904 | tf_op jit(solution)/shard_map/ppermute | solution.py:31
  11.3 6.7 %collective-permute-start.5 = (f32[136,128]{1,0:T(8,128)S(1)}, f32[136,128]{1,0:T(8,128)S(1)}, u32[]{:S(2)}, u32[]{:S(2)}) collective-permute-start(f32[136,128]{1,0:T(8,128)S(1)} %get-tuple-element.38), channel_id=1, source_target_pairs={{0,1},{1,0},{2,3},{3,2},{4,8},{5,9},{6,10},{7,11},{8,4},{9,5},{10,... | collective-permute-start | bytes 208904 | tf_op jit(solution)/shard_map/ppermute | solution.py:31

commit v5 on v4

--- a/solution.py
+++ b/solution.py
@@ -260,7 +260,7 @@
             target[k, LOW + rows : LOW + rows + HALO] = north
         return carry
 
-    lax.fori_loop(0, layers, halo, 0)
+    lax.fori_loop(0, layers, halo, 0, unroll=16)
     chunks = row_chunks(rows)
 
     def first(k, carry):
@@ -280,7 +280,7 @@
             w[k, here] = mid * value
         return carry
 
-    lax.fori_loop(1, layers - 1, first, 0)
+    lax.fori_loop(1, layers - 1, first, 0, unroll=14)
 
     def second(k, carry):
         for start, size in chunks:
@@ -301,7 +301,7 @@
             q[k, here] = mid * value
         return carry
 
-    lax.fori_loop(2, layers - 2, second, 0)
+    lax.fori_loop(2, layers - 2, second, 0, unroll=12)
 
     def third(k, carry):
         rz, pq = carry
@@ -320,7 +320,7 @@
         return rz, pq
 
     zero = jnp.zeros((8, u.shape[2]), F32)
-    rz, pq = lax.fori_loop(3, layers - 3, third, (zero, zero))
+    rz, pq = lax.fori_loop(3, layers - 3, third, (zero, zero), unroll=10)
     sums[0] = rz
     sums[1] = pq
     full = slice(HALO, LOW + rows + HALO)
@@ -351,7 +351,7 @@
         scratch_shapes=[field] * 6 + [pltpu.VMEM((4, grown, lanes), F32)],
         input_output_aliases={0: 0, 1: 1},
         compiler_params=params(12),
-        cost_estimate=pl.CostEstimate(flops=4_000_000_000, transcendentals=0, bytes_accessed=1),
+        cost_estimate=pl.CostEstimate(flops=100_000_000, transcendentals=0, bytes_accessed=1),
         name="inner",
     )(u, r, y_even, y_odd)
 

time: 33.2 us -> 32.4 us (0.976)
  Pallas kernels: 11.3 us -> 8.36 us
  blocking collectives: 11.9 us -> 12.8 us
  waiting for transfers between devices: 1.39 us -> 2 us
  starting transfers between devices: 7.74 us -> 8.35 us
    pallas_call x1, Pallas kernels: 5.28 us -> 2.31 us  [inner(): pl.pallas_call(inner_kernel, out_shape=outs, in_specs=[VMEM] * 4, out_spe...]
    all_to_all x1, blocking collectives: 11.9 us -> 12.8 us  [on_device(): sums = lax.all_to_all(sums, ('gx', 'gy'), 0, 0, tiled=True)]
    ppermute x6, waiting for transfers between devices: 1.39 us -> 2 us  [swap(): return lax.ppermute(value, ('gx', 'gy'), pairs)]
    ppermute x6, starting transfers between devices: 7.74 us -> 8.35 us  [swap(): return lax.ppermute(value, ('gx', 'gy'), pairs)]
  transfers between devices with their start and end apart: 6 -> 6, of which waited for: 1 -> 2; matrix products, arithmetic and copies ran while one was open for 0% -> 0% of each run, Pallas kernels for 21% -> 13%
where the time goes in v5:
time: 32.4 us; the launch traced here: 32.2 us
  blocking collectives  12.8 us (40%)
  Pallas kernels  8.36 us (26%)
  starting transfers between devices  8.35 us (26%)
  waiting for transfers between devices  2 us (6%)
  between operations  0.67 us (2%)
    all_to_all x1, blocking collectives, on_device(): sums = lax.all_to_all(sums, ('gx', 'gy'), 0, 0, tiled=True)  12.8 us
    ppermute x6, starting transfers between devices, swap(): return lax.ppermute(value, ('gx', 'gy'), pairs)  8.35 us
    pallas_call x1, Pallas kernels, inner(): pl.pallas_call(inner_kernel, out_shape=outs, in_specs=[VMEM] * 4, out_spe...  2.31 us
    ppermute x6, waiting for transfers between devices, swap(): return lax.ppermute(value, ('gx', 'gy'), pairs)  2 us
    pallas_call x1, Pallas kernels, update(): pl.pallas_call(update_kernel, out_shape=(out, out), in_specs=[VMEM] * 4,...  1.75 us
    pallas_call x1, Pallas kernels, load(): pl.pallas_call(load_kernel, out_shape=(grown, grown), in_specs=[HBM, HBM,...  1.56 us
    pallas_call x1, Pallas kernels, outer(): pl.pallas_call(outer_kernel, out_shape=(shape(layers, rows, lanes), shape...  1.36 us
    pallas_call x1, Pallas kernels, pack(): pl.pallas_call(pack_kernel, out_shape=(x_out, x_out, y_out, y_out), in_sp...  1.22 us
  transfers between devices with their start and end apart: 6, of which 2 were waited for; matrix products, arithmetic and copies ran while one was open for 0% of the time, Pallas kernels for 13%

profile of v5, /device:TPU:0, one launch (start us, length us, event | category | flops | bytes accessed | tf_op | source)
XLA Modules:
  0.0 32.2 jit_solution(18185995018393970470)
XLA Ops:
  0.6 1.2 %pack.1 = (f32[3,128,128]{2,1,0:T(8,128)S(1)}, f32[3,128,128]{2,1,0:T(8,128)S(1)}, f32[16,8,128]{2,1,0:T(8,128)S(1)}, f32[16,8,128]{2,1,0:T(8,128)S(1)}) custom-call(f32[16,128,128]{2,1,0:T(8,128)} %cond.3, f32[16,128,128]{2,1,0:T(8,128)} %resid.3), custom_call_target="tpu_custom_call" | custom-call | tf_op jit(solution)/shard_map/pack/pallas_call | solution.py:101
  1.9 3.0 %collective-permute-start.2 = (f32[3,128,128]{2,1,0:T(8,128)S(1)}, f32[3,128,128]{2,1,0:T(8,128)S(1)}, u32[]{:S(2)}, u32[]{:S(2)}) collective-permute-start(f32[3,128,128]{2,1,0:T(8,128)S(1)} %get-tuple-element.35), channel_id=1, source_target_pairs={{0,4},{1,5},{2,6},{3,7},{4,0},{5,1},{6,2},{7,3},{8,12},{9,13},{10,... | collective-permute-start | bytes 589832 | tf_op jit(solution)/shard_map/ppermute | solution.py:31
  4.9 0.0 collective-permute-start.3
  4.9 1.6 %collective-permute-start.1 = (f32[16,8,128]{2,1,0:T(8,128)S(1)}, f32[16,8,128]{2,1,0:T(8,128)S(1)}, u32[]{:S(2)}, u32[]{:S(2)}) collective-permute-start(f32[16,8,128]{2,1,0:T(8,128)S(1)} %get-tuple-element.25), channel_id=1, source_target_pairs={{0,3},{1,2},{2,1},{3,0},{4,7},{5,6},{6,5},{7,4},{8,11},{9,10},{10,... | collective-permute-start | bytes 196616 | tf_op jit(solution)/shard_map/ppermute | solution.py:31
  6.5 0.0 collective-permute-start
  6.5 1.6 %load.1 = (f32[16,160,128]{2,1,0:T(8,128)S(1)}, f32[16,160,128]{2,1,0:T(8,128)S(1)}) custom-call(f32[16,128,128]{2,1,0:T(8,128)} %cond.3, f32[16,128,128]{2,1,0:T(8,128)} %resid.3, f32[16,8,128]{2,1,0:T(8,128)S(1)} %get-tuple-element.22.after), custom_call_target="tpu_custom_call" | custom-call | flops 1000000000 | bytes 1048576 | tf_op jit(solution)/shard_map/load/pallas_call | solution.py:133
  8.1 0.6 %collective-permute-done.1.y_odd = f32[16,8,128]{2,1,0:T(8,128)S(1)} collective-permute-done((f32[16,8,128]{2,1,0:T(8,128)S(1)}, f32[16,8,128]{2,1,0:T(8,128)S(1)}, u32[]{:S(2)}, u32[]{:S(2)}) %collective-permute-start.1) | collective-permute-done | bytes 65568 | tf_op jit(solution)/shard_map/ppermute | solution.py:31
  8.6 0.0 collective-permute-done.y_even
  8.6 0.2 edge_terms.1
  8.8 3.7 %collective-permute-start.4 = (f32[136,128]{1,0:T(8,128)S(1)}, f32[136,128]{1,0:T(8,128)S(1)}, u32[]{:S(2)}, u32[]{:S(2)}) collective-permute-start(f32[136,128]{1,0:T(8,128)S(1)} %get-tuple-element.37), channel_id=1, source_target_pairs={{0,4},{1,5},{2,6},{3,7},{4,0},{5,1},{6,2},{7,3},{8,12},{9,13},{10,... | collective-permute-start | bytes 208904 | tf_op jit(solution)/shard_map/ppermute | solution.py:31
  12.5 0.0 collective-permute-start.5
  12.5 2.3 %inner.1 = (f32[16,160,128]{2,1,0:T(8,128)S(1)}, f32[16,160,128]{2,1,0:T(8,128)S(1)}, f32[16,128,128]{2,1,0:T(8,128)S(1)}, f32[16,128,128]{2,1,0:T(8,128)S(1)}, ...) custom-call(f32[16,160,128]{2,1,0:T(8,128)S(1)} %get-tuple-element.2, ...), custom_call_target="tpu_custom_call", output_to_operand_aliasing={{0}: (0, {}), {1}: (1, {})} | custom-call | flops 100000000 | bytes 1 | tf_op jit(solution)/shard_map/inner/pallas_call | solution.py:346
  14.8 1.4 %collective-permute-done.4.t_even = f32[136,128]{1,0:T(8,128)S(1)} collective-permute-done((f32[136,128]{1,0:T(8,128)S(1)}, f32[136,128]{1,0:T(8,128)S(1)}, u32[]{:S(2)}, u32[]{:S(2)}) %collective-permute-start.4) | collective-permute-done | bytes 69664 | tf_op jit(solution)/shard_map/ppermute | solution.py:31
  16.2 0.0 collective-permute-done.5.t_odd
  16.2 0.0 collective-permute-done.2.x_even
  16.2 0.0 collective-permute-done.3.x_odd
  16.3 1.4 %outer.1 = (f32[16,128,128]{2,1,0:T(8,128)S(1)}, f32[16,128,128]{2,1,0:T(8,128)S(1)}, f32[32,128]{1,0:T(8,128)S(1)}) custom-call(f32[16,160,128]{2,1,0:T(8,128)S(1)} %get-tuple-element.26.b_u, f32[16,160,128]{2,1,0:T(8,128)S(1)} %get-tuple-element.27.b_r.resid, ...), custom_call_target="tpu_custom_call", output_to_operand_aliasing={{0}: (2, {}), {1}: (3, {})} | custom-call | tf_op jit(solution)/shard_map/outer/pallas_call | solution.py:511
  17.6 12.8 %all_to_all.11 = f32[32,1,128]{2,1,0:T(1,128)S(1)} all-to-all(f32[32,1,128]{2,1,0:T(1,128)S(1)} %bitcast.5), channel_id=1, replica_groups=mesh['gx'=8,'gy'=4] {'gx','gy'}, dimensions={0} | all-to-all | bytes 32768 | tf_op jit(solution)/shard_map/all_to_all | solution.py:576
  30.4 1.8 %update.1 = (f32[16,128,128]{2,1,0:T(8,128)}, f32[16,128,128]{2,1,0:T(8,128)}) custom-call(f32[32,128]{1,0:T(8,128)S(1)} %bitcast.4, f32[16,128,128]{2,1,0:T(8,128)S(1)} %get-tuple-element.40.precond, f32[16,128,128]{2,1,0:T(8,128)S(1)} %get-tuple-element.41.image, f32[16,160,128]{2,1,0:T(8,128)S(1)} %get-tuple-element.27.b_r.resid), custom_call_target="tpu_custom_call" | custom-call | tf_op jit(solution)/shard_map/update/pallas_call | solution.py:553
Async XLA Ops:
  1.9 14.4 %collective-permute-start.2 = (f32[3,128,128]{2,1,0:T(8,128)S(1)}, f32[3,128,128]{2,1,0:T(8,128)S(1)}, u32[]{:S(2)}, u32[]{:S(2)}) collective-permute-start(f32[3,128,128]{2,1,0:T(8,128)S(1)} %get-tuple-element.35), channel_id=1, source_target_pairs={{0,4},{1,5},{2,6},{3,7},{4,0},{5,1},{6,2},{7,3},{8,12},{9,13},{10,... | collective-permute-start | bytes 589832 | tf_op jit(solution)/shard_map/ppermute | solution.py:31
  4.9 11.4 %collective-permute-start.3 = (f32[3,128,128]{2,1,0:T(8,128)S(1)}, f32[3,128,128]{2,1,0:T(8,128)S(1)}, u32[]{:S(2)}, u32[]{:S(2)}) collective-permute-start(f32[3,128,128]{2,1,0:T(8,128)S(1)} %get-tuple-element.36), channel_id=1, source_target_pairs={{0,1},{1,0},{2,3},{3,2},{4,8},{5,9},{6,10},{7,11},{8,4},{9,5},{10,... | collective-permute-start | bytes 589832 | tf_op jit(solution)/shard_map/ppermute | solution.py:31
  4.9 3.7 %collective-permute-start.1 = (f32[16,8,128]{2,1,0:T(8,128)S(1)}, f32[16,8,128]{2,1,0:T(8,128)S(1)}, u32[]{:S(2)}, u32[]{:S(2)}) collective-permute-start(f32[16,8,128]{2,1,0:T(8,128)S(1)} %get-tuple-element.25), channel_id=1, source_target_pairs={{0,3},{1,2},{2,1},{3,0},{4,7},{5,6},{6,5},{7,4},{8,11},{9,10},{10,... | collective-permute-start | bytes 196616 | tf_op jit(solution)/shard_map/ppermute | solution.py:31
  6.5 2.1 %collective-permute-start = (f32[16,8,128]{2,1,0:T(8,128)S(1)}, f32[16,8,128]{2,1,0:T(8,128)S(1)}, u32[]{:S(2)}, u32[]{:S(2)}) collective-permute-start(f32[16,8,128]{2,1,0:T(8,128)S(1)} %get-tuple-element.22.after), channel_id=1, source_target_pairs={{0,1},{1,0},{2,3},{3,2},{4,5},{5,4},{6,7},{7,6},{8,9},{9,8},{10,11... | collective-permute-start | bytes 196616 | tf_op jit(solution)/shard_map/ppermute | solution.py:31
  8.8 7.4 %collective-permute-start.4 = (f32[136,128]{1,0:T(8,128)S(1)}, f32[136,128]{1,0:T(8,128)S(1)}, u32[]{:S(2)}, u32[]{:S(2)}) collective-permute-start(f32[136,128]{1,0:T(8,128)S(1)} %get-tuple-element.37), channel_id=1, source_target_pairs={{0,4},{1,5},{2,6},{3,7},{4,0},{5,1},{6,2},{7,3},{8,12},{9,13},{10,... | collective-permute-start | bytes 208904 | tf_op jit(solution)/shard_map/ppermute | solution.py:31
  12.5 3.7 %collective-permute-start.5 = (f32[136,128]{1,0:T(8,128)S(1)}, f32[136,128]{1,0:T(8,128)S(1)}, u32[]{:S(2)}, u32[]{:S(2)}) collective-permute-start(f32[136,128]{1,0:T(8,128)S(1)} %get-tuple-element.38), channel_id=1, source_target_pairs={{0,1},{1,0},{2,3},{3,2},{4,8},{5,9},{6,10},{7,11},{8,4},{9,5},{10,... | collective-permute-start | bytes 208904 | tf_op jit(solution)/shard_map/ppermute | solution.py:31

commit v6 on v5

--- a/solution.py
+++ b/solution.py
@@ -356,172 +356,265 @@
     )(u, r, y_even, y_odd)
 
 
+def around_rows(start, size):
+    return (
+        slice(start, start + size),
+        slice(start - 1, start + size - 1),
+        slice(start + 1, start + size + 1),
+    )
+
+
+def side_layers(layers, side):
+    return tuple(k if side == 0 else layers - 1 - k for k in range(4))
+
+
+def side_place(side):
+    odd, has_low, has_high = place("gx")
+    has = (has_low, has_high)[side]
+    pick = jnp.logical_xor(odd, side == 1)
+
+    def arrived(first, second):
+        return jnp.where(pick, first, second) * has
+
+    return has, 1.0 + has, arrived
+
+
+def start_fields(own, near, side, chunk):
+    b_u, b_r = own[:2]
+    u, r, v, w, _, _, d, inv, masks = near
+    at = side_layers(b_u.shape[0], side)
+    has = side_place(side)[0]
+    here, down, up = around_rows(*chunk)
+    inside = masks[0, here]
+    mid, edge = u[side, 1, here], b_u[at[0], here]
+    total = 6.0 * mid + u[side, 0, here] + edge
+    total = total + u[side, 1, down] + u[side, 1, up] + z_sum(mid)
+    inverse = has * inside / jnp.maximum(total, TINY)
+    value = 2.0 * r[side, here] * inverse
+    inv[side, 0, here] = inverse
+    v[side, 0, here] = value
+    w[side, 0, here] = mid * value
+    total = 6.0 * edge + mid + b_u[at[1], here]
+    total = total + b_u[at[0], down] + b_u[at[0], up] + z_sum(edge)
+    inverse = inside / jnp.maximum(total, TINY)
+    value = 2.0 * b_r[at[0], here] * inverse
+    d[side, here] = total
+    inv[side, 1, here] = inverse
+    v[side, 1, here] = value
+    w[side, 1, here] = edge * value
+
+
+def precond_fields(own, near, side, chunk, rows, term):
+    b_u, b_r, e_v, e_i = own[:4]
+    u, r, v, w, p, q, _, inv, masks = near
+    at = side_layers(b_u.shape[0], side)
+    twice = side_place(side)[1]
+    here, down, up = around_rows(*chunk)
+    plain = is_plain(*chunk, rows)
+
+    def finish(mid, total, south, north, inverse, slot):
+        scale = twice * inverse
+        if plain:
+            total = total + south + north
+        else:
+            total = total + masks[2, here] * south + masks[3, here] * north
+            scale = scale * masks[1, here]
+        value = scale * total
+        p[side, slot, here] = value
+        q[side, slot, here] = mid * value
+        return scale
+
+    mid = u[side, 1, here]
+    total = 2.0 * r[side, here]
+    if term is not None:
+        total = total + term
+    total = total + mid * (v[side, 1, here] + z_sum(v[side, 0, here]))
+    total = total + w[side, 1, here] + z_sum(w[side, 0, here])
+    south = mid * v[side, 0, down] + w[side, 0, down]
+    north = mid * v[side, 0, up] + w[side, 0, up]
+    inv[side, 0, here] = finish(mid, total, south, north, inv[side, 0, here], 0)
+
+    mid, next_u = b_u[at[0], here], b_u[at[1], here]
+    next_v = e_v[side, 0, here]
+    total = 2.0 * b_r[at[0], here]
+    total = total + mid * (v[side, 0, here] + next_v + z_sum(v[side, 1, here]))
+    total = total + w[side, 0, here] + next_u * next_v + z_sum(w[side, 1, here])
+    south = mid * v[side, 1, down] + w[side, 1, down]
+    north = mid * v[side, 1, up] + w[side, 1, up]
+    finish(mid, total, south, north, inv[side, 1, here], 1)
+
+    inner_v = e_v[side, 1, here]
+    total = 2.0 * b_r[at[1], here]
+    total = total + next_u * (v[side, 1, here] + z_sum(next_v))
+    total = total + w[side, 1, here] + z_sum(next_u * next_v)
+    total = total + (next_u + b_u[at[2], here]) * inner_v / twice
+    south = (next_u + b_u[at[1], down]) * e_v[side, 0, down]
+    north = (next_u + b_u[at[1], up]) * e_v[side, 0, up]
+    finish(next_u, total, south, north, e_i[side, 0, here], 2)
+
+
+def image_fields(own, near, side, chunk, k, p_out, i_out):
+    b_u, b_r, _, _, e_d, e_p = own
+    _, _, _, _, p, q, d, _, _ = near
+    at = side_layers(b_u.shape[0], side)
+    here, down, up = around_rows(*chunk)
+    mid_u = b_u[at[k], here]
+    if k < 2:
+        mid, mid_q = p[side, k + 1, here], q[side, k + 1, here]
+        near_y = p[side, k + 1, down] + p[side, k + 1, up]
+        near_q = q[side, k + 1, down] + q[side, k + 1, up]
+        before_p, before_q = p[side, k, here], q[side, k, here]
+        if k == 0:
+            after_p, after_q = p[side, 2, here], q[side, 2, here]
+        else:
+            after_p = e_p[side, 0, here]
+            after_q = b_u[at[2], here] * after_p
+    else:
+        mid = e_p[side, 0, here]
+        mid_q = mid_u * mid
+        low_p, high_p = e_p[side, 0, down], e_p[side, 0, up]
+        near_y = low_p + high_p
+        near_q = b_u[at[2], down] * low_p + b_u[at[2], up] * high_p
+        before_p, before_q = p[side, 2, here], q[side, 2, here]
+        after_p = e_p[side, 1, here]
+        after_q = b_u[at[3], here] * after_p
+    around = before_p + after_p + near_y + z_sum(mid)
+    scaled = before_q + after_q + near_q + z_sum(mid_q)
+    total = d[side, here] if k == 0 else e_d[side, k - 1, here]
+    image = total * mid - mid_u * around - scaled
+    out = slice(chunk[0] - LOW, chunk[0] - LOW + chunk[1])
+    p_out[at[k], out] = mid
+    i_out[at[k], out] = image
+    return eight(b_r[at[k], here] * mid), eight(mid * image)
+
+
+def middle_chunks(rows):
+    rest = rows - 2 * HALO
+    step = rest // 2 if rest % 16 == 0 else rest
+    return [(LOW + HALO + i * step, step) for i in range(rest // step)]
+
+
 def outer_kernel(
-    b_u, b_r, p_in, i_in, e_v, e_i, e_d, e_p, sums, x_even, x_odd, t_even, t_odd,
-    p_out, i_out, total_out,
-    u, r, v, w, p, q, d, t, masks,
+    b_u, b_r, p_in, i_in, e_v, e_i, e_d, e_p, sums, x_even, x_odd,
+    p_out, i_out, sums_out, *near,
 ):
-    layers, rows = p_in.shape[0], p_in.shape[1]
-    odd, has_low, has_high = place("gx")
+    rows = p_in.shape[1]
+    u, r, masks = near[0], near[1], near[-1]
     fill_rows(masks, rows)
-    own = slice(LOW, LOW + rows)
-    zero = jnp.zeros((8, u.shape[2]), F32)
+    own = (b_u, b_r, e_v, e_i, e_d, e_p)
+    here = slice(LOW, LOW + rows)
     rz, pq = sums[0], sums[1]
-    chunks = row_chunks(rows)
+    zero = jnp.zeros(rz.shape, F32)
     for side in range(2):
-        at = tuple(k if side == 0 else layers - 1 - k for k in range(4))
-        has = (has_low, has_high)[side]
-        pick = jnp.logical_xor(odd, side == 1)
-        twice = 1.0 + has
-
-        def arrived(first, second):
-            return jnp.where(pick, first, second) * has
-
-        near, far = (1, 0) if side == 0 else (0, 1)
-        for slot, source in ((0, far), (1, near)):
-            u[slot, own] = arrived(x_even[source], x_odd[source])
-        r[own] = arrived(x_even[2], x_odd[2])
-        t[own] = arrived(t_even[0:rows], t_odd[0:rows])
+        arrived = side_place(side)[2]
+        for slot in range(2):
+            layer = slot if side == 0 else 1 - slot
+            u[side, slot, here] = arrived(x_even[layer], x_odd[layer])
+        r[side, here] = arrived(x_even[2], x_odd[2])
+        for rest in (slice(HALO, LOW), slice(LOW + rows, LOW + rows + HALO)):
+            u[side, 0, rest] = zero
+            u[side, 1, rest] = zero
+            r[side, rest] = zero
+        for chunk in row_chunks(rows):
+            start_fields(own, near, side, chunk)
+        for chunk in row_chunks(rows):
+            precond_fields(own, near, side, chunk, rows, None)
+        for chunk in own_chunks(rows):
+            add_rz, add_pq = image_fields(own, near, side, chunk, 2, p_out, i_out)
+            rz, pq = rz + add_rz, pq + add_pq
+        for chunk in middle_chunks(rows):
+            add_rz, add_pq = image_fields(own, near, side, chunk, 1, p_out, i_out)
+            rz, pq = rz + add_rz, pq + add_pq
+            rz = rz + image_fields(own, near, side, chunk, 0, p_out, i_out)[0]
+    sums_out[0] = rz
+    sums_out[1] = pq
+
+
+def corner_kernel(
+    b_u, b_r, p_in, i_in, e_v, e_i, e_d, e_p, sums, t_even, t_odd, masks, *refs,
+):
+    old, (p_out, i_out, total_out), fields = refs[:8], refs[8:11], refs[11:]
+    near = (*fields, masks)
+    rows = p_in.shape[1]
+    u, r, p, inv = near[0], near[1], near[4], near[7]
+    own = (b_u, b_r, e_v, e_i, e_d, e_p)
+    rz, pq = sums[0], sums[1]
+    zero = jnp.zeros(rz.shape, F32)
+    row = lax.broadcasted_iota(jnp.int32, zero.shape, 0)
+    low, high = slice(HALO, LOW), slice(LOW + rows, LOW + rows + HALO)
+    for side in range(2):
+        at = side_layers(b_u.shape[0], side)
+        arrived = side_place(side)[2]
         corner = arrived(t_even[rows : rows + 8], t_odd[rows : rows + 8])
-        low, high = slice(HALO, LOW), slice(LOW + rows, LOW + rows + HALO)
-        row = lax.broadcasted_iota(jnp.int32, zero.shape, 0)
 
         def one(k):
             return jnp.broadcast_to(corner[k : k + 1], zero.shape)
 
-        u[1, low] = jnp.where(row == 7, one(0), jnp.where(row == 6, one(1), 0.0))
-        u[0, low] = jnp.where(row == 7, one(2), 0.0)
-        r[low] = jnp.where(row == 7, one(3), 0.0)
-        u[1, high] = jnp.where(row == 0, one(4), jnp.where(row == 1, one(5), 0.0))
-        u[0, high] = jnp.where(row == 0, one(6), 0.0)
-        r[high] = jnp.where(row == 0, one(7), 0.0)
-        t[low] = zero
-        t[high] = zero
-
-        for start, size in chunks:
+        u[side, 1, low] = jnp.where(row == 7, one(0), jnp.where(row == 6, one(1), 0.0))
+        u[side, 0, low] = jnp.where(row == 7, one(2), 0.0)
+        r[side, low] = jnp.where(row == 7, one(3), 0.0)
+        u[side, 1, high] = jnp.where(row == 0, one(4), jnp.where(row == 1, one(5), 0.0))
+        u[side, 0, high] = jnp.where(row == 0, one(6), 0.0)
+        r[side, high] = jnp.where(row == 0, one(7), 0.0)
+        for band in range(2):
+            if band == 0:
+                term = [zero, arrived(t_even[0:HALO], t_odd[0:HALO])]
+                chunk, tile = (HALO, 2 * HALO), (LOW, HALO)
+            else:
+                tail = slice(rows - HALO, rows)
+                term = [arrived(t_even[tail], t_odd[tail]), zero]
+                chunk = (LOW + rows - HALO, 2 * HALO)
+                tile = (LOW + rows - HALO, HALO)
+            start_fields(own, near, side, chunk)
+            precond_fields(own, near, side, chunk, rows, jnp.concatenate(term, axis=0))
+            for k in range(2):
+                add_rz, add_pq = image_fields(own, near, side, tile, k, p_out, i_out)
+                rz, pq = rz + add_rz, pq + add_pq
+        for start, size in middle_chunks(rows):
             here = slice(start, start + size)
-            down, up = slice(start - 1, start + size - 1), slice(start + 1, start + size + 1)
-            inside = masks[0, here]
-            mid, edge = u[1, here], b_u[at[0], here]
-            total = 6.0 * mid + u[0, here] + edge + u[1, down] + u[1, up] + z_sum(mid)
-            inverse = has * inside / jnp.maximum(total, TINY)
-            value = 2.0 * r[here] * inverse
-            d[1, here] = inverse
-            v[0, here] = value
-            w[0, here] = mid * value
-            total = 6.0 * edge + mid + b_u[at[1], here]
-            total = total + b_u[at[0], down] + b_u[at[0], up] + z_sum(edge)
-            inverse = inside / jnp.maximum(total, TINY)
-            value = 2.0 * b_r[at[0], here] * inverse
-            d[0, here] = total
-            d[2, here] = inverse
-            v[1, here] = value
-            w[1, here] = edge * value
-
-        for start, size in chunks:
-            here = slice(start, start + size)
-            down, up = slice(start - 1, start + size - 1), slice(start + 1, start + size + 1)
-            plain = is_plain(start, size, rows)
-
-            def finish(mid, total, south, north, inverse, slot, twice):
-                if plain:
-                    value = twice * inverse * (total + south + north)
-                else:
-                    total = total + masks[2, here] * south + masks[3, here] * north
-                    value = twice * masks[1, here] * inverse * total
-                p[slot, here] = value
-                q[slot, here] = mid * value
-
-            mid = u[1, here]
-            total = 2.0 * r[here] + t[here]
-            total = total + mid * (v[1, here] + z_sum(v[0, here]))
-            total = total + w[1, here] + z_sum(w[0, here])
-            south = mid * v[0, down] + w[0, down]
-            north = mid * v[0, up] + w[0, up]
-            finish(mid, total, south, north, d[1, here], 0, twice)
-
-            mid, next_u = b_u[at[0], here], b_u[at[1], here]
-            next_v = e_v[side, 0, here]
-            total = 2.0 * b_r[at[0], here]
-            total = total + mid * (v[0, here] + next_v + z_sum(v[1, here]))
-            total = total + w[0, here] + next_u * next_v + z_sum(w[1, here])
-            south = mid * v[1, down] + w[1, down]
-            north = mid * v[1, up] + w[1, up]
-            finish(mid, total, south, north, d[2, here], 1, twice)
-
-            inner_v = e_v[side, 1, here]
-            total = 2.0 * b_r[at[1], here]
-            total = total + next_u * (v[1, here] + z_sum(next_v))
-            total = total + w[1, here] + z_sum(next_u * next_v)
-            total = total + (next_u * inner_v + b_u[at[2], here] * inner_v) / twice
-            south = (next_u + b_u[at[1], down]) * e_v[side, 0, down]
-            north = (next_u + b_u[at[1], up]) * e_v[side, 0, up]
-            finish(next_u, total, south, north, e_i[side, 0, here], 2, twice)
-
-        for start, size in own_chunks(rows):
-            here = slice(start, start + size)
-            down, up = slice(start - 1, start + size - 1), slice(start + 1, start + size + 1)
-            out_rows = slice(start - LOW, start - LOW + size)
-            for k in range(3):
-                mid_u = b_u[at[k], here]
-                if k < 2:
-                    mid = p[k + 1, here]
-                    near_y = p[k + 1, down] + p[k + 1, up]
-                    near_q = q[k + 1, down] + q[k + 1, up]
-                    mid_q = q[k + 1, here]
-                    before_p, before_q = p[k, here], q[k, here]
-                    if k == 0:
-                        after_p, after_q = p[2, here], q[2, here]
-                    else:
-                        after_p = e_p[side, 0, here]
-                        after_q = b_u[at[2], here] * after_p
-                else:
-                    mid = e_p[side, 0, here]
-                    mid_q = mid_u * mid
-                    low_p, high_p = e_p[side, 0, down], e_p[side, 0, up]
-                    near_y = low_p + high_p
-                    near_q = b_u[at[2], down] * low_p + b_u[at[2], up] * high_p
-                    before_p, before_q = p[2, here], q[2, here]
-                    after_p = e_p[side, 1, here]
-                    after_q = None
-                around = before_p + after_p + near_y + z_sum(mid)
-                if after_q is None:
-                    after_q = b_u[at[3], here] * after_p
-                scaled = before_q + after_q + near_q + z_sum(mid_q)
-                total = d[0, here] if k == 0 else e_d[side, k - 1, here]
-                image = total * mid - mid_u * around - scaled
-                p_out[at[k], out_rows] = mid
-                i_out[at[k], out_rows] = image
-                rz = rz + eight(b_r[at[k], here] * mid)
-                pq = pq + eight(mid * image)
+            out = slice(start - LOW, start - LOW + size)
+            change = inv[side, 0, here] * arrived(t_even[out], t_odd[out])
+            image = i_in[at[0], out] - (b_u[at[0], here] + u[side, 1, here]) * change
+            i_out[at[0], out] = image
+            pq = pq + eight(p[side, 1, here] * image)
     lane = lax.broadcasted_iota(jnp.int32, total_out.shape, 1)
     rz, pq = jnp.sum(rz, keepdims=True), jnp.sum(pq, keepdims=True)
     total_out[...] = jnp.where(lane < total_out.shape[1] // 2, rz, pq)
 
 
-def outer(found, x_even, x_odd, t_even, t_odd):
-    p_in = found[2]
-    parts = lax.axis_size("gx") * lax.axis_size("gy")
-    layers, rows, lanes = p_in.shape
+def outer(found, x_even, x_odd):
+    layers, rows, lanes = found[2].shape
     grown = rows + 4 * HALO
-
-    def field(*lead):
-        return pltpu.VMEM((*lead, grown, lanes), F32)
-
+    full = shape(layers, rows, lanes)
+    sizes = ((2, 2), (2,), (2, 2), (2, 2), (2, 3), (2, 3), (2,), (2, 2), (4,))
+    near = tuple(shape(*size, grown, lanes) for size in sizes)
     return pl.pallas_call(
         outer_kernel,
-        out_shape=(
-            shape(layers, rows, lanes), shape(layers, rows, lanes), shape(parts, lanes),
-        ),
-        in_specs=[VMEM] * 13,
-        out_specs=(VMEM, VMEM, VMEM),
-        scratch_shapes=[
-            field(2), field(), field(2), field(2), field(3), field(3), field(3), field(), field(4),
-        ],
+        out_shape=(full, full, shape(2, 8, lanes), *near),
+        in_specs=[VMEM] * 11,
+        out_specs=(VMEM,) * (3 + len(near)),
         input_output_aliases={2: 0, 3: 1},
         compiler_params=params(4),
         name="outer",
-    )(*found, x_even, x_odd, t_even, t_odd)
+    )(*found, x_even, x_odd)
+
+
+def corners(found, first, t_even, t_odd):
+    layers, rows, lanes = found[2].shape
+    parts = lax.axis_size("gx") * lax.axis_size("gy")
+    p, i, sums, *near, masks = first
+    u, r, _, _, e_v, e_i, e_d, e_p, _ = found
+    full = shape(layers, rows, lanes)
+    fields = tuple(shape(*field.shape) for field in near)
+    return pl.pallas_call(
+        corner_kernel,
+        out_shape=(full, full, shape(parts, lanes), *fields),
+        in_specs=[VMEM] * (12 + len(near)),
+        out_specs=(VMEM,) * (3 + len(near)),
+        input_output_aliases={2: 0, 3: 1, **{12 + k: 3 + k for k in range(len(near))}},
+        compiler_params=params(4),
+        name="corners",
+    )(u, r, p, i, e_v, e_i, e_d, e_p, sums, t_even, t_odd, masks, *near)[:3]
 
 
 def update_kernel(sums, precond, image, resid, pressure, residual, held, sem):
@@ -572,7 +665,8 @@
     t_even, t_odd = edge_terms(u, r, y_even, y_odd)
     t_even, t_odd = swap_x(t_even, 0), swap_x(t_odd, 1)
     found = inner(u, r, y_even, y_odd)
-    precond, image, sums = outer(found, x_even, x_odd, t_even, t_odd)
+    first = outer(found, x_even, x_odd)
+    precond, image, sums = corners(found, first, t_even, t_odd)
     sums = lax.all_to_all(sums, ("gx", "gy"), 0, 0, tiled=True)
     return update(sums, precond, image, found[1])
 

time: 32.4 us -> 31.9 us (0.985)
  waiting for transfers between devices: 2 us -> 0.75 us
  blocking collectives: 12.8 us -> 13.3 us
    ppermute x6, waiting for transfers between devices: 2 us -> 0.75 us  [swap(): return lax.ppermute(value, ('gx', 'gy'), pairs)]
    all_to_all x1, blocking collectives: 12.8 us -> 13.3 us  [on_device(): sums = lax.all_to_all(sums, ('gx', 'gy'), 0, 0, tiled=True)]
    pallas_call x1 -> x2, Pallas kernels: 1.36 us -> 1.65 us  [the longest x1 1.22 us: outer(): pl.pallas_call(outer_kernel, out_shape=(full, full, shape(2, 8, lanes), *...]
  transfers between devices with their start and end apart: 6 -> 6, of which waited for: 2 -> 2; matrix products, arithmetic and copies ran while one was open for 0% -> 0% of each run, Pallas kernels for 13% -> 17%
where the time goes in v6:
time: 31.9 us; the launch traced here: 31.8 us
  blocking collectives  13.3 us (42%)
  Pallas kernels  8.64 us (27%)
  starting transfers between devices  8.35 us (26%)
  waiting for transfers between devices  0.75 us (2%)
  between operations  0.69 us (2%)
    all_to_all x1, blocking collectives, on_device(): sums = lax.all_to_all(sums, ('gx', 'gy'), 0, 0, tiled=True)  13.3 us
    ppermute x6, starting transfers between devices, swap(): return lax.ppermute(value, ('gx', 'gy'), pairs)  8.35 us
    pallas_call x1, Pallas kernels, inner(): pl.pallas_call(inner_kernel, out_shape=outs, in_specs=[VMEM] * 4, out_spe...  2.31 us
    pallas_call x1, Pallas kernels, update(): pl.pallas_call(update_kernel, out_shape=(out, out), in_specs=[VMEM] * 4,...  1.75 us
    pallas_call x1, Pallas kernels, load(): pl.pallas_call(load_kernel, out_shape=(grown, grown), in_specs=[HBM, HBM,...  1.56 us
    pallas_call x1, Pallas kernels, outer(): pl.pallas_call(outer_kernel, out_shape=(full, full, shape(2, 8, lanes), *...  1.22 us
    pallas_call x1, Pallas kernels, pack(): pl.pallas_call(pack_kernel, out_shape=(x_out, x_out, y_out, y_out), in_sp...  1.22 us
    ppermute x6, waiting for transfers between devices, swap(): return lax.ppermute(value, ('gx', 'gy'), pairs)  0.75 us
  transfers between devices with their start and end apart: 6, of which 2 were waited for; matrix products, arithmetic and copies ran while one was open for 0% of the time, Pallas kernels for 17%

profile of v6, /device:TPU:0, one launch (start us, length us, event | category | flops | bytes accessed | tf_op | source)
XLA Modules:
  0.0 31.8 jit_solution(3210259399577690043)
XLA Ops:
  0.6 1.2 %pack.1 = (f32[3,128,128]{2,1,0:T(8,128)S(1)}, f32[3,128,128]{2,1,0:T(8,128)S(1)}, f32[16,8,128]{2,1,0:T(8,128)S(1)}, f32[16,8,128]{2,1,0:T(8,128)S(1)}) custom-call(f32[16,128,128]{2,1,0:T(8,128)} %cond.3, f32[16,128,128]{2,1,0:T(8,128)} %resid.3), custom_call_target="tpu_custom_call" | custom-call | tf_op jit(solution)/shard_map/pack/pallas_call | solution.py:101
  1.9 3.0 %collective-permute-start.2 = (f32[3,128,128]{2,1,0:T(8,128)S(1)}, f32[3,128,128]{2,1,0:T(8,128)S(1)}, u32[]{:S(2)}, u32[]{:S(2)}) collective-permute-start(f32[3,128,128]{2,1,0:T(8,128)S(1)} %get-tuple-element.47), channel_id=1, source_target_pairs={{0,4},{1,5},{2,6},{3,7},{4,0},{5,1},{6,2},{7,3},{8,12},{9,13},{10,... | collective-permute-start | bytes 589832 | tf_op jit(solution)/shard_map/ppermute | solution.py:31
  4.9 0.0 collective-permute-start.3
  4.9 1.6 %collective-permute-start.1 = (f32[16,8,128]{2,1,0:T(8,128)S(1)}, f32[16,8,128]{2,1,0:T(8,128)S(1)}, u32[]{:S(2)}, u32[]{:S(2)}) collective-permute-start(f32[16,8,128]{2,1,0:T(8,128)S(1)} %get-tuple-element.37), channel_id=1, source_target_pairs={{0,3},{1,2},{2,1},{3,0},{4,7},{5,6},{6,5},{7,4},{8,11},{9,10},{10,... | collective-permute-start | bytes 196616 | tf_op jit(solution)/shard_map/ppermute | solution.py:31
  6.5 0.0 collective-permute-start
  6.5 1.6 %load.1 = (f32[16,160,128]{2,1,0:T(8,128)S(1)}, f32[16,160,128]{2,1,0:T(8,128)S(1)}) custom-call(f32[16,128,128]{2,1,0:T(8,128)} %cond.3, f32[16,128,128]{2,1,0:T(8,128)} %resid.3, f32[16,8,128]{2,1,0:T(8,128)S(1)} %get-tuple-element.34.after), custom_call_target="tpu_custom_call" | custom-call | flops 1000000000 | bytes 1048576 | tf_op jit(solution)/shard_map/load/pallas_call | solution.py:133
  8.1 0.6 %collective-permute-done.1.y_odd = f32[16,8,128]{2,1,0:T(8,128)S(1)} collective-permute-done((f32[16,8,128]{2,1,0:T(8,128)S(1)}, f32[16,8,128]{2,1,0:T(8,128)S(1)}, u32[]{:S(2)}, u32[]{:S(2)}) %collective-permute-start.1) | collective-permute-done | bytes 65568 | tf_op jit(solution)/shard_map/ppermute | solution.py:31
  8.6 0.0 collective-permute-done.y_even
  8.6 0.2 edge_terms.1
  8.8 3.7 %collective-permute-start.4 = (f32[136,128]{1,0:T(8,128)S(1)}, f32[136,128]{1,0:T(8,128)S(1)}, u32[]{:S(2)}, u32[]{:S(2)}) collective-permute-start(f32[136,128]{1,0:T(8,128)S(1)} %get-tuple-element.52), channel_id=1, source_target_pairs={{0,4},{1,5},{2,6},{3,7},{4,0},{5,1},{6,2},{7,3},{8,12},{9,13},{10,... | collective-permute-start | bytes 208904 | tf_op jit(solution)/shard_map/ppermute | solution.py:31
  12.5 0.0 collective-permute-start.5
  12.5 2.3 %inner.1 = (f32[16,160,128]{2,1,0:T(8,128)S(1)}, f32[16,160,128]{2,1,0:T(8,128)S(1)}, f32[16,128,128]{2,1,0:T(8,128)S(1)}, f32[16,128,128]{2,1,0:T(8,128)S(1)}, ...) custom-call(f32[16,160,128]{2,1,0:T(8,128)S(1)} %get-tuple-element.3, ...), custom_call_target="tpu_custom_call", output_to_operand_aliasing={{0}: (0, {}), {1}: (1, {})} | custom-call | flops 100000000 | bytes 1 | tf_op jit(solution)/shard_map/inner/pallas_call | solution.py:346
  14.8 0.0 collective-permute-done.2.x_even
  14.8 0.0 collective-permute-done.3.x_odd
  14.9 1.2 %outer.1 = (f32[16,128,128]{2,1,0:T(8,128)S(1)}, f32[16,128,128]{2,1,0:T(8,128)S(1)}, f32[2,8,128]{2,1,0:T(8,128)S(1)}, f32[2,2,160,128]{3,2,1,0:T(8,128)S(1)}, ...) custom-call(f32[16,160,128]{2,1,0:T(8,128)S(1)} %get-tuple-element.3, ...), custom_call_target="tpu_custom_call", output_to_operand_aliasing={{0}: (2, {}), {1}: (3, {})} | custom-call | tf_op jit(solution)/shard_map/outer/pallas_call | solution.py:591
  16.1 0.2 collective-permute-done.4.t_even
  16.2 0.0 collective-permute-done.5.t_odd
  16.2 0.4 %corners.1 = (f32[16,128,128]{2,1,0:T(8,128)S(1)}, f32[16,128,128]{2,1,0:T(8,128)S(1)}, f32[32,128]{1,0:T(8,128)S(1)}, f32[2,2,160,128]{3,2,1,0:T(8,128)S(1)}, f...) custom-call(f32[16,160,128]{2,1,0:T(8,128)S(1)} %get-tuple-element.3, ...), custom_call_target="tpu_custom_call", output_to_operand_aliasing={{0}: (2, {}), {1}: (3, {}), {3}: (12, {}), {4}: (13, {}), {... | custom-call | tf_op jit(solution)/shard_map/corners/pallas_call | solution.py:609
  16.7 13.3 %all_to_all.11 = f32[32,1,128]{2,1,0:T(1,128)S(1)} all-to-all(f32[32,1,128]{2,1,0:T(1,128)S(1)} %bitcast.5), channel_id=1, replica_groups=mesh['gx'=8,'gy'=4] {'gx','gy'}, dimensions={0} | all-to-all | bytes 32768 | tf_op jit(solution)/shard_map/all_to_all | solution.py:670
  30.0 1.8 %update.1 = (f32[16,128,128]{2,1,0:T(8,128)}, f32[16,128,128]{2,1,0:T(8,128)}) custom-call(f32[32,128]{1,0:T(8,128)S(1)} %bitcast.4, f32[16,128,128]{2,1,0:T(8,128)S(1)} %get-tuple-element.64.precond, f32[16,128,128]{2,1,0:T(8,128)S(1)} %get-tuple-element.65.image, f32[16,160,128]{2,1,0:T(8,128)S(1)} %get-tuple-element.39.b_r.resid), custom_call_target="tpu_custom_call" | custom-call | tf_op jit(solution)/shard_map/update/pallas_call | solution.py:646
Async XLA Ops:
  1.9 13.0 %collective-permute-start.2 = (f32[3,128,128]{2,1,0:T(8,128)S(1)}, f32[3,128,128]{2,1,0:T(8,128)S(1)}, u32[]{:S(2)}, u32[]{:S(2)}) collective-permute-start(f32[3,128,128]{2,1,0:T(8,128)S(1)} %get-tuple-element.47), channel_id=1, source_target_pairs={{0,4},{1,5},{2,6},{3,7},{4,0},{5,1},{6,2},{7,3},{8,12},{9,13},{10,... | collective-permute-start | bytes 589832 | tf_op jit(solution)/shard_map/ppermute | solution.py:31
  4.9 10.0 %collective-permute-start.3 = (f32[3,128,128]{2,1,0:T(8,128)S(1)}, f32[3,128,128]{2,1,0:T(8,128)S(1)}, u32[]{:S(2)}, u32[]{:S(2)}) collective-permute-start(f32[3,128,128]{2,1,0:T(8,128)S(1)} %get-tuple-element.48), channel_id=1, source_target_pairs={{0,1},{1,0},{2,3},{3,2},{4,8},{5,9},{6,10},{7,11},{8,4},{9,5},{10,... | collective-permute-start | bytes 589832 | tf_op jit(solution)/shard_map/ppermute | solution.py:31
  4.9 3.7 %collective-permute-start.1 = (f32[16,8,128]{2,1,0:T(8,128)S(1)}, f32[16,8,128]{2,1,0:T(8,128)S(1)}, u32[]{:S(2)}, u32[]{:S(2)}) collective-permute-start(f32[16,8,128]{2,1,0:T(8,128)S(1)} %get-tuple-element.37), channel_id=1, source_target_pairs={{0,3},{1,2},{2,1},{3,0},{4,7},{5,6},{6,5},{7,4},{8,11},{9,10},{10,... | collective-permute-start | bytes 196616 | tf_op jit(solution)/shard_map/ppermute | solution.py:31
  6.5 2.1 %collective-permute-start = (f32[16,8,128]{2,1,0:T(8,128)S(1)}, f32[16,8,128]{2,1,0:T(8,128)S(1)}, u32[]{:S(2)}, u32[]{:S(2)}) collective-permute-start(f32[16,8,128]{2,1,0:T(8,128)S(1)} %get-tuple-element.34.after), channel_id=1, source_target_pairs={{0,1},{1,0},{2,3},{3,2},{4,5},{5,4},{6,7},{7,6},{8,9},{9,8},{10,11... | collective-permute-start | bytes 196616 | tf_op jit(solution)/shard_map/ppermute | solution.py:31
  8.8 7.4 %collective-permute-start.4 = (f32[136,128]{1,0:T(8,128)S(1)}, f32[136,128]{1,0:T(8,128)S(1)}, u32[]{:S(2)}, u32[]{:S(2)}) collective-permute-start(f32[136,128]{1,0:T(8,128)S(1)} %get-tuple-element.52), channel_id=1, source_target_pairs={{0,4},{1,5},{2,6},{3,7},{4,0},{5,1},{6,2},{7,3},{8,12},{9,13},{10,... | collective-permute-start | bytes 208904 | tf_op jit(solution)/shard_map/ppermute | solution.py:31
  12.5 3.7 %collective-permute-start.5 = (f32[136,128]{1,0:T(8,128)S(1)}, f32[136,128]{1,0:T(8,128)S(1)}, u32[]{:S(2)}, u32[]{:S(2)}) collective-permute-start(f32[136,128]{1,0:T(8,128)S(1)} %get-tuple-element.53), channel_id=1, source_target_pairs={{0,1},{1,0},{2,3},{3,2},{4,8},{5,9},{6,10},{7,11},{8,4},{9,5},{10,... | collective-permute-start | bytes 208904 | tf_op jit(solution)/shard_map/ppermute | solution.py:31

commit v7 on v6

--- a/solution.py
+++ b/solution.py
@@ -162,58 +162,6 @@
     return south, north
 
 
-def edge_kernel(u, r, y_even, y_odd, t_even, t_odd, grown):
-    layers, rows = u.shape[0], u.shape[1] - 4 * HALO
-    odd = place("gx")[0]
-    end = HALO + rows
-    own = slice(LOW, LOW + rows)
-    sends = []
-    for side in range(2):
-        edge, mid, far = ((0, 1, 2), (layers - 1, layers - 2, layers - 3))[side]
-        south, north = y_tiles(y_even, y_odd, mid, 0)
-        middle = u[mid, own]
-        grown[side, 0:HALO] = south
-        grown[side, HALO:end] = middle
-        grown[side, end : end + HALO] = north
-        total = 6.0 * middle + u[edge, own] + u[far, own] + z_sum(middle)
-        total = total + grown[side, HALO - 1 : end - 1] + grown[side, HALO + 1 : end + 1]
-        term = (u[edge, own] + middle) * (2.0 * r[mid, own] / total)
-        edge_south, edge_north = y_tiles(y_even, y_odd, edge, 0)
-        r_south, r_north = y_tiles(y_even, y_odd, edge, 1)
-        corner = jnp.concatenate(
-            [
-                edge_south[HALO - 1 : HALO],
-                edge_south[HALO - 2 : HALO - 1],
-                south[HALO - 1 : HALO],
-                r_south[HALO - 1 : HALO],
-                edge_north[0:1],
-                edge_north[1:2],
-                north[0:1],
-                r_north[0:1],
-            ],
-            axis=0,
-        )
-        sends.append((term, corner))
-    (t_low, c_low), (t_high, c_high) = sends
-    t_even[0:rows] = jnp.where(odd, t_low, t_high)
-    t_even[rows : rows + 8] = jnp.where(odd, c_low, c_high)
-    t_odd[0:rows] = jnp.where(odd, t_high, t_low)
-    t_odd[rows : rows + 8] = jnp.where(odd, c_high, c_low)
-
-
-def edge_terms(u, r, y_even, y_odd):
-    rows, lanes = u.shape[1] - 4 * HALO, u.shape[2]
-    return pl.pallas_call(
-        edge_kernel,
-        out_shape=(shape(rows + 8, lanes), shape(rows + 8, lanes)),
-        in_specs=[VMEM] * 4,
-        out_specs=(VMEM, VMEM),
-        scratch_shapes=[pltpu.VMEM((2, rows + 2 * HALO, lanes), F32)],
-        compiler_params=params(2),
-        name="edge_terms",
-    )(u, r, y_even, y_odd)
-
-
 def row_chunks(rows):
     total = rows + 2 * HALO
     step = total // 3 if total % 24 == 0 else total
@@ -245,28 +193,19 @@
     return jnp.sum(value.reshape(value.shape[0] // 8, 8, value.shape[1]), axis=0)
 
 
-def inner_kernel(
-    u_in, r_in, y_even, y_odd,
-    u, r, p_out, i_out, e_v, e_i, e_d, e_p, sums,
-    inv, v, w, d, p, q, masks,
+def fields_kernel(
+    u_in, r_in, y_even, y_odd, u, r, inv, v, w, d, masks, t_even, t_odd
 ):
-    layers, rows = p_out.shape[0], p_out.shape[1]
+    layers, rows = u.shape[0], u.shape[1] - 4 * HALO
     fill_rows(masks, rows)
-
-    def halo(k, carry):
+    for k in range(layers):
         for part, target in enumerate((u, r)):
             south, north = y_tiles(y_even, y_odd, k, part)
             target[k, HALO:LOW] = south
             target[k, LOW + rows : LOW + rows + HALO] = north
-        return carry
-
-    lax.fori_loop(0, layers, halo, 0, unroll=16)
-    chunks = row_chunks(rows)
-
-    def first(k, carry):
-        for start, size in chunks:
-            here = slice(start, start + size)
-            down, up = slice(start - 1, start + size - 1), slice(start + 1, start + size + 1)
+    for k in range(1, layers - 1):
+        for start, size in row_chunks(rows):
+            here, down, up = around_rows(start, size)
             mid = u[k, here]
             total = 6.0 * mid + u[k - 1, here] + u[k + 1, here]
             total = total + u[k, down] + u[k, up] + z_sum(mid)
@@ -278,14 +217,52 @@
             inv[k, here] = inverse
             v[k, here] = value
             w[k, here] = mid * value
-        return carry
-
-    lax.fori_loop(1, layers - 1, first, 0, unroll=14)
-
-    def second(k, carry):
-        for start, size in chunks:
-            here = slice(start, start + size)
-            down, up = slice(start - 1, start + size - 1), slice(start + 1, start + size + 1)
+    odd = place("gx")[0]
+    own, north = slice(LOW, LOW + rows), LOW + rows
+    sends = []
+    for side in range(2):
+        edge, mid = ((0, 1), (layers - 1, layers - 2))[side]
+        lines = (
+            u[edge, LOW - 1 : LOW],
+            u[edge, LOW - 2 : LOW - 1],
+            u[mid, LOW - 1 : LOW],
+            r[edge, LOW - 1 : LOW],
+            u[edge, north : north + 1],
+            u[edge, north + 1 : north + 2],
+            u[mid, north : north + 1],
+            r[edge, north : north + 1],
+        )
+        term = (u[edge, own] + u[mid, own]) * v[mid, own]
+        sends.append((term, jnp.concatenate(lines, axis=0)))
+    (t_low, c_low), (t_high, c_high) = sends
+    t_even[0:rows] = jnp.where(odd, t_low, t_high)
+    t_even[rows : rows + 8] = jnp.where(odd, c_low, c_high)
+    t_odd[0:rows] = jnp.where(odd, t_high, t_low)
+    t_odd[rows : rows + 8] = jnp.where(odd, c_high, c_low)
+
+
+def fields(u, r, y_even, y_odd):
+    layers, grown, lanes = u.shape
+    ext, term = shape(*u.shape), shape(grown - 4 * HALO + 8, lanes)
+    outs = (ext,) * 6 + (shape(4, grown, lanes), term, term)
+    return pl.pallas_call(
+        fields_kernel,
+        out_shape=outs,
+        in_specs=[VMEM] * 4,
+        out_specs=(VMEM,) * len(outs),
+        input_output_aliases={0: 0, 1: 1},
+        compiler_params=params(4),
+        name="fields",
+    )(u, r, y_even, y_odd)
+
+
+def inner_kernel(
+    u, r, inv, v, w, d, masks, p_out, i_out, p, sums, ready, scales, partial, q
+):
+    layers, rows = p_out.shape[0], p_out.shape[1]
+    for k in range(2, layers - 2):
+        for start, size in row_chunks(rows):
+            here, down, up = around_rows(start, size)
             mid = u[k, here]
             total = 2.0 * r[k, here]
             total = total + mid * (v[k - 1, here] + v[k + 1, here] + z_sum(v[k, here]))
@@ -299,15 +276,10 @@
                 value = masks[1, here] * inv[k, here] * total
             p[k, here] = value
             q[k, here] = mid * value
-        return carry
-
-    lax.fori_loop(2, layers - 2, second, 0, unroll=12)
-
-    def third(k, carry):
-        rz, pq = carry
+    rz = pq = jnp.zeros((8, u.shape[2]), F32)
+    for k in range(3, layers - 3):
         for start, size in own_chunks(rows):
-            here = slice(start, start + size)
-            down, up = slice(start - 1, start + size - 1), slice(start + 1, start + size + 1)
+            here, down, up = around_rows(start, size)
             mid = p[k, here]
             around = p[k - 1, here] + p[k + 1, here] + p[k, down] + p[k, up] + z_sum(mid)
             scaled = q[k - 1, here] + q[k + 1, here] + q[k, down] + q[k, up]
@@ -317,43 +289,56 @@
             p_out[k, start - LOW : start - LOW + size] = mid
             rz = rz + eight(r[k, here] * mid)
             pq = pq + eight(mid * image)
-        return rz, pq
-
-    zero = jnp.zeros((8, u.shape[2]), F32)
-    rz, pq = lax.fori_loop(3, layers - 3, third, (zero, zero), unroll=10)
+    for side in range(2):
+        at = side_layers(layers, side)
+        twice = side_place(side)[1]
+        for start, size in row_chunks(rows):
+            here, down, up = around_rows(start, size)
+            mid, value, scale = u[at[1], here], v[at[1], here], twice * inv[at[1], here]
+            total = 2.0 * r[at[1], here] + mid * z_sum(value) + z_sum(w[at[1], here])
+            total = total + (mid + u[at[2], here]) * v[at[2], here] / twice
+            south = mid * v[at[1], down] + w[at[1], down]
+            north = mid * v[at[1], up] + w[at[1], up]
+            if is_plain(start, size, rows):
+                total = total + south + north
+            else:
+                total = total + masks[2, here] * south + masks[3, here] * north
+                scale = scale * masks[1, here]
+            ready[side, here] = total
+            scales[side, here] = scale
+            edge = u[at[0], here]
+            total = 6.0 * edge + mid + u[at[0], down] + u[at[0], up] + z_sum(edge)
+            partial[side, here] = total
+        for start, size in own_chunks(rows):
+            here, down, up = around_rows(start, size)
+            mid = p[at[2], here]
+            around = p[at[3], here] + p[at[2], down] + p[at[2], up] + z_sum(mid)
+            scaled = q[at[3], here] + q[at[2], down] + q[at[2], up] + z_sum(q[at[2], here])
+            image = d[at[2], here] * mid - u[at[2], here] * around - scaled
+            i_out[at[2], start - LOW : start - LOW + size] = image
+            p_out[at[2], start - LOW : start - LOW + size] = mid
+            rz = rz + eight(r[at[2], here] * mid)
     sums[0] = rz
     sums[1] = pq
-    full = slice(HALO, LOW + rows + HALO)
-    for side in range(2):
-        order = (0, 1, 2, 3) if side == 0 else tuple(layers - 1 - k for k in range(4))
-        for k in range(2):
-            e_v[side, k, full] = v[order[k + 1], full]
-            e_d[side, k, full] = d[order[k + 1], full]
-            e_p[side, k, full] = p[order[k + 2], full]
-        e_i[side, 0, full] = inv[order[1], full]
-
-
-def inner(u, r, y_even, y_odd):
-    layers, grown, lanes = u.shape
-    rows = grown - 4 * HALO
-    field = pltpu.VMEM((layers, grown, lanes), F32)
-
-    def edge(count):
-        return shape(2, count, grown, lanes)
-
-    own, ext = shape(layers, rows, lanes), shape(layers, grown, lanes)
-    outs = (ext, ext, own, own, edge(2), edge(1), edge(2), edge(2), shape(2, 8, lanes))
+
+
+def inner(*found):
+    layers, grown, lanes = found[0].shape
+    own = shape(layers, grown - 4 * HALO, lanes)
+    face = shape(2, grown, lanes)
+    outs = (own, own, shape(layers, grown, lanes), shape(2, 8, lanes), face, face, face)
     return pl.pallas_call(
         inner_kernel,
         out_shape=outs,
-        in_specs=[VMEM] * 4,
+        in_specs=[VMEM] * 7,
         out_specs=(VMEM,) * len(outs),
-        scratch_shapes=[field] * 6 + [pltpu.VMEM((4, grown, lanes), F32)],
-        input_output_aliases={0: 0, 1: 1},
-        compiler_params=params(12),
-        cost_estimate=pl.CostEstimate(flops=100_000_000, transcendentals=0, bytes_accessed=1),
+        scratch_shapes=[pltpu.VMEM((layers, grown, lanes), F32)],
+        compiler_params=params(4),
+        cost_estimate=pl.CostEstimate(
+            flops=100_000_000, transcendentals=0, bytes_accessed=1
+        ),
         name="inner",
-    )(u, r, y_even, y_odd)
+    )(*found)
 
 
 def around_rows(start, size):
@@ -380,7 +365,7 @@
 
 
 def start_fields(own, near, side, chunk):
-    b_u, b_r = own[:2]
+    b_u, b_r, partial = own[0], own[1], own[-1]
     u, r, v, w, _, _, d, inv, masks = near
     at = side_layers(b_u.shape[0], side)
     has = side_place(side)[0]
@@ -394,8 +379,7 @@
     inv[side, 0, here] = inverse
     v[side, 0, here] = value
     w[side, 0, here] = mid * value
-    total = 6.0 * edge + mid + b_u[at[1], here]
-    total = total + b_u[at[0], down] + b_u[at[0], up] + z_sum(edge)
+    total = partial[side, here] + mid
     inverse = inside / jnp.maximum(total, TINY)
     value = 2.0 * b_r[at[0], here] * inverse
     d[side, here] = total
@@ -405,7 +389,7 @@
 
 
 def precond_fields(own, near, side, chunk, rows, term):
-    b_u, b_r, e_v, e_i = own[:4]
+    b_u, b_r, e_v, _, _, _, ready, scales, _ = own
     u, r, v, w, p, q, _, inv, masks = near
     at = side_layers(b_u.shape[0], side)
     twice = side_place(side)[1]
@@ -435,7 +419,7 @@
     inv[side, 0, here] = finish(mid, total, south, north, inv[side, 0, here], 0)
 
     mid, next_u = b_u[at[0], here], b_u[at[1], here]
-    next_v = e_v[side, 0, here]
+    next_v = e_v[at[1], here]
     total = 2.0 * b_r[at[0], here]
     total = total + mid * (v[side, 0, here] + next_v + z_sum(v[side, 1, here]))
     total = total + w[side, 0, here] + next_u * next_v + z_sum(w[side, 1, here])
@@ -443,44 +427,30 @@
     north = mid * v[side, 1, up] + w[side, 1, up]
     finish(mid, total, south, north, inv[side, 1, here], 1)
 
-    inner_v = e_v[side, 1, here]
-    total = 2.0 * b_r[at[1], here]
-    total = total + next_u * (v[side, 1, here] + z_sum(next_v))
-    total = total + w[side, 1, here] + z_sum(next_u * next_v)
-    total = total + (next_u + b_u[at[2], here]) * inner_v / twice
-    south = (next_u + b_u[at[1], down]) * e_v[side, 0, down]
-    north = (next_u + b_u[at[1], up]) * e_v[side, 0, up]
-    finish(next_u, total, south, north, e_i[side, 0, here], 2)
+    total = ready[side, here] + next_u * v[side, 1, here] + w[side, 1, here]
+    value = scales[side, here] * total
+    p[side, 2, here] = value
+    q[side, 2, here] = next_u * value
 
 
 def image_fields(own, near, side, chunk, k, p_out, i_out):
-    b_u, b_r, _, _, e_d, e_p = own
+    b_u, b_r, _, _, e_d, e_p = own[:6]
     _, _, _, _, p, q, d, _, _ = near
     at = side_layers(b_u.shape[0], side)
     here, down, up = around_rows(*chunk)
     mid_u = b_u[at[k], here]
-    if k < 2:
-        mid, mid_q = p[side, k + 1, here], q[side, k + 1, here]
-        near_y = p[side, k + 1, down] + p[side, k + 1, up]
-        near_q = q[side, k + 1, down] + q[side, k + 1, up]
-        before_p, before_q = p[side, k, here], q[side, k, here]
-        if k == 0:
-            after_p, after_q = p[side, 2, here], q[side, 2, here]
-        else:
-            after_p = e_p[side, 0, here]
-            after_q = b_u[at[2], here] * after_p
+    mid, mid_q = p[side, k + 1, here], q[side, k + 1, here]
+    near_y = p[side, k + 1, down] + p[side, k + 1, up]
+    near_q = q[side, k + 1, down] + q[side, k + 1, up]
+    before_p, before_q = p[side, k, here], q[side, k, here]
+    if k == 0:
+        after_p, after_q = p[side, 2, here], q[side, 2, here]
     else:
-        mid = e_p[side, 0, here]
-        mid_q = mid_u * mid
-        low_p, high_p = e_p[side, 0, down], e_p[side, 0, up]
-        near_y = low_p + high_p
-        near_q = b_u[at[2], down] * low_p + b_u[at[2], up] * high_p
-        before_p, before_q = p[side, 2, here], q[side, 2, here]
-        after_p = e_p[side, 1, here]
-        after_q = b_u[at[3], here] * after_p
+        after_p = e_p[at[2], here]
+        after_q = b_u[at[2], here] * after_p
     around = before_p + after_p + near_y + z_sum(mid)
     scaled = before_q + after_q + near_q + z_sum(mid_q)
-    total = d[side, here] if k == 0 else e_d[side, k - 1, here]
+    total = d[side, here] if k == 0 else e_d[at[k], here]
     image = total * mid - mid_u * around - scaled
     out = slice(chunk[0] - LOW, chunk[0] - LOW + chunk[1])
     p_out[at[k], out] = mid
@@ -495,22 +465,24 @@
 
 
 def outer_kernel(
-    b_u, b_r, p_in, i_in, e_v, e_i, e_d, e_p, sums, x_even, x_odd,
+    b_u, b_r, p_in, i_in, e_v, e_i, e_d, e_p, ready, scales, partial, sums, masks,
+    x_even, x_odd,
     p_out, i_out, sums_out, *near,
 ):
     rows = p_in.shape[1]
-    u, r, masks = near[0], near[1], near[-1]
-    fill_rows(masks, rows)
-    own = (b_u, b_r, e_v, e_i, e_d, e_p)
-    here = slice(LOW, LOW + rows)
+    near = (*near, masks)
+    u, r = near[0], near[1]
+    own = (b_u, b_r, e_v, e_i, e_d, e_p, ready, scales, partial)
+    whole = slice(LOW, LOW + rows)
     rz, pq = sums[0], sums[1]
     zero = jnp.zeros(rz.shape, F32)
     for side in range(2):
+        at = side_layers(b_u.shape[0], side)
         arrived = side_place(side)[2]
         for slot in range(2):
             layer = slot if side == 0 else 1 - slot
-            u[side, slot, here] = arrived(x_even[layer], x_odd[layer])
-        r[side, here] = arrived(x_even[2], x_odd[2])
+            u[side, slot, whole] = arrived(x_even[layer], x_odd[layer])
+        r[side, whole] = arrived(x_even[2], x_odd[2])
         for rest in (slice(HALO, LOW), slice(LOW + rows, LOW + rows + HALO)):
             u[side, 0, rest] = zero
             u[side, 1, rest] = zero
@@ -519,9 +491,12 @@
             start_fields(own, near, side, chunk)
         for chunk in row_chunks(rows):
             precond_fields(own, near, side, chunk, rows, None)
-        for chunk in own_chunks(rows):
-            add_rz, add_pq = image_fields(own, near, side, chunk, 2, p_out, i_out)
-            rz, pq = rz + add_rz, pq + add_pq
+        for start, size in own_chunks(rows):
+            here, out = slice(start, start + size), slice(start - LOW, start - LOW + size)
+            change = (b_u[at[2], here] + b_u[at[1], here]) * near[4][side, 2, here]
+            image = i_in[at[2], out] - change
+            i_out[at[2], out] = image
+            pq = pq + eight(e_p[at[2], here] * image)
         for chunk in middle_chunks(rows):
             add_rz, add_pq = image_fields(own, near, side, chunk, 1, p_out, i_out)
             rz, pq = rz + add_rz, pq + add_pq
@@ -531,13 +506,14 @@
 
 
 def corner_kernel(
-    b_u, b_r, p_in, i_in, e_v, e_i, e_d, e_p, sums, t_even, t_odd, masks, *refs,
+    b_u, b_r, p_in, i_in, e_v, e_i, e_d, e_p, ready, scales, partial, sums, t_even, t_odd,
+    masks, *refs,
 ):
     old, (p_out, i_out, total_out), fields = refs[:8], refs[8:11], refs[11:]
     near = (*fields, masks)
     rows = p_in.shape[1]
     u, r, p, inv = near[0], near[1], near[4], near[7]
-    own = (b_u, b_r, e_v, e_i, e_d, e_p)
+    own = (b_u, b_r, e_v, e_i, e_d, e_p, ready, scales, partial)
     rz, pq = sums[0], sums[1]
     zero = jnp.zeros(rz.shape, F32)
     row = lax.broadcasted_iota(jnp.int32, zero.shape, 0)
@@ -582,39 +558,39 @@
     total_out[...] = jnp.where(lane < total_out.shape[1] // 2, rz, pq)
 
 
-def outer(found, x_even, x_odd):
+def outer(found, masks, x_even, x_odd):
     layers, rows, lanes = found[2].shape
     grown = rows + 4 * HALO
     full = shape(layers, rows, lanes)
-    sizes = ((2, 2), (2,), (2, 2), (2, 2), (2, 3), (2, 3), (2,), (2, 2), (4,))
+    sizes = ((2, 2), (2,), (2, 2), (2, 2), (2, 3), (2, 3), (2,), (2, 2))
     near = tuple(shape(*size, grown, lanes) for size in sizes)
     return pl.pallas_call(
         outer_kernel,
         out_shape=(full, full, shape(2, 8, lanes), *near),
-        in_specs=[VMEM] * 11,
+        in_specs=[VMEM] * 15,
         out_specs=(VMEM,) * (3 + len(near)),
         input_output_aliases={2: 0, 3: 1},
         compiler_params=params(4),
         name="outer",
-    )(*found, x_even, x_odd)
-
-
-def corners(found, first, t_even, t_odd):
+    )(*found, masks, x_even, x_odd)
+
+
+def corners(found, first, masks, t_even, t_odd):
     layers, rows, lanes = found[2].shape
     parts = lax.axis_size("gx") * lax.axis_size("gy")
-    p, i, sums, *near, masks = first
-    u, r, _, _, e_v, e_i, e_d, e_p, _ = found
+    p, i, sums, *near = first
+    u, r, _, _, *inside, _ = found
     full = shape(layers, rows, lanes)
-    fields = tuple(shape(*field.shape) for field in near)
+    again = tuple(shape(*field.shape) for field in near)
     return pl.pallas_call(
         corner_kernel,
-        out_shape=(full, full, shape(parts, lanes), *fields),
-        in_specs=[VMEM] * (12 + len(near)),
+        out_shape=(full, full, shape(parts, lanes), *again),
+        in_specs=[VMEM] * (15 + len(near)),
         out_specs=(VMEM,) * (3 + len(near)),
-        input_output_aliases={2: 0, 3: 1, **{12 + k: 3 + k for k in range(len(near))}},
+        input_output_aliases={2: 0, 3: 1, **{15 + k: 3 + k for k in range(len(near))}},
         compiler_params=params(4),
         name="corners",
-    )(u, r, p, i, e_v, e_i, e_d, e_p, sums, t_even, t_odd, masks, *near)[:3]
+    )(u, r, p, i, *inside, sums, t_even, t_odd, masks, *near)[:3]
 
 
 def update_kernel(sums, precond, image, resid, pressure, residual, held, sem):
@@ -662,13 +638,15 @@
     u, r = load(conductivity, right_side, y_even)
     y_even, y_odd = swap_y(y_even, 0), swap_y(y_odd, 1)
     x_even, x_odd = swap_x(x_even, 0), swap_x(x_odd, 1)
-    t_even, t_odd = edge_terms(u, r, y_even, y_odd)
+    *found, t_even, t_odd = fields(u, r, y_even, y_odd)
     t_even, t_odd = swap_x(t_even, 0), swap_x(t_odd, 1)
-    found = inner(u, r, y_even, y_odd)
-    first = outer(found, x_even, x_odd)
-    precond, image, sums = corners(found, first, t_even, t_odd)
+    u, r, inv, v, _, d, masks = found
+    p_inner, i_inner, p, sums, *faces = inner(*found)
+    found = (u, r, p_inner, i_inner, v, inv, d, p, *faces, sums)
+    first = outer(found, masks, x_even, x_odd)
+    precond, image, sums = corners(found, first, masks, t_even, t_odd)
     sums = lax.all_to_all(sums, ("gx", "gy"), 0, 0, tiled=True)
-    return update(sums, precond, image, found[1])
+    return update(sums, precond, image, r)
 
 
 def solution(mesh):

time: 31.9 us -> 31.5 us (0.987)
  blocking collectives: 13.3 us -> 12.9 us
    pallas_call x2, Pallas kernels: 2.47 us -> 2.91 us  [the longest x1 2.27 us: inner(): pl.pallas_call(inner_kernel, out_shape=outs, in_specs=[VMEM] * 7, out_spe...]
    all_to_all x1, blocking collectives: 13.3 us -> 12.9 us  [on_device(): sums = lax.all_to_all(sums, ('gx', 'gy'), 0, 0, tiled=True)]
    pallas_call x1, Pallas kernels: 1.22 us -> 0.88 us  [outer(): pl.pallas_call(outer_kernel, out_shape=(full, full, shape(2, 8, lanes), *...]
where the time goes in v7:
time: 31.5 us; the launch traced here: 31.3 us
  blocking collectives  12.9 us (41%)
  Pallas kernels  8.66 us (27%)
  starting transfers between devices  8.35 us (27%)
  waiting for transfers between devices  0.75 us (2%)
  between operations  0.69 us (2%)
    all_to_all x1, blocking collectives, on_device(): sums = lax.all_to_all(sums, ('gx', 'gy'), 0, 0, tiled=True)  12.9 us
    ppermute x6, starting transfers between devices, swap(): return lax.ppermute(value, ('gx', 'gy'), pairs)  8.35 us
    pallas_call x1, Pallas kernels, inner(): pl.pallas_call(inner_kernel, out_shape=outs, in_specs=[VMEM] * 7, out_spe...  2.27 us
    pallas_call x1, Pallas kernels, update(): pl.pallas_call(update_kernel, out_shape=(out, out), in_specs=[VMEM] * 4,...  1.75 us
    pallas_call x1, Pallas kernels, load(): pl.pallas_call(load_kernel, out_shape=(grown, grown), in_specs=[HBM, HBM,...  1.56 us
    pallas_call x1, Pallas kernels, pack(): pl.pallas_call(pack_kernel, out_shape=(x_out, x_out, y_out, y_out), in_sp...  1.22 us
    pallas_call x1, Pallas kernels, outer(): pl.pallas_call(outer_kernel, out_shape=(full, full, shape(2, 8, lanes), *...  0.88 us
    ppermute x6, waiting for transfers between devices, swap(): return lax.ppermute(value, ('gx', 'gy'), pairs)  0.75 us
  transfers between devices with their start and end apart: 6, of which 2 were waited for; matrix products, arithmetic and copies ran while one was open for 0% of the time, Pallas kernels for 17%

profile of v7, /device:TPU:0, one launch (start us, length us, event | category | flops | bytes accessed | tf_op | source)
XLA Modules:
  0.0 31.3 jit_solution(15946156840802034561)
XLA Ops:
  0.6 1.2 %pack.1 = (f32[3,128,128]{2,1,0:T(8,128)S(1)}, f32[3,128,128]{2,1,0:T(8,128)S(1)}, f32[16,8,128]{2,1,0:T(8,128)S(1)}, f32[16,8,128]{2,1,0:T(8,128)S(1)}) custom-call(f32[16,128,128]{2,1,0:T(8,128)} %cond.3, f32[16,128,128]{2,1,0:T(8,128)} %resid.3), custom_call_target="tpu_custom_call" | custom-call | tf_op jit(solution)/shard_map/pack/pallas_call | solution.py:101
  1.9 3.0 %collective-permute-start.2 = (f32[3,128,128]{2,1,0:T(8,128)S(1)}, f32[3,128,128]{2,1,0:T(8,128)S(1)}, u32[]{:S(2)}, u32[]{:S(2)}) collective-permute-start(f32[3,128,128]{2,1,0:T(8,128)S(1)} %get-tuple-element.56), channel_id=1, source_target_pairs={{0,4},{1,5},{2,6},{3,7},{4,0},{5,1},{6,2},{7,3},{8,12},{9,13},{10,... | collective-permute-start | bytes 589832 | tf_op jit(solution)/shard_map/ppermute | solution.py:31
  4.9 0.0 collective-permute-start.3
  4.9 1.6 %collective-permute-start.1 = (f32[16,8,128]{2,1,0:T(8,128)S(1)}, f32[16,8,128]{2,1,0:T(8,128)S(1)}, u32[]{:S(2)}, u32[]{:S(2)}) collective-permute-start(f32[16,8,128]{2,1,0:T(8,128)S(1)} %get-tuple-element.41), channel_id=1, source_target_pairs={{0,3},{1,2},{2,1},{3,0},{4,7},{5,6},{6,5},{7,4},{8,11},{9,10},{10,... | collective-permute-start | bytes 196616 | tf_op jit(solution)/shard_map/ppermute | solution.py:31
  6.5 0.0 collective-permute-start
  6.5 1.6 %load.1 = (f32[16,160,128]{2,1,0:T(8,128)S(1)}, f32[16,160,128]{2,1,0:T(8,128)S(1)}) custom-call(f32[16,128,128]{2,1,0:T(8,128)} %cond.3, f32[16,128,128]{2,1,0:T(8,128)} %resid.3, f32[16,8,128]{2,1,0:T(8,128)S(1)} %get-tuple-element.38.after), custom_call_target="tpu_custom_call" | custom-call | flops 1000000000 | bytes 1048576 | tf_op jit(solution)/shard_map/load/pallas_call | solution.py:133
  8.1 0.6 %collective-permute-done.1.y_odd = f32[16,8,128]{2,1,0:T(8,128)S(1)} collective-permute-done((f32[16,8,128]{2,1,0:T(8,128)S(1)}, f32[16,8,128]{2,1,0:T(8,128)S(1)}, u32[]{:S(2)}, u32[]{:S(2)}) %collective-permute-start.1) | collective-permute-done | bytes 65568 | tf_op jit(solution)/shard_map/ppermute | solution.py:31
  8.6 0.0 collective-permute-done.y_even
  8.6 0.6 %fields.1 = (f32[16,160,128]{2,1,0:T(8,128)S(1)}, f32[16,160,128]{2,1,0:T(8,128)S(1)}, f32[16,160,128]{2,1,0:T(8,128)S(1)}, f32[16,160,128]{2,1,0:T(8,128)S(1)},...) custom-call(f32[16,160,128]{2,1,0:T(8,128)S(1)} %get-tuple-element.3, ...), custom_call_target="tpu_custom_call", output_to_operand_aliasing={{0}: (0, {}), {1}: (1, {})} | custom-call | tf_op jit(solution)/shard_map/fields/pallas_call | solution.py:248
  9.3 3.7 %collective-permute-start.4 = (f32[136,128]{1,0:T(8,128)S(1)}, f32[136,128]{1,0:T(8,128)S(1)}, u32[]{:S(2)}, u32[]{:S(2)}) collective-permute-start(f32[136,128]{1,0:T(8,128)S(1)} %get-tuple-element.61), channel_id=1, source_target_pairs={{0,4},{1,5},{2,6},{3,7},{4,0},{5,1},{6,2},{7,3},{8,12},{9,13},{10,... | collective-permute-start | bytes 208904 | tf_op jit(solution)/shard_map/ppermute | solution.py:31
  13.0 0.0 collective-permute-start.5
  13.0 2.3 %inner.1 = (f32[16,128,128]{2,1,0:T(8,128)S(1)}, f32[16,128,128]{2,1,0:T(8,128)S(1)}, f32[16,160,128]{2,1,0:T(8,128)S(1)}, f32[2,8,128]{2,1,0:T(8,128)S(1)}, f32...) custom-call(f32[16,160,128]{2,1,0:T(8,128)S(1)} %get-tuple-element.42.u.b_u, ...), custom_call_target="tpu_custom_call" | custom-call | flops 100000000 | bytes 1 | tf_op jit(solution)/shard_map/inner/pallas_call | solution.py:330
  15.3 0.0 collective-permute-done.2.x_even
  15.3 0.0 collective-permute-done.3.x_odd
  15.3 0.9 %outer.1 = (f32[16,128,128]{2,1,0:T(8,128)S(1)}, f32[16,128,128]{2,1,0:T(8,128)S(1)}, f32[2,8,128]{2,1,0:T(8,128)S(1)}, f32[2,2,160,128]{3,2,1,0:T(8,128)S(1)}, ...) custom-call(f32[16,160,128]{2,1,0:T(8,128)S(1)} %get-tuple-element.4, ...), custom_call_target="tpu_custom_call", output_to_operand_aliasing={{0}: (2, {}), {1}: (3, {})} | custom-call | tf_op jit(solution)/shard_map/outer/pallas_call | solution.py:567
  16.2 0.2 collective-permute-done.4.t_even
  16.3 0.0 collective-permute-done.5.t_odd
  16.3 0.4 %corners.1 = (f32[16,128,128]{2,1,0:T(8,128)S(1)}, f32[16,128,128]{2,1,0:T(8,128)S(1)}, f32[32,128]{1,0:T(8,128)S(1)}, f32[2,2,160,128]{3,2,1,0:T(8,128)S(1)}, f...) custom-call(f32[16,160,128]{2,1,0:T(8,128)S(1)} %get-tuple-element.4, ...), custom_call_target="tpu_custom_call", output_to_operand_aliasing={{0}: (2, {}), {1}: (3, {}), {3}: (15, {}), {4}: (16, {}), {... | custom-call | tf_op jit(solution)/shard_map/corners/pallas_call | solution.py:585
  16.7 12.9 %all_to_all.11 = f32[32,1,128]{2,1,0:T(1,128)S(1)} all-to-all(f32[32,1,128]{2,1,0:T(1,128)S(1)} %bitcast.5), channel_id=1, replica_groups=mesh['gx'=8,'gy'=4] {'gx','gy'}, dimensions={0} | all-to-all | bytes 32768 | tf_op jit(solution)/shard_map/all_to_all | solution.py:648
  29.6 1.7 %update.1 = (f32[16,128,128]{2,1,0:T(8,128)}, f32[16,128,128]{2,1,0:T(8,128)}) custom-call(f32[32,128]{1,0:T(8,128)S(1)} %bitcast.4, f32[16,128,128]{2,1,0:T(8,128)S(1)} %get-tuple-element.72.precond, f32[16,128,128]{2,1,0:T(8,128)S(1)} %get-tuple-element.73.image, f32[16,160,128]{2,1,0:T(8,128)S(1)} %get-tuple-element.43.r.b_r.resid), custom_call_target="tpu_custom_call" | custom-call | tf_op jit(solution)/shard_map/update/pallas_call | solution.py:622
Async XLA Ops:
  1.9 13.4 %collective-permute-start.2 = (f32[3,128,128]{2,1,0:T(8,128)S(1)}, f32[3,128,128]{2,1,0:T(8,128)S(1)}, u32[]{:S(2)}, u32[]{:S(2)}) collective-permute-start(f32[3,128,128]{2,1,0:T(8,128)S(1)} %get-tuple-element.56), channel_id=1, source_target_pairs={{0,4},{1,5},{2,6},{3,7},{4,0},{5,1},{6,2},{7,3},{8,12},{9,13},{10,... | collective-permute-start | bytes 589832 | tf_op jit(solution)/shard_map/ppermute | solution.py:31
  4.9 10.4 %collective-permute-start.3 = (f32[3,128,128]{2,1,0:T(8,128)S(1)}, f32[3,128,128]{2,1,0:T(8,128)S(1)}, u32[]{:S(2)}, u32[]{:S(2)}) collective-permute-start(f32[3,128,128]{2,1,0:T(8,128)S(1)} %get-tuple-element.57), channel_id=1, source_target_pairs={{0,1},{1,0},{2,3},{3,2},{4,8},{5,9},{6,10},{7,11},{8,4},{9,5},{10,... | collective-permute-start | bytes 589832 | tf_op jit(solution)/shard_map/ppermute | solution.py:31
  4.9 3.7 %collective-permute-start.1 = (f32[16,8,128]{2,1,0:T(8,128)S(1)}, f32[16,8,128]{2,1,0:T(8,128)S(1)}, u32[]{:S(2)}, u32[]{:S(2)}) collective-permute-start(f32[16,8,128]{2,1,0:T(8,128)S(1)} %get-tuple-element.41), channel_id=1, source_target_pairs={{0,3},{1,2},{2,1},{3,0},{4,7},{5,6},{6,5},{7,4},{8,11},{9,10},{10,... | collective-permute-start | bytes 196616 | tf_op jit(solution)/shard_map/ppermute | solution.py:31
  6.5 2.1 %collective-permute-start = (f32[16,8,128]{2,1,0:T(8,128)S(1)}, f32[16,8,128]{2,1,0:T(8,128)S(1)}, u32[]{:S(2)}, u32[]{:S(2)}) collective-permute-start(f32[16,8,128]{2,1,0:T(8,128)S(1)} %get-tuple-element.38.after), channel_id=1, source_target_pairs={{0,1},{1,0},{2,3},{3,2},{4,5},{5,4},{6,7},{7,6},{8,9},{9,8},{10,11... | collective-permute-start | bytes 196616 | tf_op jit(solution)/shard_map/ppermute | solution.py:31
  9.3 7.1 %collective-permute-start.4 = (f32[136,128]{1,0:T(8,128)S(1)}, f32[136,128]{1,0:T(8,128)S(1)}, u32[]{:S(2)}, u32[]{:S(2)}) collective-permute-start(f32[136,128]{1,0:T(8,128)S(1)} %get-tuple-element.61), channel_id=1, source_target_pairs={{0,4},{1,5},{2,6},{3,7},{4,0},{5,1},{6,2},{7,3},{8,12},{9,13},{10,... | collective-permute-start | bytes 208904 | tf_op jit(solution)/shard_map/ppermute | solution.py:31
  13.0 3.4 %collective-permute-start.5 = (f32[136,128]{1,0:T(8,128)S(1)}, f32[136,128]{1,0:T(8,128)S(1)}, u32[]{:S(2)}, u32[]{:S(2)}) collective-permute-start(f32[136,128]{1,0:T(8,128)S(1)} %get-tuple-element.62), channel_id=1, source_target_pairs={{0,1},{1,0},{2,3},{3,2},{4,8},{5,9},{6,10},{7,11},{8,4},{9,5},{10,... | collective-permute-start | bytes 208904 | tf_op jit(solution)/shard_map/ppermute | solution.py:31

commit v8 on v7

--- a/solution.py
+++ b/solution.py
@@ -596,11 +596,13 @@
 def update_kernel(sums, precond, image, resid, pressure, residual, held, sem):
     total = jnp.sum(sums[...], axis=0, keepdims=True)
     half = total.shape[1] // 2
-    half_alpha = total[0:1, 0:1] / total[0:1, half : half + 1]
+    other = pltpu.roll(total, half, 1)
+    first = lax.broadcasted_iota(jnp.int32, total.shape, 1) < half
+    half_alpha = jnp.where(first, total, other) / jnp.where(first, other, total)
     alpha = 2.0 * half_alpha
     layers, rows, _ = precond.shape
     own = slice(LOW, LOW + rows)
-    step = 4 if layers % 4 == 0 else layers
+    step = 1
     started = []
     for start in range(0, layers, step):
         for k in range(start, start + step):

time: 31.5 us -> 31.4 us (level)
  no operation moved by 1% of the time
where the time goes in v8:
time: 31.4 us; the launch traced here: 31.3 us
  blocking collectives  12.9 us (41%)
  Pallas kernels  8.58 us (27%)
  starting transfers between devices  8.35 us (27%)
  waiting for transfers between devices  0.75 us (2%)
  between operations  0.69 us (2%)
    all_to_all x1, blocking collectives, on_device(): sums = lax.all_to_all(sums, ('gx', 'gy'), 0, 0, tiled=True)  12.9 us
    ppermute x6, starting transfers between devices, swap(): return lax.ppermute(value, ('gx', 'gy'), pairs)  8.35 us
    pallas_call x1, Pallas kernels, inner(): pl.pallas_call(inner_kernel, out_shape=outs, in_specs=[VMEM] * 7, out_spe...  2.27 us
    pallas_call x1, Pallas kernels, update(): pl.pallas_call(update_kernel, out_shape=(out, out), in_specs=[VMEM] * 4,...  1.66 us
    pallas_call x1, Pallas kernels, load(): pl.pallas_call(load_kernel, out_shape=(grown, grown), in_specs=[HBM, HBM,...  1.56 us
    pallas_call x1, Pallas kernels, pack(): pl.pallas_call(pack_kernel, out_shape=(x_out, x_out, y_out, y_out), in_sp...  1.22 us
    pallas_call x1, Pallas kernels, outer(): pl.pallas_call(outer_kernel, out_shape=(full, full, shape(2, 8, lanes), *...  0.88 us
    ppermute x6, waiting for transfers between devices, swap(): return lax.ppermute(value, ('gx', 'gy'), pairs)  0.75 us
  transfers between devices with their start and end apart: 6, of which 2 were waited for; matrix products, arithmetic and copies ran while one was open for 0% of the time, Pallas kernels for 17%

profile of v8, /device:TPU:0, one launch (start us, length us, event | category | flops | bytes accessed | tf_op | source)
XLA Modules:
  0.0 31.3 jit_solution(16082309165523419450)
XLA Ops:
  0.6 1.2 %pack.1 = (f32[3,128,128]{2,1,0:T(8,128)S(1)}, f32[3,128,128]{2,1,0:T(8,128)S(1)}, f32[16,8,128]{2,1,0:T(8,128)S(1)}, f32[16,8,128]{2,1,0:T(8,128)S(1)}) custom-call(f32[16,128,128]{2,1,0:T(8,128)} %cond.3, f32[16,128,128]{2,1,0:T(8,128)} %resid.3), custom_call_target="tpu_custom_call" | custom-call | tf_op jit(solution)/shard_map/pack/pallas_call | solution.py:101
  1.9 3.0 %collective-permute-start.2 = (f32[3,128,128]{2,1,0:T(8,128)S(1)}, f32[3,128,128]{2,1,0:T(8,128)S(1)}, u32[]{:S(2)}, u32[]{:S(2)}) collective-permute-start(f32[3,128,128]{2,1,0:T(8,128)S(1)} %get-tuple-element.56), channel_id=1, source_target_pairs={{0,4},{1,5},{2,6},{3,7},{4,0},{5,1},{6,2},{7,3},{8,12},{9,13},{10,... | collective-permute-start | bytes 589832 | tf_op jit(solution)/shard_map/ppermute | solution.py:31
  4.9 0.0 collective-permute-start.3
  4.9 1.6 %collective-permute-start.1 = (f32[16,8,128]{2,1,0:T(8,128)S(1)}, f32[16,8,128]{2,1,0:T(8,128)S(1)}, u32[]{:S(2)}, u32[]{:S(2)}) collective-permute-start(f32[16,8,128]{2,1,0:T(8,128)S(1)} %get-tuple-element.41), channel_id=1, source_target_pairs={{0,3},{1,2},{2,1},{3,0},{4,7},{5,6},{6,5},{7,4},{8,11},{9,10},{10,... | collective-permute-start | bytes 196616 | tf_op jit(solution)/shard_map/ppermute | solution.py:31
  6.5 0.0 collective-permute-start
  6.5 1.6 %load.1 = (f32[16,160,128]{2,1,0:T(8,128)S(1)}, f32[16,160,128]{2,1,0:T(8,128)S(1)}) custom-call(f32[16,128,128]{2,1,0:T(8,128)} %cond.3, f32[16,128,128]{2,1,0:T(8,128)} %resid.3, f32[16,8,128]{2,1,0:T(8,128)S(1)} %get-tuple-element.38.after), custom_call_target="tpu_custom_call" | custom-call | flops 1000000000 | bytes 1048576 | tf_op jit(solution)/shard_map/load/pallas_call | solution.py:133
  8.1 0.6 %collective-permute-done.1.y_odd = f32[16,8,128]{2,1,0:T(8,128)S(1)} collective-permute-done((f32[16,8,128]{2,1,0:T(8,128)S(1)}, f32[16,8,128]{2,1,0:T(8,128)S(1)}, u32[]{:S(2)}, u32[]{:S(2)}) %collective-permute-start.1) | collective-permute-done | bytes 65568 | tf_op jit(solution)/shard_map/ppermute | solution.py:31
  8.6 0.0 collective-permute-done.y_even
  8.6 0.6 %fields.1 = (f32[16,160,128]{2,1,0:T(8,128)S(1)}, f32[16,160,128]{2,1,0:T(8,128)S(1)}, f32[16,160,128]{2,1,0:T(8,128)S(1)}, f32[16,160,128]{2,1,0:T(8,128)S(1)},...) custom-call(f32[16,160,128]{2,1,0:T(8,128)S(1)} %get-tuple-element.3, ...), custom_call_target="tpu_custom_call", output_to_operand_aliasing={{0}: (0, {}), {1}: (1, {})} | custom-call | tf_op jit(solution)/shard_map/fields/pallas_call | solution.py:248
  9.3 3.7 %collective-permute-start.4 = (f32[136,128]{1,0:T(8,128)S(1)}, f32[136,128]{1,0:T(8,128)S(1)}, u32[]{:S(2)}, u32[]{:S(2)}) collective-permute-start(f32[136,128]{1,0:T(8,128)S(1)} %get-tuple-element.61), channel_id=1, source_target_pairs={{0,4},{1,5},{2,6},{3,7},{4,0},{5,1},{6,2},{7,3},{8,12},{9,13},{10,... | collective-permute-start | bytes 208904 | tf_op jit(solution)/shard_map/ppermute | solution.py:31
  13.0 0.0 collective-permute-start.5
  13.0 2.3 %inner.1 = (f32[16,128,128]{2,1,0:T(8,128)S(1)}, f32[16,128,128]{2,1,0:T(8,128)S(1)}, f32[16,160,128]{2,1,0:T(8,128)S(1)}, f32[2,8,128]{2,1,0:T(8,128)S(1)}, f32...) custom-call(f32[16,160,128]{2,1,0:T(8,128)S(1)} %get-tuple-element.42.u.b_u, ...), custom_call_target="tpu_custom_call" | custom-call | flops 100000000 | bytes 1 | tf_op jit(solution)/shard_map/inner/pallas_call | solution.py:330
  15.3 0.0 collective-permute-done.2.x_even
  15.3 0.0 collective-permute-done.3.x_odd
  15.3 0.9 %outer.1 = (f32[16,128,128]{2,1,0:T(8,128)S(1)}, f32[16,128,128]{2,1,0:T(8,128)S(1)}, f32[2,8,128]{2,1,0:T(8,128)S(1)}, f32[2,2,160,128]{3,2,1,0:T(8,128)S(1)}, ...) custom-call(f32[16,160,128]{2,1,0:T(8,128)S(1)} %get-tuple-element.4, ...), custom_call_target="tpu_custom_call", output_to_operand_aliasing={{0}: (2, {}), {1}: (3, {})} | custom-call | tf_op jit(solution)/shard_map/outer/pallas_call | solution.py:567
  16.2 0.2 collective-permute-done.4.t_even
  16.3 0.0 collective-permute-done.5.t_odd
  16.3 0.4 %corners.1 = (f32[16,128,128]{2,1,0:T(8,128)S(1)}, f32[16,128,128]{2,1,0:T(8,128)S(1)}, f32[32,128]{1,0:T(8,128)S(1)}, f32[2,2,160,128]{3,2,1,0:T(8,128)S(1)}, f...) custom-call(f32[16,160,128]{2,1,0:T(8,128)S(1)} %get-tuple-element.4, ...), custom_call_target="tpu_custom_call", output_to_operand_aliasing={{0}: (2, {}), {1}: (3, {}), {3}: (15, {}), {4}: (16, {}), {... | custom-call | tf_op jit(solution)/shard_map/corners/pallas_call | solution.py:585
  16.7 12.9 %all_to_all.11 = f32[32,1,128]{2,1,0:T(1,128)S(1)} all-to-all(f32[32,1,128]{2,1,0:T(1,128)S(1)} %bitcast.5), channel_id=1, replica_groups=mesh['gx'=8,'gy'=4] {'gx','gy'}, dimensions={0} | all-to-all | bytes 32768 | tf_op jit(solution)/shard_map/all_to_all | solution.py:650
  29.6 1.7 %update.1 = (f32[16,128,128]{2,1,0:T(8,128)}, f32[16,128,128]{2,1,0:T(8,128)}) custom-call(f32[32,128]{1,0:T(8,128)S(1)} %bitcast.4, f32[16,128,128]{2,1,0:T(8,128)S(1)} %get-tuple-element.72.precond, f32[16,128,128]{2,1,0:T(8,128)S(1)} %get-tuple-element.73.image, f32[16,160,128]{2,1,0:T(8,128)S(1)} %get-tuple-element.43.r.b_r.resid), custom_call_target="tpu_custom_call" | custom-call | tf_op jit(solution)/shard_map/update/pallas_call | solution.py:624
Async XLA Ops:
  1.9 13.4 %collective-permute-start.2 = (f32[3,128,128]{2,1,0:T(8,128)S(1)}, f32[3,128,128]{2,1,0:T(8,128)S(1)}, u32[]{:S(2)}, u32[]{:S(2)}) collective-permute-start(f32[3,128,128]{2,1,0:T(8,128)S(1)} %get-tuple-element.56), channel_id=1, source_target_pairs={{0,4},{1,5},{2,6},{3,7},{4,0},{5,1},{6,2},{7,3},{8,12},{9,13},{10,... | collective-permute-start | bytes 589832 | tf_op jit(solution)/shard_map/ppermute | solution.py:31
  4.9 10.4 %collective-permute-start.3 = (f32[3,128,128]{2,1,0:T(8,128)S(1)}, f32[3,128,128]{2,1,0:T(8,128)S(1)}, u32[]{:S(2)}, u32[]{:S(2)}) collective-permute-start(f32[3,128,128]{2,1,0:T(8,128)S(1)} %get-tuple-element.57), channel_id=1, source_target_pairs={{0,1},{1,0},{2,3},{3,2},{4,8},{5,9},{6,10},{7,11},{8,4},{9,5},{10,... | collective-permute-start | bytes 589832 | tf_op jit(solution)/shard_map/ppermute | solution.py:31
  4.9 3.7 %collective-permute-start.1 = (f32[16,8,128]{2,1,0:T(8,128)S(1)}, f32[16,8,128]{2,1,0:T(8,128)S(1)}, u32[]{:S(2)}, u32[]{:S(2)}) collective-permute-start(f32[16,8,128]{2,1,0:T(8,128)S(1)} %get-tuple-element.41), channel_id=1, source_target_pairs={{0,3},{1,2},{2,1},{3,0},{4,7},{5,6},{6,5},{7,4},{8,11},{9,10},{10,... | collective-permute-start | bytes 196616 | tf_op jit(solution)/shard_map/ppermute | solution.py:31
  6.5 2.1 %collective-permute-start = (f32[16,8,128]{2,1,0:T(8,128)S(1)}, f32[16,8,128]{2,1,0:T(8,128)S(1)}, u32[]{:S(2)}, u32[]{:S(2)}) collective-permute-start(f32[16,8,128]{2,1,0:T(8,128)S(1)} %get-tuple-element.38.after), channel_id=1, source_target_pairs={{0,1},{1,0},{2,3},{3,2},{4,5},{5,4},{6,7},{7,6},{8,9},{9,8},{10,11... | collective-permute-start | bytes 196616 | tf_op jit(solution)/shard_map/ppermute | solution.py:31
  9.3 7.1 %collective-permute-start.4 = (f32[136,128]{1,0:T(8,128)S(1)}, f32[136,128]{1,0:T(8,128)S(1)}, u32[]{:S(2)}, u32[]{:S(2)}) collective-permute-start(f32[136,128]{1,0:T(8,128)S(1)} %get-tuple-element.61), channel_id=1, source_target_pairs={{0,4},{1,5},{2,6},{3,7},{4,0},{5,1},{6,2},{7,3},{8,12},{9,13},{10,... | collective-permute-start | bytes 208904 | tf_op jit(solution)/shard_map/ppermute | solution.py:31
  13.0 3.4 %collective-permute-start.5 = (f32[136,128]{1,0:T(8,128)S(1)}, f32[136,128]{1,0:T(8,128)S(1)}, u32[]{:S(2)}, u32[]{:S(2)}) collective-permute-start(f32[136,128]{1,0:T(8,128)S(1)} %get-tuple-element.62), channel_id=1, source_target_pairs={{0,1},{1,0},{2,3},{3,2},{4,8},{5,9},{6,10},{7,11},{8,4},{9,5},{10,... | collective-permute-start | bytes 208904 | tf_op jit(solution)/shard_map/ppermute | solution.py:31

commit v9 on v8

--- a/solution.py
+++ b/solution.py
@@ -62,25 +62,52 @@
     return below + above
 
 
-def pack_kernel(cond, resid, x_even, x_odd, y_even, y_odd, tiles, sem):
-    layers, rows, lanes = cond.shape
+def pack_kernel(cond, resid, x_even, x_odd, sem):
+    layers = cond.shape[0]
     odd = lax.rem(lax.axis_index("gx"), 2)
-    x_copies, y_copies = [], []
+    copies = []
     for out, high in ((x_even, 1 - odd), (x_odd, odd)):
         two = pl.ds(high * (layers - 2), 2)
         one = pl.ds(high * (layers - 1), 1)
-        x_copies.append((cond.at[two], out.at[pl.ds(0, 2)]))
-        x_copies.append((resid.at[one], out.at[pl.ds(2, 1)]))
-    for side, start in enumerate((0, rows - HALO)):
-        for part, source in enumerate((cond, resid)):
-            y_copies.append((source.at[:, pl.ds(start, HALO)], tiles.at[side, part]))
+        copies.append((cond.at[two], out.at[pl.ds(0, 2)]))
+        copies.append((resid.at[one], out.at[pl.ds(2, 1)]))
     started = [
         pltpu.make_async_copy(source, target, sem.at[i])
-        for i, (source, target) in enumerate(y_copies + x_copies)
+        for i, (source, target) in enumerate(copies)
     ]
     for copy in started:
         copy.start()
-    for copy in started[:4]:
+    for copy in started:
+        copy.wait()
+
+
+def pack(cond, resid):
+    out = shape(3, *cond.shape[1:])
+    return pl.pallas_call(
+        pack_kernel,
+        out_shape=(out, out),
+        in_specs=[HBM, HBM],
+        out_specs=(VMEM, VMEM),
+        scratch_shapes=[pltpu.SemaphoreType.DMA((4,))],
+        compiler_params=params(1),
+        name="pack",
+    )(
+        pltpu.with_memory_space_constraint(cond, pltpu.HBM),
+        pltpu.with_memory_space_constraint(resid, pltpu.HBM),
+    )
+
+
+def pack_y_kernel(cond, resid, after, y_even, y_odd, tiles, sem):
+    layers, rows, lanes = cond.shape
+    started = []
+    for side, start in enumerate((0, rows - HALO)):
+        for part, source in enumerate((cond, resid)):
+            copy = pltpu.make_async_copy(
+                source.at[:, pl.ds(start, HALO)], tiles.at[side, part], sem.at[2 * side + part]
+            )
+            copy.start()
+            started.append(copy)
+    for copy in started:
         copy.wait()
     odd = lax.rem(lax.axis_index("gy"), 2) == 1
     first = lax.broadcasted_iota(jnp.int32, (HALO, lanes), 0) < 3
@@ -91,27 +118,29 @@
         )
         y_even[k] = jnp.where(odd, low, high)
         y_odd[k] = jnp.where(odd, high, low)
-    for copy in started[4:]:
-        copy.wait()
-
-
-def pack(cond, resid):
+
+
+def pack_y(cond, resid, after):
     layers, rows, lanes = cond.shape
-    x_out, y_out = shape(3, rows, lanes), shape(layers, HALO, lanes)
-    return pl.pallas_call(
-        pack_kernel,
-        out_shape=(x_out, x_out, y_out, y_out),
-        in_specs=[HBM, HBM],
-        out_specs=(VMEM,) * 4,
+    out = shape(layers, HALO, lanes)
+    return pl.pallas_call(
+        pack_y_kernel,
+        out_shape=(out, out),
+        in_specs=[HBM, HBM, VMEM],
+        out_specs=(VMEM, VMEM),
         scratch_shapes=[
             pltpu.VMEM((2, 2, layers, HALO, lanes), F32),
-            pltpu.SemaphoreType.DMA((8,)),
+            pltpu.SemaphoreType.DMA((4,)),
         ],
         compiler_params=params(2),
-        name="pack",
+        cost_estimate=pl.CostEstimate(
+            flops=1_000_000, transcendentals=0, bytes_accessed=1
+        ),
+        name="pack_y",
     )(
         pltpu.with_memory_space_constraint(cond, pltpu.HBM),
         pltpu.with_memory_space_constraint(resid, pltpu.HBM),
+        after,
     )
 
 
@@ -162,6 +191,58 @@
     return south, north
 
 
+def edge_kernel(u, r, y_even, y_odd, t_even, t_odd, grown):
+    layers, rows = u.shape[0], u.shape[1] - 4 * HALO
+    odd = place("gx")[0]
+    end = HALO + rows
+    own = slice(LOW, LOW + rows)
+    sends = []
+    for side in range(2):
+        edge, mid, far = ((0, 1, 2), (layers - 1, layers - 2, layers - 3))[side]
+        south, north = y_tiles(y_even, y_odd, mid, 0)
+        middle = u[mid, own]
+        grown[side, 0:HALO] = south
+        grown[side, HALO:end] = middle
+        grown[side, end : end + HALO] = north
+        total = 6.0 * middle + u[edge, own] + u[far, own] + z_sum(middle)
+        total = total + grown[side, HALO - 1 : end - 1] + grown[side, HALO + 1 : end + 1]
+        term = (u[edge, own] + middle) * (2.0 * r[mid, own] / total)
+        edge_south, edge_north = y_tiles(y_even, y_odd, edge, 0)
+        r_south, r_north = y_tiles(y_even, y_odd, edge, 1)
+        corner = jnp.concatenate(
+            [
+                edge_south[HALO - 1 : HALO],
+                edge_south[HALO - 2 : HALO - 1],
+                south[HALO - 1 : HALO],
+                r_south[HALO - 1 : HALO],
+                edge_north[0:1],
+                edge_north[1:2],
+                north[0:1],
+                r_north[0:1],
+            ],
+            axis=0,
+        )
+        sends.append((term, corner))
+    (t_low, c_low), (t_high, c_high) = sends
+    t_even[0:rows] = jnp.where(odd, t_low, t_high)
+    t_even[rows : rows + 8] = jnp.where(odd, c_low, c_high)
+    t_odd[0:rows] = jnp.where(odd, t_high, t_low)
+    t_odd[rows : rows + 8] = jnp.where(odd, c_high, c_low)
+
+
+def edge_terms(u, r, y_even, y_odd):
+    rows, lanes = u.shape[1] - 4 * HALO, u.shape[2]
+    return pl.pallas_call(
+        edge_kernel,
+        out_shape=(shape(rows + 8, lanes), shape(rows + 8, lanes)),
+        in_specs=[VMEM] * 4,
+        out_specs=(VMEM, VMEM),
+        scratch_shapes=[pltpu.VMEM((2, rows + 2 * HALO, lanes), F32)],
+        compiler_params=params(2),
+        name="edge_terms",
+    )(u, r, y_even, y_odd)
+
+
 def row_chunks(rows):
     total = rows + 2 * HALO
     step = total // 3 if total % 24 == 0 else total
@@ -194,7 +275,7 @@
 
 
 def fields_kernel(
-    u_in, r_in, y_even, y_odd, u, r, inv, v, w, d, masks, t_even, t_odd
+    u_in, r_in, y_even, y_odd, u, r, inv, v, w, d, masks
 ):
     layers, rows = u.shape[0], u.shape[1] - 4 * HALO
     fill_rows(masks, rows)
@@ -217,34 +298,11 @@
             inv[k, here] = inverse
             v[k, here] = value
             w[k, here] = mid * value
-    odd = place("gx")[0]
-    own, north = slice(LOW, LOW + rows), LOW + rows
-    sends = []
-    for side in range(2):
-        edge, mid = ((0, 1), (layers - 1, layers - 2))[side]
-        lines = (
-            u[edge, LOW - 1 : LOW],
-            u[edge, LOW - 2 : LOW - 1],
-            u[mid, LOW - 1 : LOW],
-            r[edge, LOW - 1 : LOW],
-            u[edge, north : north + 1],
-            u[edge, north + 1 : north + 2],
-            u[mid, north : north + 1],
-            r[edge, north : north + 1],
-        )
-        term = (u[edge, own] + u[mid, own]) * v[mid, own]
-        sends.append((term, jnp.concatenate(lines, axis=0)))
-    (t_low, c_low), (t_high, c_high) = sends
-    t_even[0:rows] = jnp.where(odd, t_low, t_high)
-    t_even[rows : rows + 8] = jnp.where(odd, c_low, c_high)
-    t_odd[0:rows] = jnp.where(odd, t_high, t_low)
-    t_odd[rows : rows + 8] = jnp.where(odd, c_high, c_low)
 
 
 def fields(u, r, y_even, y_odd):
     layers, grown, lanes = u.shape
-    ext, term = shape(*u.shape), shape(grown - 4 * HALO + 8, lanes)
-    outs = (ext,) * 6 + (shape(4, grown, lanes), term, term)
+    outs = (shape(*u.shape),) * 6 + (shape(4, grown, lanes),)
     return pl.pallas_call(
         fields_kernel,
         out_shape=outs,
@@ -636,12 +694,14 @@
 
 
 def on_device(right_side, conductivity):
-    x_even, x_odd, y_even, y_odd = pack(conductivity, right_side)
+    x_even, x_odd = pack(conductivity, right_side)
+    y_even, y_odd = pack_y(conductivity, right_side, x_odd)
     u, r = load(conductivity, right_side, y_even)
     y_even, y_odd = swap_y(y_even, 0), swap_y(y_odd, 1)
     x_even, x_odd = swap_x(x_even, 0), swap_x(x_odd, 1)
-    *found, t_even, t_odd = fields(u, r, y_even, y_odd)
+    t_even, t_odd = edge_terms(u, r, y_even, y_odd)
     t_even, t_odd = swap_x(t_even, 0), swap_x(t_odd, 1)
+    found = fields(u, r, y_even, y_odd)
     u, r, inv, v, _, d, masks = found
     p_inner, i_inner, p, sums, *faces = inner(*found)
     found = (u, r, p_inner, i_inner, v, inv, d, p, *faces, sums)

time: 31.4 us -> 31.3 us (level)
  blocking collectives: 12.9 us -> 11.8 us
  Pallas kernels: 8.58 us -> 9.57 us
    all_to_all x1, blocking collectives: 12.9 us -> 11.8 us  [on_device(): sums = lax.all_to_all(sums, ('gx', 'gy'), 0, 0, tiled=True)]
    pallas_call x1 -> x3, Pallas kernels: 1.22 us -> 2.19 us  [the longest x1 1.05 us: pack(): pl.pallas_call(pack_kernel, out_shape=(out, out), in_specs=[HBM, HBM], ou...]
  transfers between devices with their start and end apart: 6 -> 6, of which waited for: 2 -> 1; matrix products, arithmetic and copies ran while one was open for 0% -> 0% of each run, Pallas kernels for 17% -> 21%
where the time goes in v9:
time: 31.3 us; the launch traced here: 31.1 us
  blocking collectives  11.8 us (38%)
  Pallas kernels  9.57 us (31%)
  starting transfers between devices  8.41 us (27%)
  between operations  0.72 us (2%)
  waiting for transfers between devices  0.59 us (2%)
    all_to_all x1, blocking collectives, on_device(): sums = lax.all_to_all(sums, ('gx', 'gy'), 0, 0, tiled=True)  11.8 us
    ppermute x6, starting transfers between devices, swap(): return lax.ppermute(value, ('gx', 'gy'), pairs)  8.41 us
    pallas_call x1, Pallas kernels, inner(): pl.pallas_call(inner_kernel, out_shape=outs, in_specs=[VMEM] * 7, out_spe...  2.27 us
    pallas_call x1, Pallas kernels, update(): pl.pallas_call(update_kernel, out_shape=(out, out), in_specs=[VMEM] * 4,...  1.66 us
    pallas_call x1, Pallas kernels, load(): pl.pallas_call(load_kernel, out_shape=(grown, grown), in_specs=[HBM, HBM,...  1.56 us
    pallas_call x1, Pallas kernels, pack(): pl.pallas_call(pack_kernel, out_shape=(out, out), in_specs=[HBM, HBM], ou...  1.05 us
    pallas_call x1, Pallas kernels, pack_y(): pl.pallas_call(pack_y_kernel, out_shape=(out, out), in_specs=[HBM, HBM, V...  0.99 us
    pallas_call x1, Pallas kernels, outer(): pl.pallas_call(outer_kernel, out_shape=(full, full, shape(2, 8, lanes), *...  0.88 us
  transfers between devices with their start and end apart: 6, of which 1 were waited for; matrix products, arithmetic and copies ran while one was open for 0% of the time, Pallas kernels for 21%

profile of v9, /device:TPU:0, one launch (start us, length us, event | category | flops | bytes accessed | tf_op | source)
XLA Modules:
  0.0 31.1 jit_solution(3170733728182713717)
XLA Ops:
  0.6 1.1 %pack.1 = (f32[3,128,128]{2,1,0:T(8,128)S(1)}, f32[3,128,128]{2,1,0:T(8,128)S(1)}) custom-call(f32[16,128,128]{2,1,0:T(8,128)} %cond.5, f32[16,128,128]{2,1,0:T(8,128)} %resid.5), custom_call_target="tpu_custom_call" | custom-call | tf_op jit(solution)/shard_map/pack/pallas_call | solution.py:86
  1.7 3.0 %collective-permute-start.2 = (f32[3,128,128]{2,1,0:T(8,128)S(1)}, f32[3,128,128]{2,1,0:T(8,128)S(1)}, u32[]{:S(2)}, u32[]{:S(2)}) collective-permute-start(f32[3,128,128]{2,1,0:T(8,128)S(1)} %get-tuple-element.57), channel_id=1, source_target_pairs={{0,4},{1,5},{2,6},{3,7},{4,0},{5,1},{6,2},{7,3},{8,12},{9,13},{10,... | collective-permute-start | bytes 589832 | tf_op jit(solution)/shard_map/ppermute | solution.py:31
  4.7 0.0 collective-permute-start.3
  4.7 1.0 %pack_y.1 = (f32[16,8,128]{2,1,0:T(8,128)S(1)}, f32[16,8,128]{2,1,0:T(8,128)S(1)}) custom-call(f32[16,128,128]{2,1,0:T(8,128)} %cond.5, f32[16,128,128]{2,1,0:T(8,128)} %resid.5, f32[3,128,128]{2,1,0:T(8,128)S(1)} %get-tuple-element.38.after), custom_call_target="tpu_custom_call" | custom-call | flops 1000000 | bytes 1 | tf_op jit(solution)/shard_map/pack_y/pallas_call | solution.py:126
  5.7 1.7 %collective-permute-start.1 = (f32[16,8,128]{2,1,0:T(8,128)S(1)}, f32[16,8,128]{2,1,0:T(8,128)S(1)}, u32[]{:S(2)}, u32[]{:S(2)}) collective-permute-start(f32[16,8,128]{2,1,0:T(8,128)S(1)} %get-tuple-element.42), channel_id=1, source_target_pairs={{0,3},{1,2},{2,1},{3,0},{4,7},{5,6},{6,5},{7,4},{8,11},{9,10},{10,... | collective-permute-start | bytes 196616 | tf_op jit(solution)/shard_map/ppermute | solution.py:31
  7.4 0.0 collective-permute-start
  7.4 1.6 %load.1 = (f32[16,160,128]{2,1,0:T(8,128)S(1)}, f32[16,160,128]{2,1,0:T(8,128)S(1)}) custom-call(f32[16,128,128]{2,1,0:T(8,128)} %cond.5, f32[16,128,128]{2,1,0:T(8,128)} %resid.5, f32[16,8,128]{2,1,0:T(8,128)S(1)} %get-tuple-element.39.after), custom_call_target="tpu_custom_call" | custom-call | flops 1000000000 | bytes 1048576 | tf_op jit(solution)/shard_map/load/pallas_call | solution.py:162
  9.0 0.6 %collective-permute-done.1.y_odd = f32[16,8,128]{2,1,0:T(8,128)S(1)} collective-permute-done((f32[16,8,128]{2,1,0:T(8,128)S(1)}, f32[16,8,128]{2,1,0:T(8,128)S(1)}, u32[]{:S(2)}, u32[]{:S(2)}) %collective-permute-start.1) | collective-permute-done | bytes 65568 | tf_op jit(solution)/shard_map/ppermute | solution.py:31
  9.5 0.0 collective-permute-done.y_even
  9.5 0.2 edge_terms.1
  9.7 3.7 %collective-permute-start.4 = (f32[136,128]{1,0:T(8,128)S(1)}, f32[136,128]{1,0:T(8,128)S(1)}, u32[]{:S(2)}, u32[]{:S(2)}) collective-permute-start(f32[136,128]{1,0:T(8,128)S(1)} %get-tuple-element.61), channel_id=1, source_target_pairs={{0,4},{1,5},{2,6},{3,7},{4,0},{5,1},{6,2},{7,3},{8,12},{9,13},{10,... | collective-permute-start | bytes 208904 | tf_op jit(solution)/shard_map/ppermute | solution.py:31
  13.4 0.0 collective-permute-start.5
  13.4 0.6 %fields.1 = (f32[16,160,128]{2,1,0:T(8,128)S(1)}, f32[16,160,128]{2,1,0:T(8,128)S(1)}, f32[16,160,128]{2,1,0:T(8,128)S(1)}, f32[16,160,128]{2,1,0:T(8,128)S(1)},...) custom-call(f32[16,160,128]{2,1,0:T(8,128)S(1)} %get-tuple-element.4, ...), custom_call_target="tpu_custom_call", output_to_operand_aliasing={{0}: (0, {}), {1}: (1, {})} | custom-call | tf_op jit(solution)/shard_map/fields/pallas_call | solution.py:306
  14.0 2.3 %inner.1 = (f32[16,128,128]{2,1,0:T(8,128)S(1)}, f32[16,128,128]{2,1,0:T(8,128)S(1)}, f32[16,160,128]{2,1,0:T(8,128)S(1)}, f32[2,8,128]{2,1,0:T(8,128)S(1)}, f32...) custom-call(f32[16,160,128]{2,1,0:T(8,128)S(1)} %get-tuple-element.43.u.b_u, ...), custom_call_target="tpu_custom_call" | custom-call | flops 100000000 | bytes 1 | tf_op jit(solution)/shard_map/inner/pallas_call | solution.py:388
  16.3 0.0 collective-permute-done.2.x_even
  16.3 0.0 collective-permute-done.3.x_odd
  16.3 0.9 %outer.1 = (f32[16,128,128]{2,1,0:T(8,128)S(1)}, f32[16,128,128]{2,1,0:T(8,128)S(1)}, f32[2,8,128]{2,1,0:T(8,128)S(1)}, f32[2,2,160,128]{3,2,1,0:T(8,128)S(1)}, ...) custom-call(f32[16,160,128]{2,1,0:T(8,128)S(1)} %get-tuple-element.4, ...), custom_call_target="tpu_custom_call", output_to_operand_aliasing={{0}: (2, {}), {1}: (3, {})} | custom-call | tf_op jit(solution)/shard_map/outer/pallas_call | solution.py:625
  17.2 0.0 collective-permute-done.4.t_even
  17.2 0.0 collective-permute-done.5.t_odd
  17.2 0.4 %corners.1 = (f32[16,128,128]{2,1,0:T(8,128)S(1)}, f32[16,128,128]{2,1,0:T(8,128)S(1)}, f32[32,128]{1,0:T(8,128)S(1)}, f32[2,2,160,128]{3,2,1,0:T(8,128)S(1)}, f...) custom-call(f32[16,160,128]{2,1,0:T(8,128)S(1)} %get-tuple-element.4, ...), custom_call_target="tpu_custom_call", output_to_operand_aliasing={{0}: (2, {}), {1}: (3, {}), {3}: (15, {}), {4}: (16, {}), {... | custom-call | tf_op jit(solution)/shard_map/corners/pallas_call | solution.py:643
  17.6 11.8 %all_to_all.11 = f32[32,1,128]{2,1,0:T(1,128)S(1)} all-to-all(f32[32,1,128]{2,1,0:T(1,128)S(1)} %bitcast.5), channel_id=1, replica_groups=mesh['gx'=8,'gy'=4] {'gx','gy'}, dimensions={0} | all-to-all | bytes 32768 | tf_op jit(solution)/shard_map/all_to_all | solution.py:710
  29.4 1.7 %update.1 = (f32[16,128,128]{2,1,0:T(8,128)}, f32[16,128,128]{2,1,0:T(8,128)}) custom-call(f32[32,128]{1,0:T(8,128)S(1)} %bitcast.4, f32[16,128,128]{2,1,0:T(8,128)S(1)} %get-tuple-element.72.precond, f32[16,128,128]{2,1,0:T(8,128)S(1)} %get-tuple-element.73.image, f32[16,160,128]{2,1,0:T(8,128)S(1)} %get-tuple-element.44.r.b_r.resid), custom_call_target="tpu_custom_call" | custom-call | tf_op jit(solution)/shard_map/update/pallas_call | solution.py:682
Async XLA Ops:
  1.7 14.6 %collective-permute-start.2 = (f32[3,128,128]{2,1,0:T(8,128)S(1)}, f32[3,128,128]{2,1,0:T(8,128)S(1)}, u32[]{:S(2)}, u32[]{:S(2)}) collective-permute-start(f32[3,128,128]{2,1,0:T(8,128)S(1)} %get-tuple-element.57), channel_id=1, source_target_pairs={{0,4},{1,5},{2,6},{3,7},{4,0},{5,1},{6,2},{7,3},{8,12},{9,13},{10,... | collective-permute-start | bytes 589832 | tf_op jit(solution)/shard_map/ppermute | solution.py:31
  4.7 11.6 %collective-permute-start.3 = (f32[3,128,128]{2,1,0:T(8,128)S(1)}, f32[3,128,128]{2,1,0:T(8,128)S(1)}, u32[]{:S(2)}, u32[]{:S(2)}) collective-permute-start(f32[3,128,128]{2,1,0:T(8,128)S(1)} %get-tuple-element.38.after), channel_id=1, source_target_pairs={{0,1},{1,0},{2,3},{3,2},{4,8},{5,9},{6,10},{7,11},{8,4},{9,5},{10,... | collective-permute-start | bytes 589832 | tf_op jit(solution)/shard_map/ppermute | solution.py:31
  5.7 3.8 %collective-permute-start.1 = (f32[16,8,128]{2,1,0:T(8,128)S(1)}, f32[16,8,128]{2,1,0:T(8,128)S(1)}, u32[]{:S(2)}, u32[]{:S(2)}) collective-permute-start(f32[16,8,128]{2,1,0:T(8,128)S(1)} %get-tuple-element.42), channel_id=1, source_target_pairs={{0,3},{1,2},{2,1},{3,0},{4,7},{5,6},{6,5},{7,4},{8,11},{9,10},{10,... | collective-permute-start | bytes 196616 | tf_op jit(solution)/shard_map/ppermute | solution.py:31
  7.4 2.1 %collective-permute-start = (f32[16,8,128]{2,1,0:T(8,128)S(1)}, f32[16,8,128]{2,1,0:T(8,128)S(1)}, u32[]{:S(2)}, u32[]{:S(2)}) collective-permute-start(f32[16,8,128]{2,1,0:T(8,128)S(1)} %get-tuple-element.39.after), channel_id=1, source_target_pairs={{0,1},{1,0},{2,3},{3,2},{4,5},{5,4},{6,7},{7,6},{8,9},{9,8},{10,11... | collective-permute-start | bytes 196616 | tf_op jit(solution)/shard_map/ppermute | solution.py:31
  9.7 7.5 %collective-permute-start.4 = (f32[136,128]{1,0:T(8,128)S(1)}, f32[136,128]{1,0:T(8,128)S(1)}, u32[]{:S(2)}, u32[]{:S(2)}) collective-permute-start(f32[136,128]{1,0:T(8,128)S(1)} %get-tuple-element.61), channel_id=1, source_target_pairs={{0,4},{1,5},{2,6},{3,7},{4,0},{5,1},{6,2},{7,3},{8,12},{9,13},{10,... | collective-permute-start | bytes 208904 | tf_op jit(solution)/shard_map/ppermute | solution.py:31
  13.4 3.8 %collective-permute-start.5 = (f32[136,128]{1,0:T(8,128)S(1)}, f32[136,128]{1,0:T(8,128)S(1)}, u32[]{:S(2)}, u32[]{:S(2)}) collective-permute-start(f32[136,128]{1,0:T(8,128)S(1)} %get-tuple-element.62), channel_id=1, source_target_pairs={{0,1},{1,0},{2,3},{3,2},{4,8},{5,9},{6,10},{7,11},{8,4},{9,5},{10,... | collective-permute-start | bytes 208904 | tf_op jit(solution)/shard_map/ppermute | solution.py:31
